TPU v7x, 256 devices: a whole 4x4x8 slice. The times are simulated.
256 devices in a mesh: seq: 16 (over y_lo, z), dp: 16 (over x, y_hi, core).
Axes of the slice: x: 4, y: 4 (y_hi: 2, y_lo: 2; y = y_hi * 2 + y_lo), z: 8, core: 2. Of those that a mesh axis runs over, the one named last changes fastest.
Arguments:
- layer_rows: bfloat16 [16, 2048, 1024], P('dp', 'seq'), may hold values from -6 to 6
- doc_ids: int32 [16, 2048], P('dp', 'seq'), may hold values from 0 to 5, never falling along the last dimension, each value on 1 to 1024 neighbouring positions
- packing: int32 [16, 16], P('dp'), may hold values from 0 to 15, each once within a row
- norm_gain: float32 [1024], replicated, may hold values from 0.1 to 1.9
- w_qkv: bfloat16 [1024, 3072], replicated, may hold values from -0.1875 to 0.1875
- d_attn: bfloat16 [16, 2048, 1024], P('dp', 'seq'), may hold values from -6 to 6
Outputs:
- d_input: bfloat16 [16, 2048, 1024], P('dp', 'seq')
- w_grad: float32 [1024, 3072], P('seq')
Inputs may be any that keep to these rules, and one draw needn't show every extreme that they name: `doc_ids`: in each group the song numbers never fall along the initial order; every number occurs, and one song spans exactly 1024 frames. `packing`: each group's row names every block number once.
All inputs are finite; a program needn't handle non-finite values.
Results may differ from a plain program's by a relative error of at most 0.024.
Values may be sent and summed in bfloat16 or wider, within the bound.
No kernel may reach another device: no remote copies, remote signals or barrier semaphores. Data moves between devices by JAX's collectives and lax.ppermute only.
A program may use at most 128 MiB of HBM per device.

v0:
```python
import math

import jax
import jax.numpy as jnp
from jax import lax
from jax.experimental import pallas as pl
from jax.experimental.pallas import tpu as pltpu
from jax.sharding import Mesh
from jax.sharding import PartitionSpec as P

HEADS = 8
HEAD = 128
BLOCK = 128
HALF = 64
NBLK = 16
D = 1024
STEPS = 4
QROWS = 256
KROWS = 512
EXTRA = 8
FACTOR = 1.0 / math.sqrt(HEAD)
EPS = 1e-05
F32 = jnp.float32
BF16 = jnp.bfloat16


def dot(a, b, ca, cb):
    return lax.dot_general(a, b, (((ca,), (cb,)), ((), ())), preferred_element_type=F32)


def place_of(p):
    return (p % 8) * 2 + p // 8


PIECES = 9


def head_kernel(*refs):
    meta, pieces, others, rest = refs[0], refs[1 : 1 + PIECES], refs[1 + PIECES : 1 + 2 * PIECES], refs[1 + 2 * PIECES :]
    (
        do, gain, wq, wk, wv,
        normed, mine, part,
        rows_s, q_s, do_s, k_s, v_s, dk_s, dv_s, e_s, p_s, docs, inv, sems,
    ) = rest
    step = pl.program_id(0)
    z = meta[NBLK]
    half = meta[NBLK + 1]

    @pl.when(step == 0)
    def _():
        copies = []
        for c, group in enumerate((pieces, others)):
            side = half if c == 0 else 1 - half
            for n, ref in enumerate(group):
                offset = (0, 1, 7, 2, 6, 3, 5, 4, 4)[n]
                target = rows_s.at[side * 8 + (z + offset) % 8]
                if n == 7:
                    target = target.at[0:HALF]
                elif n == 8:
                    target = target.at[HALF : BLOCK + EXTRA]
                copies.append(pltpu.make_async_copy(ref, target, sems.at[c * PIECES + n]))
        for copy in copies:
            copy.start()

        def put(p, carry):
            inv[meta[p]] = p
            return carry

        lax.fori_loop(0, NBLK, put, 0)
        docs[...] = jnp.full(docs.shape, 1000.0, F32)
        dk_s[...] = jnp.zeros(dk_s.shape, F32)
        dv_s[...] = jnp.zeros(dv_s.shape, F32)
        for copy in copies:
            copy.wait()
        mine[...] = rows_s[meta[half * 8 + z], 0:BLOCK, :]

    rows = rows_s[pl.ds(step * 4, 4), 0:BLOCK, :].astype(F32)
    inverse = lax.rsqrt(jnp.mean(rows * rows, axis=-1, keepdims=True) + EPS)
    nrm = (rows * inverse * gain[...][None]).astype(BF16)
    normed[...] = nrm
    nrm = nrm.reshape(KROWS, D)
    k_s[step] = dot(nrm, wk[...], 1, 0).astype(BF16)
    v_s[step] = dot(nrm, wv[...], 1, 0).astype(BF16)
    own = pl.multiple_of(half * HALF, HALF)
    qn = normed[:, pl.ds(own, HALF), :].reshape(QROWS, D)
    q_s[...] = dot(qn, wq[...], 1, 0).astype(BF16)
    for t in range(4):
        do_s[t * HALF : (t + 1) * HALF, :] = do[place_of(inv[step * 4 + t])]

    info = jnp.sum(rows_s[pl.ds(step * 4, 4), BLOCK : BLOCK + EXTRA, 0:QROWS].astype(F32), axis=0)
    docs[step] = info
    mine_docs = jnp.where(half == 0, info[0:1, :], info[1:2, :])
    lane = lax.broadcasted_iota(jnp.int32, (1, QROWS), 1)
    q_pos = step * KROWS + (lane // HALF) * BLOCK + half * HALF + lane % HALF
    known = docs[...]
    real = lax.broadcasted_iota(jnp.int32, known.shape, 1) < 2
    first = jnp.zeros((1, QROWS), F32)
    for number in range(1, 6):
        below = jnp.sum(jnp.where((known < number) & real, 1.0, 0.0))
        first = first + jnp.where(mine_docs == number, below, 0.0)
    q_first = first.astype(jnp.int32)

    def scores(g, total):
        s = dot(k_s[g], q_s[...], 1, 1) * FACTOR
        j = g * KROWS + lax.broadcasted_iota(jnp.int32, (KROWS, QROWS), 0)
        e = jnp.where((j >= q_first) & (j <= q_pos), jnp.exp(s), 0.0)
        e_s[g] = e
        return total + jnp.sum(e, axis=0, keepdims=True)

    total = lax.fori_loop(0, step + 1, scores, jnp.zeros((1, QROWS), F32))
    scale = 1.0 / total

    def deltas(g, delta):
        grad = dot(v_s[g], do_s[...], 1, 1)
        p_s[g] = grad
        low = (e_s[g] * scale).astype(BF16)
        dv_s[g] += dot(low, do_s[...], 1, 0)
        return delta + jnp.sum(low.astype(F32) * grad, axis=0, keepdims=True)

    delta = lax.fori_loop(0, step + 1, deltas, jnp.zeros((1, QROWS), F32))

    def grads(g, dq):
        ds = (e_s[g] * scale * (p_s[g] - delta)).astype(BF16)
        dk_s[g] += dot(ds, q_s[...], 1, 0)
        return dq + dot(ds, k_s[g], 0, 0)

    dq = lax.fori_loop(0, step + 1, grads, jnp.zeros((QROWS, HEAD), F32))
    dq = (dq * FACTOR).astype(BF16)
    part[pl.ds(step * 4, 4), 0:HALF, :] = dq.reshape(4, HALF, HEAD)

    @pl.when(step == STEPS - 1)
    def _():
        part[:, HALF : HALF + BLOCK, :] = (dk_s[...] * FACTOR).astype(BF16).reshape(NBLK, BLOCK, HEAD)
        part[:, HALF + BLOCK :, :] = dv_s[...].astype(BF16).reshape(NBLK, BLOCK, HEAD)


def head_pass(meta, pieces, others, do, gain, w_qkv):
    pack = (NBLK, HALF + 2 * BLOCK, HEAD)
    grid_spec = pltpu.PrefetchScalarGridSpec(
        num_scalar_prefetch=1,
        grid=(STEPS,),
        in_specs=[pl.BlockSpec(memory_space=pl.ANY)] * (2 * PIECES)
        + [
            pl.BlockSpec((NBLK, HALF, HEAD), lambda i, m: (0, 0, 0)),
            pl.BlockSpec((1, D), lambda i, m: (0, 0)),
            pl.BlockSpec((D, HEAD), lambda i, m: (0, m[NBLK])),
            pl.BlockSpec((D, HEAD), lambda i, m: (0, HEADS + m[NBLK])),
            pl.BlockSpec((D, HEAD), lambda i, m: (0, 2 * HEADS + m[NBLK])),
        ],
        out_specs=[
            pl.BlockSpec((4, BLOCK, D), lambda i, m: (i, 0, 0)),
            pl.BlockSpec((BLOCK, D), lambda i, m: (0, 0)),
            pl.BlockSpec(pack, lambda i, m: (0, 0, 0)),
        ],
        scratch_shapes=[
            pltpu.VMEM((NBLK, BLOCK + EXTRA, D), BF16),
            pltpu.VMEM((QROWS, HEAD), BF16),
            pltpu.VMEM((QROWS, HEAD), BF16),
            pltpu.VMEM((STEPS, KROWS, HEAD), BF16),
            pltpu.VMEM((STEPS, KROWS, HEAD), BF16),
            pltpu.VMEM((STEPS, KROWS, HEAD), F32),
            pltpu.VMEM((STEPS, KROWS, HEAD), F32),
            pltpu.VMEM((STEPS, KROWS, QROWS), F32),
            pltpu.VMEM((STEPS, KROWS, QROWS), F32),
            pltpu.VMEM((STEPS, EXTRA, QROWS), F32),
            pltpu.SMEM((NBLK,), jnp.int32),
            pltpu.SemaphoreType.DMA((2 * PIECES,)),
        ],
    )
    return pl.pallas_call(
        head_kernel,
        grid_spec=grid_spec,
        out_shape=[
            jax.ShapeDtypeStruct((NBLK, BLOCK, D), BF16),
            jax.ShapeDtypeStruct((BLOCK, D), BF16),
            jax.ShapeDtypeStruct(pack, BF16),
        ],
        name="head_pass",
    )(meta, *pieces, *others, do, gain, w_qkv, w_qkv, w_qkv)


def total_of(part, came, half, blocks):
    low = part[blocks, 0:HALF, :]
    high = came[blocks, 0:HALF, :]
    first = jnp.where(half == 0, low, high)
    second = jnp.where(half == 0, high, low)
    both = part[blocks, HALF:, :].astype(F32) + came[blocks, HALF:, :].astype(F32)
    return first, second, both.astype(BF16)


def weight_kernel(meta, normed, part, came, here, there, dw_s):
    step = pl.program_id(0)
    half = meta[NBLK + 1]
    y = meta[NBLK + 2]
    first, second, both = total_of(part, came, half, slice(None))
    dq = jnp.concatenate([first, second], axis=1).reshape(KROWS, HEAD)
    dk = both[:, 0:BLOCK, :].reshape(KROWS, HEAD)
    dv = both[:, BLOCK:, :].reshape(KROWS, HEAD)
    grads = jnp.concatenate([dq, dk, dv], axis=1)
    made = dot(normed[...].reshape(KROWS, D // 2), grads, 0, 0)

    @pl.when(step == 0)
    def _():
        dw_s[...] = made

    @pl.when(step > 0)
    def _():
        dw_s[...] += made

    @pl.when(step == STEPS - 1)
    def _():
        every = dw_s[...].reshape(8, 2, 32, 3 * HEAD)
        here[...] = jnp.where(y == 0, every[:, 0], every[:, 1]).astype(BF16)
        there[...] = jnp.where(y == 0, every[:, 1], every[:, 0]).astype(BF16)


def weight_pass(meta, normed, part, came):
    pack = (4, HALF + 2 * BLOCK, HEAD)
    shape = (8, 32, 3 * HEAD)
    grid_spec = pltpu.PrefetchScalarGridSpec(
        num_scalar_prefetch=1,
        grid=(STEPS,),
        in_specs=[
            pl.BlockSpec((4, BLOCK, D // 2), lambda i, m: (i, 0, m[NBLK + 1])),
            pl.BlockSpec(pack, lambda i, m: (i, 0, 0)),
            pl.BlockSpec(pack, lambda i, m: (i, 0, 0)),
        ],
        out_specs=[pl.BlockSpec(shape, lambda i, m: (0, 0, 0))] * 2,
        scratch_shapes=[pltpu.VMEM((D // 2, 3 * HEAD), F32)],
    )
    return pl.pallas_call(
        weight_kernel,
        grid_spec=grid_spec,
        out_shape=[jax.ShapeDtypeStruct(shape, BF16)] * 2,
        name="weight_pass",
    )(meta, normed, part, came)


def join_kernel(meta, part, came, out):
    half = meta[NBLK + 1]
    for n in range(8):
        first, second, both = total_of(part, came, half, meta[half * 8 + n])
        out[n, 0:HALF, :] = first
        out[n, HALF:BLOCK, :] = second
        out[n, BLOCK:, :] = both


def join_pass(meta, part, came):
    shape = (NBLK, HALF + 2 * BLOCK, HEAD)
    made = (8, 3 * BLOCK, HEAD)
    grid_spec = pltpu.PrefetchScalarGridSpec(
        num_scalar_prefetch=1,
        grid=(1,),
        in_specs=[pl.BlockSpec(shape, lambda i, m: (0, 0, 0))] * 2,
        out_specs=pl.BlockSpec(made, lambda i, m: (0, 0, 0)),
    )
    return pl.pallas_call(
        join_kernel, grid_spec=grid_spec, out_shape=jax.ShapeDtypeStruct(made, BF16), name="join_pass"
    )(meta, part, came)


def rows_kernel(back, mine, gain, w, out, grad, d_norm):
    step = pl.program_id(0)

    @pl.when(step == 0)
    def _():
        for h in range(HEADS):
            for n in range(3):
                to = n * D + h * HEAD
                grad[:, to : to + HEAD] = back[h, n * BLOCK : (n + 1) * BLOCK, :]

    d_norm[pl.ds(pl.multiple_of(step * 256, 256), 256), :] = dot(w[...], grad[...], 1, 1)

    @pl.when(step == STEPS - 1)
    def _():
        values = mine[...].astype(F32)
        inverse = lax.rsqrt(jnp.mean(values * values, axis=-1, keepdims=True) + EPS)
        unit = values * inverse
        gained = d_norm[...].T * gain[...]
        shared = jnp.mean(gained * unit, axis=-1, keepdims=True)
        out[...] = (inverse * (gained - unit * shared)).astype(BF16)


def rows_pass(back, mine, gain, w_qkv):
    return pl.pallas_call(
        rows_kernel,
        grid=(STEPS,),
        in_specs=[
            pl.BlockSpec((HEADS, 3 * BLOCK, HEAD), lambda i: (0, 0, 0)),
            pl.BlockSpec((BLOCK, D), lambda i: (0, 0)),
            pl.BlockSpec((1, D), lambda i: (0, 0)),
            pl.BlockSpec((D // STEPS, 3 * D), lambda i: (i, 0)),
        ],
        out_specs=pl.BlockSpec((BLOCK, D), lambda i: (0, 0)),
        scratch_shapes=[
            pltpu.VMEM((BLOCK, 3 * D), BF16),
            pltpu.VMEM((D, BLOCK), F32),
        ],
        out_shape=jax.ShapeDtypeStruct((BLOCK, D), BF16),
        name="rows_pass",
    )(back, mine, gain, w_qkv)


def final_kernel(meta, own, other, out):
    half = meta[NBLK + 1]
    for side, ref in ((half, own), (1 - half, other)):
        row = pl.multiple_of(side * 32, 32)
        for h in range(HEADS):
            for n in range(3):
                value = ref[h, :, n * HEAD : (n + 1) * HEAD].astype(F32)
                out[pl.ds(row, 32), n * D + h * HEAD : n * D + (h + 1) * HEAD] = value * (1.0 / math.sqrt(32768))


def final_pass(meta, own, other):
    shape = (HEADS, 32, 3 * HEAD)
    grid_spec = pltpu.PrefetchScalarGridSpec(
        num_scalar_prefetch=1,
        grid=(1,),
        in_specs=[pl.BlockSpec(shape, lambda i, m: (0, 0, 0))] * 2,
        out_specs=pl.BlockSpec((64, 3 * D), lambda i, m: (0, 0)),
    )
    return pl.pallas_call(
        final_kernel, grid_spec=grid_spec, out_shape=jax.ShapeDtypeStruct((64, 3 * D), F32), name="final_pass"
    )(meta, own, other)


def flip(x, axis, bit, size):
    return lax.ppermute(x, axis, [(i, i ^ bit) for i in range(size)])


def ring(x, axis, by, size):
    return lax.ppermute(x, axis, [(i, (i + by) % size) for i in range(size)])


def turn(x, by=0, other=0):
    pairs = []
    for y in range(2):
        for z in range(8):
            for c in range(2):
                pairs.append(((y * 8 + z) * 2 + c, (c * 8 + (z + by) % 8) * 2 + (y ^ other)))
    return lax.ppermute(x, ("y_lo", "z", "core"), pairs)


def added(a, b):
    return (a.astype(F32) + b.astype(F32)).astype(BF16)


def relay(payload):
    home = turn(payload)
    down, up = turn(payload, -1), turn(payload, 1)
    made = [home, down, up]
    for _ in range(2):
        down, up = ring(down, "z", -1, 8), ring(up, "z", 1, 8)
        made += [down, up]
    made.append(ring(up[:HALF], "z", 1, 8))
    made.append(ring(down[HALF:], "z", -1, 8))
    return made


def work(layer_rows, doc_ids, packing, norm_gain, w_qkv, d_attn):
    z = lax.axis_index("z")
    y = lax.axis_index("y_lo")
    x = lax.axis_index("x")
    core = lax.axis_index("core")
    halves = doc_ids[0].astype(BF16).reshape(2, 1, HALF)
    at = (jnp.arange(4, dtype=jnp.int32) == z % 4).astype(BF16)[None, :, None]
    info = jnp.pad((halves * at).reshape(2, QROWS), ((0, EXTRA - 2), (0, D - QROWS)))
    payload = jnp.concatenate([layer_rows[0], info], axis=0)
    order = turn(packing[0])
    parts = d_attn[0].reshape(2, HALF, HEADS, HEAD).transpose(2, 0, 1, 3)
    parts = turn(parts.reshape(NBLK, HALF, HEAD))
    meta = jnp.concatenate([order, jnp.stack([z, core, y, x]).astype(jnp.int32)])
    gain = norm_gain[None, :]

    pieces = relay(payload)
    others = [flip(piece, "core", 1, 2) for piece in pieces]
    do = lax.all_to_all(parts, ("z", "core"), 0, 0, tiled=True)
    normed, mine, part = head_pass(meta, pieces, others, do, gain, w_qkv)
    came = flip(part, "core", 1, 2)
    here, there = weight_pass(meta, normed, part, came)
    back = join_pass(meta, part, came)
    back = lax.all_to_all(back, "z", 0, 0, tiled=True)

    here = turn(here)
    there = turn(there, 0, 1)
    w_sum = added(here, there)
    w_sum = added(w_sum, flip(w_sum, "x", 1, 4))
    w_sum = added(w_sum, flip(w_sum, "x", 2, 4))
    w_sum = added(w_sum, flip(w_sum, "y_hi", 1, 2))
    w_sum = lax.all_to_all(w_sum, "z", 0, 0, tiled=True)
    other = flip(w_sum, "core", 1, 2)
    w_grad = final_pass(meta, w_sum, other)

    d_rows = rows_pass(back, mine, gain, w_qkv)
    d_rows = turn(d_rows)
    return (d_rows[None], w_grad)


def solution(mesh):
    fine = Mesh(
        mesh.devices.reshape(2, 8, 4, 2, 2), ("y_lo", "z", "x", "y_hi", "core")
    )
    seq = ("y_lo", "z")
    dp = ("x", "y_hi", "core")
    return jax.shard_map(
        work,
        mesh=fine,
        in_specs=(
            P(dp, seq, None),
            P(dp, seq),
            P(dp, None),
            P(),
            P(),
            P(dp, seq, None),
        ),
        out_specs=(P(dp, seq, None), P(seq, None)),
        check_vma=False,
    )
```

profile of v0, /device:TPU:1, one launch (start us, length us, event | category | flops | bytes accessed | tf_op | source)
XLA Modules:
  0.0 142.5 jit_solution(3201083126928412532)
XLA Ops:
  0.7 0.7 convert_reduce_fusion
  1.7 1.0 fusion.1
  2.7 8.0 %collective-permute-start.2 = (bf16[136,1024]{1,0:T(8,128)(2,1)S(1)}, bf16[136,1024]{1,0:T(8,128)(2,1)S(1)}, u32[]{:S(2)}, u32[]{:S(2)}) collective-permute-start(bf16[136,1024]{1,0:T(8,128)(2,1)S(1)} %fusion.1), channel_id=1, source_target_pairs={{0,112},{1,240},{16,0},{17,128},{32,16},{33,144},{48,32},{49,160},... | collective-permute-start | bytes 835592 | tf_op jit(solution)/shard_map/ppermute | solution.py:341
  10.7 6.0 %collective-permute-done.2.refs_2_ = bf16[136,1024]{1,0:T(8,128)(2,1)S(1)} collective-permute-done((bf16[136,1024]{1,0:T(8,128)(2,1)S(1)}, bf16[136,1024]{1,0:T(8,128)(2,1)S(1)}, u32[]{:S(2)}, u32[]{:S(2)}) %collective-permute-start.2) | collective-permute-done | bytes 278560 | tf_op jit(solution)/shard_map/ppermute | solution.py:341
  16.7 4.0 %collective-permute-start.4 = (bf16[136,1024]{1,0:T(8,128)(2,1)S(1)}, bf16[136,1024]{1,0:T(8,128)(2,1)S(1)}, u32[]{:S(2)}, u32[]{:S(2)}) collective-permute-start(bf16[136,1024]{1,0:T(8,128)(2,1)S(1)} %collective-permute-done.2.refs_2_), channel_id=1, source_target_pairs={{0,112},{16,0},{32,16},{48,32},{64,48},{80,64},{96,80},{112,96},{1... | collective-permute-start | bytes 835592 | tf_op jit(solution)/shard_map/ppermute | solution.py:332
  20.7 3.1 %collective-permute-start.1 = (bf16[136,1024]{1,0:T(8,128)(2,1)S(1)}, bf16[136,1024]{1,0:T(8,128)(2,1)S(1)}, u32[]{:S(2)}, u32[]{:S(2)}) collective-permute-start(bf16[136,1024]{1,0:T(8,128)(2,1)S(1)} %fusion.1), channel_id=1, source_target_pairs={{0,0},{1,128},{16,16},{17,144},{32,32},{33,160},{48,48},{49,176},{... | collective-permute-start | bytes 835592 | tf_op jit(solution)/shard_map/ppermute | solution.py:341
  23.8 1.0 copy.9
  24.9 2.5 %collective-permute-start.19 = (bf16[16,64,128]{2,1,0:T(8,128)(2,1)S(1)}, bf16[16,64,128]{2,1,0:T(8,128)(2,1)S(1)}, u32[]{:S(2)}, u32[]{:S(2)}) collective-permute-start(bf16[16,64,128]{2,1,0:T(8,128)(2,1)S(1)} %bitcast.18), channel_id=1, source_target_pairs={{0,0},{1,128},{16,16},{17,144},{32,32},{33,160},{48,48},{49,176},{... | collective-permute-start | bytes 786440 | tf_op jit(solution)/shard_map/ppermute | solution.py:341
  27.4 2.9 %collective-permute-start.6 = (bf16[136,1024]{1,0:T(8,128)(2,1)S(1)}, bf16[136,1024]{1,0:T(8,128)(2,1)S(1)}, u32[]{:S(2)}, u32[]{:S(2)}) collective-permute-start(bf16[136,1024]{1,0:T(8,128)(2,1)S(1)} %collective-permute-done.4.refs_4_), channel_id=1, source_target_pairs={{0,112},{16,0},{32,16},{48,32},{64,48},{80,64},{96,80},{112,96},{1... | collective-permute-start | bytes 835592 | tf_op jit(solution)/shard_map/ppermute | solution.py:332
  30.3 3.5 %collective-permute-start = (s32[16]{0:T(128)}, s32[16]{0:T(128)S(1)}, u32[]{:S(2)}, u32[]{:S(2)}) collective-permute-start(s32[16]{0:T(128)} %bitcast.22), channel_id=1, source_target_pairs={{0,0},{1,128},{16,16},{17,144},{32,32},{33,160},{48,48},{49,176},{... | collective-permute-start | bytes 200 | tf_op jit(solution)/shard_map/ppermute | solution.py:341
  33.8 1.8 %collective-permute-done = s32[16]{0:T(128)S(1)} collective-permute-done((s32[16]{0:T(128)}, s32[16]{0:T(128)S(1)}, u32[]{:S(2)}, u32[]{:S(2)}) %collective-permute-start) | collective-permute-done | bytes 96 | tf_op jit(solution)/shard_map/ppermute | solution.py:341
  35.6 0.5 collective-permute-start.11
  36.1 0.2 collective-permute-start.10
  36.3 0.8 collective-permute-start.14
  37.2 5.1 %all-to-all-start = ((bf16[16,64,128]{2,1,0:T(8,128)(2,1)}), bf16[16,64,128]{2,1,0:T(8,128)(2,1)S(1)}, u32[]{:S(2)}, u32[]{:S(2)}) async-start(bf16[16,64,128]{2,1,0:T(8,128)(2,1)} %copy-done.15), calls=%async_computation | async-start | bytes 524288 | tf_op jit(solution)/shard_map/all_to_all | solution.py:377
  42.3 2.6 %collective-permute-start.9 = (bf16[72,1024]{1,0:T(8,128)(2,1)S(1)}, bf16[72,1024]{1,0:T(8,128)(2,1)S(1)}, u32[]{:S(2)}, u32[]{:S(2)}) collective-permute-start(bf16[72,1024]{1,0:T(8,128)(2,1)S(1)} %slice.9), channel_id=1, source_target_pairs={{0,112},{16,0},{32,16},{48,32},{64,48},{80,64},{96,80},{112,96},{1... | collective-permute-start | bytes 442376 | tf_op jit(solution)/shard_map/ppermute | solution.py:332
  44.9 0.7 collective-permute-start.13
  45.6 0.8 collective-permute-start.16
  46.6 6.7 %collective-permute-done.9.refs_9_ = bf16[72,1024]{1,0:T(8,128)(2,1)S(1)} collective-permute-done((bf16[72,1024]{1,0:T(8,128)(2,1)S(1)}, bf16[72,1024]{1,0:T(8,128)(2,1)S(1)}, u32[]{:S(2)}, u32[]{:S(2)}) %collective-permute-start.9) | collective-permute-done | bytes 147488 | tf_op jit(solution)/shard_map/ppermute | solution.py:332
  53.4 0.9 collective-permute-start.18
  54.2 0.2 collective-permute-done.8.refs_8_
  54.4 0.8 collective-permute-start.17
  55.2 0.7 concatenate.6.refs_0_.meta
  55.9 0.7 collective-permute-done.17.refs_17_
  56.7 19.9 %head_pass.1 = (bf16[16,128,1024]{2,1,0:T(8,128)(2,1)}, bf16[128,1024]{1,0:T(8,128)(2,1)}, bf16[16,320,128]{2,1,0:T(8,128)(2,1)}) custom-call(s32[20]{0:T(128)} %concatenate.6.refs_0_.meta, bf16[136,1024]{1,0:T(8,128)(2,1)} %copy-done.10, bf16[136,1024]{1,0:T(8,128)(2,1)} %copy-done.6, bf16[136,1024]{1,0:T(8,128)(2,1)} %copy-done.7, ...), custom_call_target="tpu_custom_call" | custom-call | tf_op jit(solution)/shard_map/head_pass/pallas_call | solution.py:170
  76.6 0.4 collective-permute-start.20
  77.0 2.9 %collective-permute-done.20.came = bf16[16,320,128]{2,1,0:T(8,128)(2,1)S(1)} collective-permute-done((bf16[16,320,128]{2,1,0:T(8,128)(2,1)}, bf16[16,320,128]{2,1,0:T(8,128)(2,1)S(1)}, u32[]{:S(2)}, u32[]{:S(2)}) %collective-permute-start.20) | collective-permute-done | bytes 1310752 | tf_op jit(solution)/shard_map/ppermute | solution.py:328
  79.9 1.1 copy-done
  81.0 5.7 %weight_pass.1 = (bf16[8,32,384]{2,1,0:T(8,128)(2,1)}, bf16[8,32,384]{2,1,0:T(8,128)(2,1)}) custom-call(s32[20]{0:T(128)} %concatenate.6.refs_0_.meta, bf16[16,128,1024]{2,1,0:T(8,128)(2,1)} %get-tuple-element.9.normed, bf16[16,320,128]{2,1,0:T(8,128)(2,1)} %get-tuple-element.7.part, bf16[16,320,128]{2,1,0:T(8,128)(2,1)} %copy-done), custom_call_target="tpu_custom_call" | custom-call | tf_op jit(solution)/shard_map/weight_pass/pallas_call | solution.py:231
  86.6 2.9 %collective-permute-start.22 = (bf16[8,32,384]{2,1,0:T(8,128)(2,1)}, bf16[8,32,384]{2,1,0:T(8,128)(2,1)S(1)}, u32[]{:S(2)}, u32[]{:S(2)}) collective-permute-start(bf16[8,32,384]{2,1,0:T(8,128)(2,1)} %get-tuple-element.10), channel_id=1, source_target_pairs={{0,0},{1,128},{16,16},{17,144},{32,32},{33,160},{48,48},{49,176},{... | collective-permute-start | bytes 589832 | tf_op jit(solution)/shard_map/ppermute | solution.py:341
  89.7 3.4 %join_pass.1 = bf16[8,384,128]{2,1,0:T(8,128)(2,1)} custom-call(s32[20]{0:T(128)} %concatenate.6.refs_0_.meta, bf16[16,320,128]{2,1,0:T(8,128)(2,1)} %get-tuple-element.7.part, bf16[16,320,128]{2,1,0:T(8,128)(2,1)} %copy-done), custom_call_target="tpu_custom_call" | custom-call | tf_op jit(solution)/shard_map/join_pass/pallas_call | solution.py:257
  93.1 4.4 %all-to-all-start.1 = ((bf16[8,384,128]{2,1,0:T(8,128)(2,1)}), bf16[8,384,128]{2,1,0:T(8,128)(2,1)S(1)}, u32[]{:S(2)}, u32[]{:S(2)}) async-start(bf16[8,384,128]{2,1,0:T(8,128)(2,1)} %join_pass.1), calls=%async_computation.1 | async-start | bytes 1572864 | tf_op jit(solution)/shard_map/all_to_all | solution.py:382
  97.5 1.3 collective-permute-start.24
  98.8 4.5 %collective-permute-done.24 = bf16[8,32,384]{2,1,0:T(8,128)(2,1)S(1)} collective-permute-done((bf16[8,32,384]{2,1,0:T(8,128)(2,1)S(1)}, bf16[8,32,384]{2,1,0:T(8,128)(2,1)S(1)}, u32[]{:S(2)}, u32[]{:S(2)}) %collective-permute-start.24) | collective-permute-done | bytes 196640 | tf_op jit(solution)/shard_map/ppermute | solution.py:328
  103.4 2.8 %collective-permute-start.25 = (bf16[8,32,384]{2,1,0:T(8,128)(2,1)S(1)}, bf16[8,32,384]{2,1,0:T(8,128)(2,1)S(1)}, u32[]{:S(2)}, u32[]{:S(2)}) collective-permute-start(bf16[8,32,384]{2,1,0:T(8,128)(2,1)S(1)} %add_convert_fusion.2), channel_id=1, source_target_pairs={{0,8},{4,12},{8,0},{12,4},{1,9},{5,13},{9,1},{13,5},{2,10},{6,14},... | collective-permute-start | bytes 589832 | tf_op jit(solution)/shard_map/ppermute | solution.py:328
  106.2 3.6 %collective-permute-done.25 = bf16[8,32,384]{2,1,0:T(8,128)(2,1)S(1)} collective-permute-done((bf16[8,32,384]{2,1,0:T(8,128)(2,1)S(1)}, bf16[8,32,384]{2,1,0:T(8,128)(2,1)S(1)}, u32[]{:S(2)}, u32[]{:S(2)}) %collective-permute-start.25) | collective-permute-done | bytes 196640 | tf_op jit(solution)/shard_map/ppermute | solution.py:328
  109.8 3.0 %collective-permute-start.26 = (bf16[8,32,384]{2,1,0:T(8,128)(2,1)S(1)}, bf16[8,32,384]{2,1,0:T(8,128)(2,1)S(1)}, u32[]{:S(2)}, u32[]{:S(2)}) collective-permute-start(bf16[8,32,384]{2,1,0:T(8,128)(2,1)S(1)} %add_convert_fusion.1), channel_id=1, source_target_pairs={{0,2},{2,0},{1,3},{3,1},{4,6},{6,4},{5,7},{7,5},{8,10},{10,8},{9,1... | collective-permute-start | bytes 589832 | tf_op jit(solution)/shard_map/ppermute | solution.py:328
  112.8 3.1 %collective-permute-done.26 = bf16[8,32,384]{2,1,0:T(8,128)(2,1)S(1)} collective-permute-done((bf16[8,32,384]{2,1,0:T(8,128)(2,1)S(1)}, bf16[8,32,384]{2,1,0:T(8,128)(2,1)S(1)}, u32[]{:S(2)}, u32[]{:S(2)}) %collective-permute-start.26) | collective-permute-done | bytes 196640 | tf_op jit(solution)/shard_map/ppermute | solution.py:328
  115.9 0.7 add_convert_fusion
  116.7 4.3 %all-to-all-done.1.back = bf16[8,384,128]{2,1,0:T(8,128)(2,1)S(1)} async-done(((bf16[8,384,128]{2,1,0:T(8,128)(2,1)}), bf16[8,384,128]{2,1,0:T(8,128)(2,1)S(1)}, u32[]{:S(2)}, u32[]{:S(2)}) %all-to-all-start.1) | async-done | bytes 786464 | tf_op jit(solution)/shard_map/all_to_all | solution.py:382
  121.0 3.4 %all-to-all-start.2 = ((bf16[8,32,384]{2,1,0:T(8,128)(2,1)}), bf16[8,32,384]{2,1,0:T(8,128)(2,1)S(1)}, u32[]{:S(2)}, u32[]{:S(2)}) async-start(bf16[8,32,384]{2,1,0:T(8,128)(2,1)} %add_convert_fusion), calls=%async_computation.2 | async-start | bytes 393216 | tf_op jit(solution)/shard_map/all_to_all | solution.py:390
  124.4 6.3 %rows_pass.1 = bf16[128,1024]{1,0:T(8,128)(2,1)} custom-call(bf16[8,384,128]{2,1,0:T(8,128)(2,1)} %copy-done.1, bf16[128,1024]{1,0:T(8,128)(2,1)} %get-tuple-element.8.mine, f32[1,1024]{1,0:T(1,128)} %bitcast.21, bf16[1024,3072]{1,0:T(8,128)(2,1)} %w.1), custom_call_target="tpu_custom_call" | custom-call | tf_op jit(solution)/shard_map/rows_pass/pallas_call | solution.py:285
  130.8 6.1 %collective-permute-start.21 = (bf16[128,1024]{1,0:T(8,128)(2,1)}, bf16[128,1024]{1,0:T(8,128)(2,1)S(1)}, u32[]{:S(2)}, u32[]{:S(2)}) collective-permute-start(bf16[128,1024]{1,0:T(8,128)(2,1)} %rows_pass.1), channel_id=1, source_target_pairs={{0,0},{1,128},{16,16},{17,144},{32,32},{33,160},{48,48},{49,176},{... | collective-permute-start | bytes 786440 | tf_op jit(solution)/shard_map/ppermute | solution.py:341
  136.9 0.1 collective-permute-start.27
  137.0 1.4 collective-permute-done.27.other
  138.4 0.7 copy-done.16
  139.1 2.6 %final_pass.1 = f32[64,3072]{1,0:T(8,128)} custom-call(s32[20]{0:T(128)} %concatenate.6.refs_0_.meta, bf16[8,32,384]{2,1,0:T(8,128)(2,1)} %copy-done.3, bf16[8,32,384]{2,1,0:T(8,128)(2,1)} %copy-done.16), custom_call_target="tpu_custom_call" | custom-call | tf_op jit(solution)/shard_map/final_pass/pallas_call | solution.py:322
  141.8 0.7 copy.11
  (74 shorter events, 1.0 us)
Async XLA Ops:
  2.7 14.1 %collective-permute-start.2 = (bf16[136,1024]{1,0:T(8,128)(2,1)S(1)}, bf16[136,1024]{1,0:T(8,128)(2,1)S(1)}, u32[]{:S(2)}, u32[]{:S(2)}) collective-permute-start(bf16[136,1024]{1,0:T(8,128)(2,1)S(1)} %fusion.1), channel_id=1, source_target_pairs={{0,112},{1,240},{16,0},{17,128},{32,16},{33,144},{48,32},{49,160},... | collective-permute-start | bytes 835592 | tf_op jit(solution)/shard_map/ppermute | solution.py:341
  10.7 10.0 %collective-permute-start.3 = (bf16[136,1024]{1,0:T(8,128)(2,1)S(1)}, bf16[136,1024]{1,0:T(8,128)(2,1)S(1)}, u32[]{:S(2)}, u32[]{:S(2)}) collective-permute-start(bf16[136,1024]{1,0:T(8,128)(2,1)S(1)} %fusion.1), channel_id=1, source_target_pairs={{0,16},{1,144},{16,32},{17,160},{32,48},{33,176},{48,64},{49,192},... | collective-permute-start | bytes 835592 | tf_op jit(solution)/shard_map/ppermute | solution.py:341
  16.7 39.8 %copy-start.6 = (bf16[136,1024]{1,0:T(8,128)(2,1)}, bf16[136,1024]{1,0:T(8,128)(2,1)S(1)}, u32[]{:S(2)}) copy-start(bf16[136,1024]{1,0:T(8,128)(2,1)S(1)} %collective-permute-done.2.refs_2_) | copy-start | bytes 835588
  16.7 10.6 %collective-permute-start.4 = (bf16[136,1024]{1,0:T(8,128)(2,1)S(1)}, bf16[136,1024]{1,0:T(8,128)(2,1)S(1)}, u32[]{:S(2)}, u32[]{:S(2)}) collective-permute-start(bf16[136,1024]{1,0:T(8,128)(2,1)S(1)} %collective-permute-done.2.refs_2_), channel_id=1, source_target_pairs={{0,112},{16,0},{32,16},{48,32},{64,48},{80,64},{96,80},{112,96},{1... | collective-permute-start | bytes 835592 | tf_op jit(solution)/shard_map/ppermute | solution.py:332
  20.7 35.8 %copy-start.7 = (bf16[136,1024]{1,0:T(8,128)(2,1)}, bf16[136,1024]{1,0:T(8,128)(2,1)S(1)}, u32[]{:S(2)}) copy-start(bf16[136,1024]{1,0:T(8,128)(2,1)S(1)} %collective-permute-done.3.refs_3_) | copy-start | bytes 835588
  20.7 15.4 %collective-permute-start.5 = (bf16[136,1024]{1,0:T(8,128)(2,1)S(1)}, bf16[136,1024]{1,0:T(8,128)(2,1)S(1)}, u32[]{:S(2)}, u32[]{:S(2)}) collective-permute-start(bf16[136,1024]{1,0:T(8,128)(2,1)S(1)} %collective-permute-done.3.refs_3_), channel_id=1, source_target_pairs={{0,16},{16,32},{32,48},{48,64},{64,80},{80,96},{96,112},{112,0},{1... | collective-permute-start | bytes 835592 | tf_op jit(solution)/shard_map/ppermute | solution.py:332
  20.7 15.4 %collective-permute-start.1 = (bf16[136,1024]{1,0:T(8,128)(2,1)S(1)}, bf16[136,1024]{1,0:T(8,128)(2,1)S(1)}, u32[]{:S(2)}, u32[]{:S(2)}) collective-permute-start(bf16[136,1024]{1,0:T(8,128)(2,1)S(1)} %fusion.1), channel_id=1, source_target_pairs={{0,0},{1,128},{16,16},{17,144},{32,32},{33,160},{48,48},{49,176},{... | collective-permute-start | bytes 835592 | tf_op jit(solution)/shard_map/ppermute | solution.py:341
  24.9 10.7 %collective-permute-start.19 = (bf16[16,64,128]{2,1,0:T(8,128)(2,1)S(1)}, bf16[16,64,128]{2,1,0:T(8,128)(2,1)S(1)}, u32[]{:S(2)}, u32[]{:S(2)}) collective-permute-start(bf16[16,64,128]{2,1,0:T(8,128)(2,1)S(1)} %bitcast.18), channel_id=1, source_target_pairs={{0,0},{1,128},{16,16},{17,144},{32,32},{33,160},{48,48},{49,176},{... | collective-permute-start | bytes 786440 | tf_op jit(solution)/shard_map/ppermute | solution.py:341
  27.4 29.2 %copy-start.8 = (bf16[136,1024]{1,0:T(8,128)(2,1)}, bf16[136,1024]{1,0:T(8,128)(2,1)S(1)}, u32[]{:S(2)}) copy-start(bf16[136,1024]{1,0:T(8,128)(2,1)S(1)} %collective-permute-done.4.refs_4_) | copy-start | bytes 835588
  27.4 8.9 %collective-permute-start.6 = (bf16[136,1024]{1,0:T(8,128)(2,1)S(1)}, bf16[136,1024]{1,0:T(8,128)(2,1)S(1)}, u32[]{:S(2)}, u32[]{:S(2)}) collective-permute-start(bf16[136,1024]{1,0:T(8,128)(2,1)S(1)} %collective-permute-done.4.refs_4_), channel_id=1, source_target_pairs={{0,112},{16,0},{32,16},{48,32},{64,48},{80,64},{96,80},{112,96},{1... | collective-permute-start | bytes 835592 | tf_op jit(solution)/shard_map/ppermute | solution.py:332
  30.3 5.3 %collective-permute-start = (s32[16]{0:T(128)}, s32[16]{0:T(128)S(1)}, u32[]{:S(2)}, u32[]{:S(2)}) collective-permute-start(s32[16]{0:T(128)} %bitcast.22), channel_id=1, source_target_pairs={{0,0},{1,128},{16,16},{17,144},{32,32},{33,160},{48,48},{49,176},{... | collective-permute-start | bytes 200 | tf_op jit(solution)/shard_map/ppermute | solution.py:341
  35.6 6.7 %collective-permute-start.12 = (bf16[136,1024]{1,0:T(8,128)(2,1)S(1)}, bf16[136,1024]{1,0:T(8,128)(2,1)S(1)}, u32[]{:S(2)}, u32[]{:S(2)}) collective-permute-start(bf16[136,1024]{1,0:T(8,128)(2,1)S(1)} %collective-permute-done.3.refs_3_), channel_id=1, source_target_pairs={{0,1},{1,0},{2,3},{3,2},{4,5},{5,4},{6,7},{7,6},{8,9},{9,8},{10,11... | collective-permute-start | bytes 835592 | tf_op jit(solution)/shard_map/ppermute | solution.py:328
  35.6 0.7 copy-start.15
  35.6 9.3 %collective-permute-start.11 = (bf16[136,1024]{1,0:T(8,128)(2,1)S(1)}, bf16[136,1024]{1,0:T(8,128)(2,1)S(1)}, u32[]{:S(2)}, u32[]{:S(2)}) collective-permute-start(bf16[136,1024]{1,0:T(8,128)(2,1)S(1)} %collective-permute-done.2.refs_2_), channel_id=1, source_target_pairs={{0,1},{1,0},{2,3},{3,2},{4,5},{5,4},{6,7},{7,6},{8,9},{9,8},{10,11... | collective-permute-start | bytes 835592 | tf_op jit(solution)/shard_map/ppermute | solution.py:328
  36.1 20.5 %copy-start.9 = (bf16[136,1024]{1,0:T(8,128)(2,1)}, bf16[136,1024]{1,0:T(8,128)(2,1)S(1)}, u32[]{:S(2)}) copy-start(bf16[136,1024]{1,0:T(8,128)(2,1)S(1)} %collective-permute-done.5.refs_5_) | copy-start | bytes 835588
  36.1 9.5 %collective-permute-start.7 = (bf16[136,1024]{1,0:T(8,128)(2,1)S(1)}, bf16[136,1024]{1,0:T(8,128)(2,1)S(1)}, u32[]{:S(2)}, u32[]{:S(2)}) collective-permute-start(bf16[136,1024]{1,0:T(8,128)(2,1)S(1)} %collective-permute-done.5.refs_5_), channel_id=1, source_target_pairs={{0,16},{16,32},{32,48},{48,64},{64,80},{80,96},{96,112},{112,0},{1... | collective-permute-start | bytes 835592 | tf_op jit(solution)/shard_map/ppermute | solution.py:332
  36.1 20.5 %copy-start.10 = (bf16[136,1024]{1,0:T(8,128)(2,1)}, bf16[136,1024]{1,0:T(8,128)(2,1)S(1)}, u32[]{:S(2)}) copy-start(bf16[136,1024]{1,0:T(8,128)(2,1)S(1)} %collective-permute-done.1.refs_1_) | copy-start | bytes 835588
  36.1 10.3 %collective-permute-start.10 = (bf16[136,1024]{1,0:T(8,128)(2,1)S(1)}, bf16[136,1024]{1,0:T(8,128)(2,1)S(1)}, u32[]{:S(2)}, u32[]{:S(2)}) collective-permute-start(bf16[136,1024]{1,0:T(8,128)(2,1)S(1)} %collective-permute-done.1.refs_1_), channel_id=1, source_target_pairs={{0,1},{1,0},{2,3},{3,2},{4,5},{5,4},{6,7},{7,6},{8,9},{9,8},{10,11... | collective-permute-start | bytes 835592 | tf_op jit(solution)/shard_map/ppermute | solution.py:328
  36.3 20.3 %copy-start.4 = (bf16[136,1024]{1,0:T(8,128)(2,1)}, bf16[136,1024]{1,0:T(8,128)(2,1)S(1)}, u32[]{:S(2)}) copy-start(bf16[136,1024]{1,0:T(8,128)(2,1)S(1)} %collective-permute-done.6.refs_6_) | copy-start | bytes 835588
  36.3 10.2 %collective-permute-start.14 = (bf16[136,1024]{1,0:T(8,128)(2,1)S(1)}, bf16[136,1024]{1,0:T(8,128)(2,1)S(1)}, u32[]{:S(2)}, u32[]{:S(2)}) collective-permute-start(bf16[136,1024]{1,0:T(8,128)(2,1)S(1)} %collective-permute-done.5.refs_5_), channel_id=1, source_target_pairs={{0,1},{1,0},{2,3},{3,2},{4,5},{5,4},{6,7},{7,6},{8,9},{9,8},{10,11... | collective-permute-start | bytes 835592 | tf_op jit(solution)/shard_map/ppermute | solution.py:328
  37.2 18.7 %all-to-all-start = ((bf16[16,64,128]{2,1,0:T(8,128)(2,1)}), bf16[16,64,128]{2,1,0:T(8,128)(2,1)S(1)}, u32[]{:S(2)}, u32[]{:S(2)}) async-start(bf16[16,64,128]{2,1,0:T(8,128)(2,1)} %copy-done.15), calls=%async_computation | async-start | bytes 524288 | tf_op jit(solution)/shard_map/all_to_all | solution.py:377
  42.3 14.3 %copy-start.11 = (bf16[136,1024]{1,0:T(8,128)(2,1)}, bf16[136,1024]{1,0:T(8,128)(2,1)S(1)}, u32[]{:S(2)}) copy-start(bf16[136,1024]{1,0:T(8,128)(2,1)S(1)} %collective-permute-done.12.refs_12_) | copy-start | bytes 835588
  42.3 11.1 %collective-permute-start.9 = (bf16[72,1024]{1,0:T(8,128)(2,1)S(1)}, bf16[72,1024]{1,0:T(8,128)(2,1)S(1)}, u32[]{:S(2)}, u32[]{:S(2)}) collective-permute-start(bf16[72,1024]{1,0:T(8,128)(2,1)S(1)} %slice.9), channel_id=1, source_target_pairs={{0,112},{16,0},{32,16},{48,32},{64,48},{80,64},{96,80},{112,96},{1... | collective-permute-start | bytes 442376 | tf_op jit(solution)/shard_map/ppermute | solution.py:332
  44.9 11.7 %copy-start.12 = (bf16[136,1024]{1,0:T(8,128)(2,1)}, bf16[136,1024]{1,0:T(8,128)(2,1)S(1)}, u32[]{:S(2)}) copy-start(bf16[136,1024]{1,0:T(8,128)(2,1)S(1)} %collective-permute-done.11.refs_11_) | copy-start | bytes 835588
  44.9 10.9 %collective-permute-start.13 = (bf16[136,1024]{1,0:T(8,128)(2,1)S(1)}, bf16[136,1024]{1,0:T(8,128)(2,1)}, u32[]{:S(2)}, u32[]{:S(2)}) collective-permute-start(bf16[136,1024]{1,0:T(8,128)(2,1)S(1)} %collective-permute-done.4.refs_4_), channel_id=1, source_target_pairs={{0,1},{1,0},{2,3},{3,2},{4,5},{5,4},{6,7},{7,6},{8,9},{9,8},{10,11... | collective-permute-start | bytes 835592 | tf_op jit(solution)/shard_map/ppermute | solution.py:328
  45.6 11.0 %copy-start.5 = (bf16[136,1024]{1,0:T(8,128)(2,1)}, bf16[136,1024]{1,0:T(8,128)(2,1)S(1)}, u32[]{:S(2)}) copy-start(bf16[136,1024]{1,0:T(8,128)(2,1)S(1)} %collective-permute-done.7.refs_7_) | copy-start | bytes 835588
  45.6 10.9 %collective-permute-start.16 = (bf16[136,1024]{1,0:T(8,128)(2,1)S(1)}, bf16[136,1024]{1,0:T(8,128)(2,1)}, u32[]{:S(2)}, u32[]{:S(2)}) collective-permute-start(bf16[136,1024]{1,0:T(8,128)(2,1)S(1)} %collective-permute-done.7.refs_7_), channel_id=1, source_target_pairs={{0,1},{1,0},{2,3},{3,2},{4,5},{5,4},{6,7},{7,6},{8,9},{9,8},{10,11... | collective-permute-start | bytes 835592 | tf_op jit(solution)/shard_map/ppermute | solution.py:328
  46.4 10.2 %copy-start.13 = (bf16[136,1024]{1,0:T(8,128)(2,1)}, bf16[136,1024]{1,0:T(8,128)(2,1)S(1)}, u32[]{:S(2)}) copy-start(bf16[136,1024]{1,0:T(8,128)(2,1)S(1)} %collective-permute-done.10.refs_10_) | copy-start | bytes 835588
  46.4 10.1 %collective-permute-start.15 = (bf16[136,1024]{1,0:T(8,128)(2,1)S(1)}, bf16[136,1024]{1,0:T(8,128)(2,1)}, u32[]{:S(2)}, u32[]{:S(2)}) collective-permute-start(bf16[136,1024]{1,0:T(8,128)(2,1)S(1)} %collective-permute-done.6.refs_6_), channel_id=1, source_target_pairs={{0,1},{1,0},{2,3},{3,2},{4,5},{5,4},{6,7},{7,6},{8,9},{9,8},{10,11... | collective-permute-start | bytes 835592 | tf_op jit(solution)/shard_map/ppermute | solution.py:328
  46.5 10.1 %copy-start.14 = (bf16[136,1024]{1,0:T(8,128)(2,1)}, bf16[136,1024]{1,0:T(8,128)(2,1)S(1)}, u32[]{:S(2)}) copy-start(bf16[136,1024]{1,0:T(8,128)(2,1)S(1)} %collective-permute-done.14.refs_14_) | copy-start | bytes 835588
  46.5 7.9 %collective-permute-start.8 = (bf16[64,1024]{1,0:T(8,128)(2,1)S(1)}, bf16[64,1024]{1,0:T(8,128)(2,1)}, u32[]{:S(2)}, u32[]{:S(2)}) collective-permute-start(bf16[64,1024]{1,0:T(8,128)(2,1)S(1)} %slice.8), channel_id=1, source_target_pairs={{0,16},{16,32},{32,48},{48,64},{64,80},{80,96},{96,112},{112,0},{1... | collective-permute-start | bytes 393224 | tf_op jit(solution)/shard_map/ppermute | solution.py:332
  53.4 3.3 %copy-start.17 = (bf16[72,1024]{1,0:T(8,128)(2,1)}, bf16[72,1024]{1,0:T(8,128)(2,1)S(1)}, u32[]{:S(2)}) copy-start(bf16[72,1024]{1,0:T(8,128)(2,1)S(1)} %collective-permute-done.9.refs_9_) | copy-start | bytes 442372
  53.4 3.2 %collective-permute-start.18 = (bf16[72,1024]{1,0:T(8,128)(2,1)S(1)}, bf16[72,1024]{1,0:T(8,128)(2,1)}, u32[]{:S(2)}, u32[]{:S(2)}) collective-permute-start(bf16[72,1024]{1,0:T(8,128)(2,1)S(1)} %collective-permute-done.9.refs_9_), channel_id=1, source_target_pairs={{0,1},{1,0},{2,3},{3,2},{4,5},{5,4},{6,7},{7,6},{8,9},{9,8},{10,11... | collective-permute-start | bytes 442376 | tf_op jit(solution)/shard_map/ppermute | solution.py:328
  54.4 2.1 %collective-permute-start.17 = (bf16[64,1024]{1,0:T(8,128)(2,1)}, bf16[64,1024]{1,0:T(8,128)(2,1)}, u32[]{:S(2)}, u32[]{:S(2)}) collective-permute-start(bf16[64,1024]{1,0:T(8,128)(2,1)} %collective-permute-done.8.refs_8_), channel_id=1, source_target_pairs={{0,1},{1,0},{2,3},{3,2},{4,5},{5,4},{6,7},{7,6},{8,9},{9,8},{10,11... | collective-permute-start | bytes 393224 | tf_op jit(solution)/shard_map/ppermute | solution.py:328
  55.9 0.8 copy-start.2
  76.6 3.3 %collective-permute-start.20 = (bf16[16,320,128]{2,1,0:T(8,128)(2,1)}, bf16[16,320,128]{2,1,0:T(8,128)(2,1)S(1)}, u32[]{:S(2)}, u32[]{:S(2)}) collective-permute-start(bf16[16,320,128]{2,1,0:T(8,128)(2,1)} %get-tuple-element.7.part), channel_id=1, source_target_pairs={{0,1},{1,0},{2,3},{3,2},{4,5},{5,4},{6,7},{7,6},{8,9},{9,8},{10,11... | collective-permute-start | bytes 3932168 | tf_op jit(solution)/shard_map/ppermute | solution.py:328
  79.9 1.1 copy-start
  86.6 10.8 %collective-permute-start.22 = (bf16[8,32,384]{2,1,0:T(8,128)(2,1)}, bf16[8,32,384]{2,1,0:T(8,128)(2,1)S(1)}, u32[]{:S(2)}, u32[]{:S(2)}) collective-permute-start(bf16[8,32,384]{2,1,0:T(8,128)(2,1)} %get-tuple-element.10), channel_id=1, source_target_pairs={{0,0},{1,128},{16,16},{17,144},{32,32},{33,160},{48,48},{49,176},{... | collective-permute-start | bytes 589832 | tf_op jit(solution)/shard_map/ppermute | solution.py:341
  89.6 7.9 %collective-permute-start.23 = (bf16[8,32,384]{2,1,0:T(8,128)(2,1)}, bf16[8,32,384]{2,1,0:T(8,128)(2,1)S(1)}, u32[]{:S(2)}, u32[]{:S(2)}) collective-permute-start(bf16[8,32,384]{2,1,0:T(8,128)(2,1)} %get-tuple-element.11), channel_id=1, source_target_pairs={{0,1},{1,129},{16,17},{17,145},{32,33},{33,161},{48,49},{49,177},{... | collective-permute-start | bytes 589832 | tf_op jit(solution)/shard_map/ppermute | solution.py:341
  93.1 27.9 %all-to-all-start.1 = ((bf16[8,384,128]{2,1,0:T(8,128)(2,1)}), bf16[8,384,128]{2,1,0:T(8,128)(2,1)S(1)}, u32[]{:S(2)}, u32[]{:S(2)}) async-start(bf16[8,384,128]{2,1,0:T(8,128)(2,1)} %join_pass.1), calls=%async_computation.1 | async-start | bytes 1572864 | tf_op jit(solution)/shard_map/all_to_all | solution.py:382
  97.5 5.8 %collective-permute-start.24 = (bf16[8,32,384]{2,1,0:T(8,128)(2,1)S(1)}, bf16[8,32,384]{2,1,0:T(8,128)(2,1)S(1)}, u32[]{:S(2)}, u32[]{:S(2)}) collective-permute-start(bf16[8,32,384]{2,1,0:T(8,128)(2,1)S(1)} %add_convert_fusion.3), channel_id=1, source_target_pairs={{0,4},{4,0},{8,12},{12,8},{1,5},{5,1},{9,13},{13,9},{2,6},{6,2},{1... | collective-permute-start | bytes 589832 | tf_op jit(solution)/shard_map/ppermute | solution.py:328
  103.4 6.4 %collective-permute-start.25 = (bf16[8,32,384]{2,1,0:T(8,128)(2,1)S(1)}, bf16[8,32,384]{2,1,0:T(8,128)(2,1)S(1)}, u32[]{:S(2)}, u32[]{:S(2)}) collective-permute-start(bf16[8,32,384]{2,1,0:T(8,128)(2,1)S(1)} %add_convert_fusion.2), channel_id=1, source_target_pairs={{0,8},{4,12},{8,0},{12,4},{1,9},{5,13},{9,1},{13,5},{2,10},{6,14},... | collective-permute-start | bytes 589832 | tf_op jit(solution)/shard_map/ppermute | solution.py:328
  109.8 6.1 %collective-permute-start.26 = (bf16[8,32,384]{2,1,0:T(8,128)(2,1)S(1)}, bf16[8,32,384]{2,1,0:T(8,128)(2,1)S(1)}, u32[]{:S(2)}, u32[]{:S(2)}) collective-permute-start(bf16[8,32,384]{2,1,0:T(8,128)(2,1)S(1)} %add_convert_fusion.1), channel_id=1, source_target_pairs={{0,2},{2,0},{1,3},{3,1},{4,6},{6,4},{5,7},{7,5},{8,10},{10,8},{9,1... | collective-permute-start | bytes 589832 | tf_op jit(solution)/shard_map/ppermute | solution.py:328
  121.0 3.4 %copy-start.1 = (bf16[8,384,128]{2,1,0:T(8,128)(2,1)}, bf16[8,384,128]{2,1,0:T(8,128)(2,1)S(1)}, u32[]{:S(2)}) copy-start(bf16[8,384,128]{2,1,0:T(8,128)(2,1)S(1)} %all-to-all-done.1.back) | copy-start | bytes 2359300
  121.0 15.8 %all-to-all-start.2 = ((bf16[8,32,384]{2,1,0:T(8,128)(2,1)}), bf16[8,32,384]{2,1,0:T(8,128)(2,1)S(1)}, u32[]{:S(2)}, u32[]{:S(2)}) async-start(bf16[8,32,384]{2,1,0:T(8,128)(2,1)} %add_convert_fusion), calls=%async_computation.2 | async-start | bytes 393216 | tf_op jit(solution)/shard_map/all_to_all | solution.py:390
  130.8 11.0 %collective-permute-start.21 = (bf16[128,1024]{1,0:T(8,128)(2,1)}, bf16[128,1024]{1,0:T(8,128)(2,1)S(1)}, u32[]{:S(2)}, u32[]{:S(2)}) collective-permute-start(bf16[128,1024]{1,0:T(8,128)(2,1)} %rows_pass.1), channel_id=1, source_target_pairs={{0,0},{1,128},{16,16},{17,144},{32,32},{33,160},{48,48},{49,176},{... | collective-permute-start | bytes 786440 | tf_op jit(solution)/shard_map/ppermute | solution.py:341
  136.9 1.5 %copy-start.3 = (bf16[8,32,384]{2,1,0:T(8,128)(2,1)}, bf16[8,32,384]{2,1,0:T(8,128)(2,1)S(1)}, u32[]{:S(2)}) copy-start(bf16[8,32,384]{2,1,0:T(8,128)(2,1)S(1)} %all-to-all-done.2.own) | copy-start | bytes 589828
  136.9 1.5 %collective-permute-start.27 = (bf16[8,32,384]{2,1,0:T(8,128)(2,1)S(1)}, bf16[8,32,384]{2,1,0:T(8,128)(2,1)S(1)}, u32[]{:S(2)}, u32[]{:S(2)}) collective-permute-start(bf16[8,32,384]{2,1,0:T(8,128)(2,1)S(1)} %all-to-all-done.2.own), channel_id=1, source_target_pairs={{0,1},{1,0},{2,3},{3,2},{4,5},{5,4},{6,7},{7,6},{8,9},{9,8},{10,11... | collective-permute-start | bytes 589832 | tf_op jit(solution)/shard_map/ppermute | solution.py:328
  (1 other events, 0.7 us)
where the time goes:
time: 143 us; the launch traced here: 142 us
  starting transfers between devices  61.1 us (43%)
  Pallas kernels  37.9 us (27%)
  waiting for transfers between devices  35.3 us (25%)
  local copies, waits for them, and re-layouts  4.57 us (3%)
  other arithmetic  2.56 us (2%)
    ppermute x8, starting transfers between devices, turn(): return lax.ppermute(x, ('y_lo', 'z', 'core'), pairs)  26.2 us
    pallas_call x1, Pallas kernels, head_pass(): pl.pallas_call(head_kernel, grid_spec=grid_spec, out_shape=[jax.ShapeDtyp...  19.9 us
    ppermute x14, waiting for transfers between devices, flip(): return lax.ppermute(x, axis, [(i, i ^ bit) for i in range(size)])  16.1 us
    ppermute x14, starting transfers between devices, flip(): return lax.ppermute(x, axis, [(i, i ^ bit) for i in range(size)])  12.4 us
    ppermute x6, starting transfers between devices, ring(): return lax.ppermute(x, axis, [(i, (i + by) % size) for i in range(size)])  9.61 us
    ppermute x8, waiting for transfers between devices, turn(): return lax.ppermute(x, ('y_lo', 'z', 'core'), pairs)  7.88 us
    ppermute x6, waiting for transfers between devices, ring(): return lax.ppermute(x, axis, [(i, (i + by) % size) for i in range(size)])  6.92 us
    pallas_call x1, Pallas kernels, rows_pass(): pl.pallas_call(rows_kernel, grid=(STEPS,), in_specs=[pl.BlockSpec((HEADS,...  6.32 us
  transfers between devices with their start and end apart: 31, of which 11 were waited for; matrix products, arithmetic and copies ran while one was open for 2% of the time, Pallas kernels for 9%

commit v1 on v0

--- a/solution.py
+++ b/solution.py
@@ -175,7 +175,7 @@
             jax.ShapeDtypeStruct((BLOCK, D), BF16),
             jax.ShapeDtypeStruct(pack, BF16),
         ],
-        name="head_pass",
+        name="head_pass", compiler_params=pltpu.CompilerParams(vmem_limit_bytes=26 * 1024 * 1024),
     )(meta, *pieces, *others, do, gain, w_qkv, w_qkv, w_qkv)
 
 
@@ -232,7 +232,7 @@
         weight_kernel,
         grid_spec=grid_spec,
         out_shape=[jax.ShapeDtypeStruct(shape, BF16)] * 2,
-        name="weight_pass",
+        name="weight_pass", compiler_params=pltpu.CompilerParams(vmem_limit_bytes=10 * 1024 * 1024),
     )(meta, normed, part, came)
 
 
@@ -255,7 +255,7 @@
         out_specs=pl.BlockSpec(made, lambda i, m: (0, 0, 0)),
     )
     return pl.pallas_call(
-        join_kernel, grid_spec=grid_spec, out_shape=jax.ShapeDtypeStruct(made, BF16), name="join_pass"
+        join_kernel, grid_spec=grid_spec, out_shape=jax.ShapeDtypeStruct(made, BF16), name="join_pass", compiler_params=pltpu.CompilerParams(vmem_limit_bytes=10 * 1024 * 1024)
     )(meta, part, came)
 
 
@@ -297,7 +297,7 @@
             pltpu.VMEM((D, BLOCK), F32),
         ],
         out_shape=jax.ShapeDtypeStruct((BLOCK, D), BF16),
-        name="rows_pass",
+        name="rows_pass", compiler_params=pltpu.CompilerParams(vmem_limit_bytes=12 * 1024 * 1024),
     )(back, mine, gain, w_qkv)
 
 
@@ -320,7 +320,7 @@
         out_specs=pl.BlockSpec((64, 3 * D), lambda i, m: (0, 0)),
     )
     return pl.pallas_call(
-        final_kernel, grid_spec=grid_spec, out_shape=jax.ShapeDtypeStruct((64, 3 * D), F32), name="final_pass"
+        final_kernel, grid_spec=grid_spec, out_shape=jax.ShapeDtypeStruct((64, 3 * D), F32), name="final_pass", compiler_params=pltpu.CompilerParams(vmem_limit_bytes=6 * 1024 * 1024)
     )(meta, own, other)
 
 

time: 143 us -> 136 us (0.951)
  Pallas kernels: 37.9 us -> 25.9 us
  local copies, waits for them, and re-layouts: 4.57 us -> 8.45 us
    unnamed x38 -> x16, local copies, waits for them, and re-layouts: 3.51 us -> 7.97 us
    pallas_call x1, Pallas kernels: 6.32 us -> 2.95 us  [rows_pass(): pl.pallas_call(rows_kernel, grid=(STEPS,), in_specs=[pl.BlockSpec((HEADS,...]
    pallas_call x1, Pallas kernels: 19.9 us -> 16.8 us  [head_pass(): pl.pallas_call(head_kernel, grid_spec=grid_spec, out_shape=[jax.ShapeDtyp...]
    pallas_call x1, Pallas kernels: 5.69 us -> 3 us  [weight_pass(): pl.pallas_call(weight_kernel, grid_spec=grid_spec, out_shape=[jax.ShapeDt...]
    pallas_call x1, Pallas kernels: 3.39 us -> 1.57 us  [join_pass(): pl.pallas_call(join_kernel, grid_spec=grid_spec, out_shape=jax.ShapeDtype...]
  transfers between devices with their start and end apart: 31 -> 31, of which waited for: 11 -> 12; matrix products, arithmetic and copies ran while one was open for 2% -> 2% of each run, Pallas kernels for 9% -> 4%
where the time goes in v1:
time: 136 us
  starting transfers between devices  61.6 us (45%)
  waiting for transfers between devices  36.4 us (27%)
  Pallas kernels  25.9 us (19%)
  local copies, waits for them, and re-layouts  8.45 us (6%)
  other arithmetic  2.55 us (2%)
    ppermute x8, starting transfers between devices, turn(): return lax.ppermute(x, ('y_lo', 'z', 'core'), pairs)  26.5 us
    pallas_call x1, Pallas kernels, head_pass(): pl.pallas_call(head_kernel, grid_spec=grid_spec, out_shape=[jax.ShapeDtyp...  16.8 us
    ppermute x14, waiting for transfers between devices, flip(): return lax.ppermute(x, axis, [(i, i ^ bit) for i in range(size)])  15.7 us
    ppermute x14, starting transfers between devices, flip(): return lax.ppermute(x, axis, [(i, i ^ bit) for i in range(size)])  12.8 us
    ppermute x6, starting transfers between devices, ring(): return lax.ppermute(x, axis, [(i, (i + by) % size) for i in range(size)])  9.63 us
    ppermute x8, waiting for transfers between devices, turn(): return lax.ppermute(x, ('y_lo', 'z', 'core'), pairs)  8.88 us
    unnamed x16, local copies, waits for them, and re-layouts  7.97 us
    ppermute x6, waiting for transfers between devices, ring(): return lax.ppermute(x, axis, [(i, (i + by) % size) for i in range(size)])  7.05 us
  transfers between devices with their start and end apart: 31, of which 12 were waited for; matrix products, arithmetic and copies ran while one was open for 2% of the time, Pallas kernels for 4%

profile of v1, /device:TPU:1, one launch (start us, length us, event | category | flops | bytes accessed | tf_op | source)
XLA Modules:
  0.0 135.8 jit_solution(17124431454977251968)
XLA Ops:
  0.7 0.7 convert_reduce_fusion
  1.7 1.0 fusion.1
  2.7 8.0 %collective-permute-start.2 = (bf16[136,1024]{1,0:T(8,128)(2,1)S(1)}, bf16[136,1024]{1,0:T(8,128)(2,1)S(1)}, u32[]{:S(2)}, u32[]{:S(2)}) collective-permute-start(bf16[136,1024]{1,0:T(8,128)(2,1)S(1)} %fusion.1), channel_id=1, source_target_pairs={{0,112},{1,240},{16,0},{17,128},{32,16},{33,144},{48,32},{49,160},... | collective-permute-start | bytes 835592 | tf_op jit(solution)/shard_map/ppermute | solution.py:341
  10.7 6.0 %collective-permute-done.2.refs_2_ = bf16[136,1024]{1,0:T(8,128)(2,1)S(1)} collective-permute-done((bf16[136,1024]{1,0:T(8,128)(2,1)S(1)}, bf16[136,1024]{1,0:T(8,128)(2,1)S(1)}, u32[]{:S(2)}, u32[]{:S(2)}) %collective-permute-start.2) | collective-permute-done | bytes 278560 | tf_op jit(solution)/shard_map/ppermute | solution.py:341
  16.7 4.0 %collective-permute-start.4 = (bf16[136,1024]{1,0:T(8,128)(2,1)S(1)}, bf16[136,1024]{1,0:T(8,128)(2,1)S(1)}, u32[]{:S(2)}, u32[]{:S(2)}) collective-permute-start(bf16[136,1024]{1,0:T(8,128)(2,1)S(1)} %collective-permute-done.2.refs_2_), channel_id=1, source_target_pairs={{0,112},{16,0},{32,16},{48,32},{64,48},{80,64},{96,80},{112,96},{1... | collective-permute-start | bytes 835592 | tf_op jit(solution)/shard_map/ppermute | solution.py:332
  20.7 3.1 %collective-permute-start.1 = (bf16[136,1024]{1,0:T(8,128)(2,1)S(1)}, bf16[136,1024]{1,0:T(8,128)(2,1)S(1)}, u32[]{:S(2)}, u32[]{:S(2)}) collective-permute-start(bf16[136,1024]{1,0:T(8,128)(2,1)S(1)} %fusion.1), channel_id=1, source_target_pairs={{0,0},{1,128},{16,16},{17,144},{32,32},{33,160},{48,48},{49,176},{... | collective-permute-start | bytes 835592 | tf_op jit(solution)/shard_map/ppermute | solution.py:341
  23.8 1.0 copy.9
  24.9 2.5 %collective-permute-start.19 = (bf16[16,64,128]{2,1,0:T(8,128)(2,1)S(1)}, bf16[16,64,128]{2,1,0:T(8,128)(2,1)S(1)}, u32[]{:S(2)}, u32[]{:S(2)}) collective-permute-start(bf16[16,64,128]{2,1,0:T(8,128)(2,1)S(1)} %bitcast.20), channel_id=1, source_target_pairs={{0,0},{1,128},{16,16},{17,144},{32,32},{33,160},{48,48},{49,176},{... | collective-permute-start | bytes 786440 | tf_op jit(solution)/shard_map/ppermute | solution.py:341
  27.4 2.9 %collective-permute-start.6 = (bf16[136,1024]{1,0:T(8,128)(2,1)S(1)}, bf16[136,1024]{1,0:T(8,128)(2,1)S(1)}, u32[]{:S(2)}, u32[]{:S(2)}) collective-permute-start(bf16[136,1024]{1,0:T(8,128)(2,1)S(1)} %collective-permute-done.4.refs_4_), channel_id=1, source_target_pairs={{0,112},{16,0},{32,16},{48,32},{64,48},{80,64},{96,80},{112,96},{1... | collective-permute-start | bytes 835592 | tf_op jit(solution)/shard_map/ppermute | solution.py:332
  30.3 3.5 %collective-permute-start = (s32[16]{0:T(128)}, s32[16]{0:T(128)S(1)}, u32[]{:S(2)}, u32[]{:S(2)}) collective-permute-start(s32[16]{0:T(128)} %bitcast.22), channel_id=1, source_target_pairs={{0,0},{1,128},{16,16},{17,144},{32,32},{33,160},{48,48},{49,176},{... | collective-permute-start | bytes 200 | tf_op jit(solution)/shard_map/ppermute | solution.py:341
  33.7 1.8 %collective-permute-done = s32[16]{0:T(128)S(1)} collective-permute-done((s32[16]{0:T(128)}, s32[16]{0:T(128)S(1)}, u32[]{:S(2)}, u32[]{:S(2)}) %collective-permute-start) | collective-permute-done | bytes 96 | tf_op jit(solution)/shard_map/ppermute | solution.py:341
  35.6 0.5 collective-permute-start.11
  36.3 0.8 collective-permute-start.14
  37.1 5.1 %all-to-all-start = ((bf16[16,64,128]{2,1,0:T(8,128)(2,1)}), bf16[16,64,128]{2,1,0:T(8,128)(2,1)S(1)}, u32[]{:S(2)}, u32[]{:S(2)}) async-start(bf16[16,64,128]{2,1,0:T(8,128)(2,1)} %copy-done.6), calls=%async_computation | async-start | bytes 524288 | tf_op jit(solution)/shard_map/all_to_all | solution.py:377
  42.3 2.6 %collective-permute-start.9 = (bf16[72,1024]{1,0:T(8,128)(2,1)S(1)}, bf16[72,1024]{1,0:T(8,128)(2,1)S(1)}, u32[]{:S(2)}, u32[]{:S(2)}) collective-permute-start(bf16[72,1024]{1,0:T(8,128)(2,1)S(1)} %slice.9), channel_id=1, source_target_pairs={{0,112},{16,0},{32,16},{48,32},{64,48},{80,64},{96,80},{112,96},{1... | collective-permute-start | bytes 442376 | tf_op jit(solution)/shard_map/ppermute | solution.py:332
  44.9 0.7 collective-permute-start.13
  45.6 0.8 collective-permute-start.16
  46.5 6.8 %collective-permute-done.9.refs_9_ = bf16[72,1024]{1,0:T(8,128)(2,1)S(1)} collective-permute-done((bf16[72,1024]{1,0:T(8,128)(2,1)S(1)}, bf16[72,1024]{1,0:T(8,128)(2,1)S(1)}, u32[]{:S(2)}, u32[]{:S(2)}) %collective-permute-start.9) | collective-permute-done | bytes 147488 | tf_op jit(solution)/shard_map/ppermute | solution.py:332
  53.4 0.9 collective-permute-start.18
  54.2 0.2 collective-permute-done.8.refs_8_
  54.4 0.8 collective-permute-start.17
  55.3 1.2 collective-permute-done.17.refs_17_
  56.5 2.8 %copy-done = bf16[1024,3072]{1,0:T(8,128)(2,1)S(1)} copy-done((bf16[1024,3072]{1,0:T(8,128)(2,1)S(1)}, bf16[1024,3072]{1,0:T(8,128)(2,1)}, u32[]{:S(2)}) %copy-start) | copy-done | bytes 6291480
  59.3 0.7 copy-done.4
  60.0 16.8 %head_pass.1 = (bf16[16,128,1024]{2,1,0:T(8,128)(2,1)S(1)}, bf16[128,1024]{1,0:T(8,128)(2,1)S(1)}, bf16[16,320,128]{2,1,0:T(8,128)(2,1)S(1)}) custom-call(s32[20]{0:T(128)S(1)} %concatenate.6.refs_0_.meta, bf16[136,1024]{1,0:T(8,128)(2,1)S(1)} %collective-permute-done.1.refs_1_, bf16[136,1024]{1,0:T(8,128)(2,1)S(1)} %collective-permute-done.2.refs_2_, ...), custom_call_target="tpu_custom_call" | custom-call | tf_op jit(solution)/shard_map/head_pass/pallas_call | solution.py:170
  76.9 0.4 collective-permute-start.20
  77.3 2.7 %collective-permute-done.20.came = bf16[16,320,128]{2,1,0:T(8,128)(2,1)S(1)} collective-permute-done((bf16[16,320,128]{2,1,0:T(8,128)(2,1)S(1)}, bf16[16,320,128]{2,1,0:T(8,128)(2,1)S(1)}, u32[]{:S(2)}, u32[]{:S(2)}) %collective-permute-start.20) | collective-permute-done | bytes 1310752 | tf_op jit(solution)/shard_map/ppermute | solution.py:328
  80.0 3.0 %weight_pass.1 = (bf16[8,32,384]{2,1,0:T(8,128)(2,1)S(1)}, bf16[8,32,384]{2,1,0:T(8,128)(2,1)S(1)}) custom-call(s32[20]{0:T(128)S(1)} %concatenate.6.refs_0_.meta, bf16[16,128,1024]{2,1,0:T(8,128)(2,1)S(1)} %get-tuple-element.9.normed, bf16[16,320,128]{2,1,0:T(8,128)(2,1)S(1)} %get-tuple-element.7.part, bf16[16,320,128]{2,1,0:T(8,128)(2,1)S(1)} %collective-permute-done.20.came), custom_call_target="tpu_custom_call" | custom-call | tf_op jit(solution)/shard_map/weight_pass/pallas_call | solution.py:231
  83.0 3.0 %collective-permute-start.22 = (bf16[8,32,384]{2,1,0:T(8,128)(2,1)S(1)}, bf16[8,32,384]{2,1,0:T(8,128)(2,1)S(1)}, u32[]{:S(2)}, u32[]{:S(2)}) collective-permute-start(bf16[8,32,384]{2,1,0:T(8,128)(2,1)S(1)} %get-tuple-element.10), channel_id=1, source_target_pairs={{0,0},{1,128},{16,16},{17,144},{32,32},{33,160},{48,48},{49,176},{... | collective-permute-start | bytes 589832 | tf_op jit(solution)/shard_map/ppermute | solution.py:341
  86.1 1.6 %join_pass.1 = bf16[8,384,128]{2,1,0:T(8,128)(2,1)} custom-call(s32[20]{0:T(128)S(1)} %concatenate.6.refs_0_.meta, bf16[16,320,128]{2,1,0:T(8,128)(2,1)S(1)} %get-tuple-element.7.part, bf16[16,320,128]{2,1,0:T(8,128)(2,1)S(1)} %collective-permute-done.20.came), custom_call_target="tpu_custom_call" | custom-call | tf_op jit(solution)/shard_map/join_pass/pallas_call | solution.py:257
  87.7 4.2 %all-to-all-start.1 = ((bf16[8,384,128]{2,1,0:T(8,128)(2,1)}), bf16[8,384,128]{2,1,0:T(8,128)(2,1)S(1)}, u32[]{:S(2)}, u32[]{:S(2)}) async-start(bf16[8,384,128]{2,1,0:T(8,128)(2,1)} %join_pass.1), calls=%async_computation.1 | async-start | bytes 1572864 | tf_op jit(solution)/shard_map/all_to_all | solution.py:382
  92.0 1.3 collective-permute-start.24
  93.3 4.2 %collective-permute-done.24 = bf16[8,32,384]{2,1,0:T(8,128)(2,1)S(1)} collective-permute-done((bf16[8,32,384]{2,1,0:T(8,128)(2,1)S(1)}, bf16[8,32,384]{2,1,0:T(8,128)(2,1)S(1)}, u32[]{:S(2)}, u32[]{:S(2)}) %collective-permute-start.24) | collective-permute-done | bytes 196640 | tf_op jit(solution)/shard_map/ppermute | solution.py:328
  97.6 2.8 %collective-permute-start.25 = (bf16[8,32,384]{2,1,0:T(8,128)(2,1)S(1)}, bf16[8,32,384]{2,1,0:T(8,128)(2,1)S(1)}, u32[]{:S(2)}, u32[]{:S(2)}) collective-permute-start(bf16[8,32,384]{2,1,0:T(8,128)(2,1)S(1)} %add_convert_fusion.2), channel_id=1, source_target_pairs={{0,8},{4,12},{8,0},{12,4},{1,9},{5,13},{9,1},{13,5},{2,10},{6,14},... | collective-permute-start | bytes 589832 | tf_op jit(solution)/shard_map/ppermute | solution.py:328
  100.5 3.4 %collective-permute-done.25 = bf16[8,32,384]{2,1,0:T(8,128)(2,1)S(1)} collective-permute-done((bf16[8,32,384]{2,1,0:T(8,128)(2,1)S(1)}, bf16[8,32,384]{2,1,0:T(8,128)(2,1)S(1)}, u32[]{:S(2)}, u32[]{:S(2)}) %collective-permute-start.25) | collective-permute-done | bytes 196640 | tf_op jit(solution)/shard_map/ppermute | solution.py:328
  103.9 3.1 %collective-permute-start.26 = (bf16[8,32,384]{2,1,0:T(8,128)(2,1)S(1)}, bf16[8,32,384]{2,1,0:T(8,128)(2,1)S(1)}, u32[]{:S(2)}, u32[]{:S(2)}) collective-permute-start(bf16[8,32,384]{2,1,0:T(8,128)(2,1)S(1)} %add_convert_fusion.1), channel_id=1, source_target_pairs={{0,2},{2,0},{1,3},{3,1},{4,6},{6,4},{5,7},{7,5},{8,10},{10,8},{9,1... | collective-permute-start | bytes 589832 | tf_op jit(solution)/shard_map/ppermute | solution.py:328
  107.0 3.1 %collective-permute-done.26 = bf16[8,32,384]{2,1,0:T(8,128)(2,1)S(1)} collective-permute-done((bf16[8,32,384]{2,1,0:T(8,128)(2,1)S(1)}, bf16[8,32,384]{2,1,0:T(8,128)(2,1)S(1)}, u32[]{:S(2)}, u32[]{:S(2)}) %collective-permute-start.26) | collective-permute-done | bytes 196640 | tf_op jit(solution)/shard_map/ppermute | solution.py:328
  110.1 0.7 add_convert_fusion
  110.8 4.7 %all-to-all-done.1.back = bf16[8,384,128]{2,1,0:T(8,128)(2,1)S(1)} async-done(((bf16[8,384,128]{2,1,0:T(8,128)(2,1)}), bf16[8,384,128]{2,1,0:T(8,128)(2,1)S(1)}, u32[]{:S(2)}, u32[]{:S(2)}) %all-to-all-start.1) | async-done | bytes 786464 | tf_op jit(solution)/shard_map/all_to_all | solution.py:382
  115.5 3.4 %all-to-all-start.2 = ((bf16[8,32,384]{2,1,0:T(8,128)(2,1)}), bf16[8,32,384]{2,1,0:T(8,128)(2,1)S(1)}, u32[]{:S(2)}, u32[]{:S(2)}) async-start(bf16[8,32,384]{2,1,0:T(8,128)(2,1)} %add_convert_fusion), calls=%async_computation.2 | async-start | bytes 393216 | tf_op jit(solution)/shard_map/all_to_all | solution.py:390
  118.9 2.8 %copy-done.1 = bf16[1024,3072]{1,0:T(8,128)(2,1)S(1)} copy-done((bf16[1024,3072]{1,0:T(8,128)(2,1)S(1)}, bf16[1024,3072]{1,0:T(8,128)(2,1)}, u32[]{:S(2)}) %copy-start.1) | copy-done | bytes 6291480
  121.7 2.9 %rows_pass.1 = bf16[128,1024]{1,0:T(8,128)(2,1)S(1)} custom-call(bf16[8,384,128]{2,1,0:T(8,128)(2,1)S(1)} %all-to-all-done.1.back, bf16[128,1024]{1,0:T(8,128)(2,1)S(1)} %copy-done.3, f32[1,1024]{1,0:T(1,128)S(1)} %bitcast.16, bf16[1024,3072]{1,0:T(8,128)(2,1)S(1)} %copy-done.1), custom_call_target="tpu_custom_call" | custom-call | tf_op jit(solution)/shard_map/rows_pass/pallas_call | solution.py:285
  124.7 6.3 %collective-permute-start.21 = (bf16[128,1024]{1,0:T(8,128)(2,1)S(1)}, bf16[128,1024]{1,0:T(8,128)(2,1)S(1)}, u32[]{:S(2)}, u32[]{:S(2)}) collective-permute-start(bf16[128,1024]{1,0:T(8,128)(2,1)S(1)} %rows_pass.1), channel_id=1, source_target_pairs={{0,0},{1,128},{16,16},{17,144},{32,32},{33,160},{48,48},{49,176},{... | collective-permute-start | bytes 786440 | tf_op jit(solution)/shard_map/ppermute | solution.py:341
  131.0 0.5 collective-permute-start.27
  131.5 1.1 collective-permute-done.27.other
  132.6 1.5 %final_pass.1 = f32[64,3072]{1,0:T(8,128)} custom-call(s32[20]{0:T(128)S(1)} %concatenate.6.refs_0_.meta, bf16[8,32,384]{2,1,0:T(8,128)(2,1)S(1)} %all-to-all-done.2.own, bf16[8,32,384]{2,1,0:T(8,128)(2,1)S(1)} %collective-permute-done.27.other), custom_call_target="tpu_custom_call" | custom-call | tf_op jit(solution)/shard_map/final_pass/pallas_call | solution.py:322
  134.1 1.0 collective-permute-done.21
  135.1 0.7 copy.11
  (52 shorter events, 1.1 us)
Async XLA Ops:
  2.7 14.1 %collective-permute-start.2 = (bf16[136,1024]{1,0:T(8,128)(2,1)S(1)}, bf16[136,1024]{1,0:T(8,128)(2,1)S(1)}, u32[]{:S(2)}, u32[]{:S(2)}) collective-permute-start(bf16[136,1024]{1,0:T(8,128)(2,1)S(1)} %fusion.1), channel_id=1, source_target_pairs={{0,112},{1,240},{16,0},{17,128},{32,16},{33,144},{48,32},{49,160},... | collective-permute-start | bytes 835592 | tf_op jit(solution)/shard_map/ppermute | solution.py:341
  10.7 10.0 %collective-permute-start.3 = (bf16[136,1024]{1,0:T(8,128)(2,1)S(1)}, bf16[136,1024]{1,0:T(8,128)(2,1)S(1)}, u32[]{:S(2)}, u32[]{:S(2)}) collective-permute-start(bf16[136,1024]{1,0:T(8,128)(2,1)S(1)} %fusion.1), channel_id=1, source_target_pairs={{0,16},{1,144},{16,32},{17,160},{32,48},{33,176},{48,64},{49,192},... | collective-permute-start | bytes 835592 | tf_op jit(solution)/shard_map/ppermute | solution.py:341
  16.7 10.6 %collective-permute-start.4 = (bf16[136,1024]{1,0:T(8,128)(2,1)S(1)}, bf16[136,1024]{1,0:T(8,128)(2,1)S(1)}, u32[]{:S(2)}, u32[]{:S(2)}) collective-permute-start(bf16[136,1024]{1,0:T(8,128)(2,1)S(1)} %collective-permute-done.2.refs_2_), channel_id=1, source_target_pairs={{0,112},{16,0},{32,16},{48,32},{64,48},{80,64},{96,80},{112,96},{1... | collective-permute-start | bytes 835592 | tf_op jit(solution)/shard_map/ppermute | solution.py:332
  20.7 15.4 %collective-permute-start.5 = (bf16[136,1024]{1,0:T(8,128)(2,1)S(1)}, bf16[136,1024]{1,0:T(8,128)(2,1)S(1)}, u32[]{:S(2)}, u32[]{:S(2)}) collective-permute-start(bf16[136,1024]{1,0:T(8,128)(2,1)S(1)} %collective-permute-done.3.refs_3_), channel_id=1, source_target_pairs={{0,16},{16,32},{32,48},{48,64},{64,80},{80,96},{96,112},{112,0},{1... | collective-permute-start | bytes 835592 | tf_op jit(solution)/shard_map/ppermute | solution.py:332
  20.7 15.4 %collective-permute-start.1 = (bf16[136,1024]{1,0:T(8,128)(2,1)S(1)}, bf16[136,1024]{1,0:T(8,128)(2,1)S(1)}, u32[]{:S(2)}, u32[]{:S(2)}) collective-permute-start(bf16[136,1024]{1,0:T(8,128)(2,1)S(1)} %fusion.1), channel_id=1, source_target_pairs={{0,0},{1,128},{16,16},{17,144},{32,32},{33,160},{48,48},{49,176},{... | collective-permute-start | bytes 835592 | tf_op jit(solution)/shard_map/ppermute | solution.py:341
  24.9 10.7 %collective-permute-start.19 = (bf16[16,64,128]{2,1,0:T(8,128)(2,1)S(1)}, bf16[16,64,128]{2,1,0:T(8,128)(2,1)S(1)}, u32[]{:S(2)}, u32[]{:S(2)}) collective-permute-start(bf16[16,64,128]{2,1,0:T(8,128)(2,1)S(1)} %bitcast.20), channel_id=1, source_target_pairs={{0,0},{1,128},{16,16},{17,144},{32,32},{33,160},{48,48},{49,176},{... | collective-permute-start | bytes 786440 | tf_op jit(solution)/shard_map/ppermute | solution.py:341
  27.4 8.9 %collective-permute-start.6 = (bf16[136,1024]{1,0:T(8,128)(2,1)S(1)}, bf16[136,1024]{1,0:T(8,128)(2,1)S(1)}, u32[]{:S(2)}, u32[]{:S(2)}) collective-permute-start(bf16[136,1024]{1,0:T(8,128)(2,1)S(1)} %collective-permute-done.4.refs_4_), channel_id=1, source_target_pairs={{0,112},{16,0},{32,16},{48,32},{64,48},{80,64},{96,80},{112,96},{1... | collective-permute-start | bytes 835592 | tf_op jit(solution)/shard_map/ppermute | solution.py:332
  30.3 5.3 %collective-permute-start = (s32[16]{0:T(128)}, s32[16]{0:T(128)S(1)}, u32[]{:S(2)}, u32[]{:S(2)}) collective-permute-start(s32[16]{0:T(128)} %bitcast.22), channel_id=1, source_target_pairs={{0,0},{1,128},{16,16},{17,144},{32,32},{33,160},{48,48},{49,176},{... | collective-permute-start | bytes 200 | tf_op jit(solution)/shard_map/ppermute | solution.py:341
  35.6 6.7 %collective-permute-start.12 = (bf16[136,1024]{1,0:T(8,128)(2,1)S(1)}, bf16[136,1024]{1,0:T(8,128)(2,1)S(1)}, u32[]{:S(2)}, u32[]{:S(2)}) collective-permute-start(bf16[136,1024]{1,0:T(8,128)(2,1)S(1)} %collective-permute-done.3.refs_3_), channel_id=1, source_target_pairs={{0,1},{1,0},{2,3},{3,2},{4,5},{5,4},{6,7},{7,6},{8,9},{9,8},{10,11... | collective-permute-start | bytes 835592 | tf_op jit(solution)/shard_map/ppermute | solution.py:328
  35.6 0.7 copy-start.6
  35.6 9.3 %collective-permute-start.11 = (bf16[136,1024]{1,0:T(8,128)(2,1)S(1)}, bf16[136,1024]{1,0:T(8,128)(2,1)S(1)}, u32[]{:S(2)}, u32[]{:S(2)}) collective-permute-start(bf16[136,1024]{1,0:T(8,128)(2,1)S(1)} %collective-permute-done.2.refs_2_), channel_id=1, source_target_pairs={{0,1},{1,0},{2,3},{3,2},{4,5},{5,4},{6,7},{7,6},{8,9},{9,8},{10,11... | collective-permute-start | bytes 835592 | tf_op jit(solution)/shard_map/ppermute | solution.py:328
  36.1 9.5 %collective-permute-start.7 = (bf16[136,1024]{1,0:T(8,128)(2,1)S(1)}, bf16[136,1024]{1,0:T(8,128)(2,1)S(1)}, u32[]{:S(2)}, u32[]{:S(2)}) collective-permute-start(bf16[136,1024]{1,0:T(8,128)(2,1)S(1)} %collective-permute-done.5.refs_5_), channel_id=1, source_target_pairs={{0,16},{16,32},{32,48},{48,64},{64,80},{80,96},{96,112},{112,0},{1... | collective-permute-start | bytes 835592 | tf_op jit(solution)/shard_map/ppermute | solution.py:332
  36.1 10.3 %collective-permute-start.10 = (bf16[136,1024]{1,0:T(8,128)(2,1)S(1)}, bf16[136,1024]{1,0:T(8,128)(2,1)S(1)}, u32[]{:S(2)}, u32[]{:S(2)}) collective-permute-start(bf16[136,1024]{1,0:T(8,128)(2,1)S(1)} %collective-permute-done.1.refs_1_), channel_id=1, source_target_pairs={{0,1},{1,0},{2,3},{3,2},{4,5},{5,4},{6,7},{7,6},{8,9},{9,8},{10,11... | collective-permute-start | bytes 835592 | tf_op jit(solution)/shard_map/ppermute | solution.py:328
  36.3 10.1 %collective-permute-start.14 = (bf16[136,1024]{1,0:T(8,128)(2,1)S(1)}, bf16[136,1024]{1,0:T(8,128)(2,1)S(1)}, u32[]{:S(2)}, u32[]{:S(2)}) collective-permute-start(bf16[136,1024]{1,0:T(8,128)(2,1)S(1)} %collective-permute-done.5.refs_5_), channel_id=1, source_target_pairs={{0,1},{1,0},{2,3},{3,2},{4,5},{5,4},{6,7},{7,6},{8,9},{9,8},{10,11... | collective-permute-start | bytes 835592 | tf_op jit(solution)/shard_map/ppermute | solution.py:328
  37.1 18.1 %all-to-all-start = ((bf16[16,64,128]{2,1,0:T(8,128)(2,1)}), bf16[16,64,128]{2,1,0:T(8,128)(2,1)S(1)}, u32[]{:S(2)}, u32[]{:S(2)}) async-start(bf16[16,64,128]{2,1,0:T(8,128)(2,1)} %copy-done.6), calls=%async_computation | async-start | bytes 524288 | tf_op jit(solution)/shard_map/all_to_all | solution.py:377
  42.3 11.1 %collective-permute-start.9 = (bf16[72,1024]{1,0:T(8,128)(2,1)S(1)}, bf16[72,1024]{1,0:T(8,128)(2,1)S(1)}, u32[]{:S(2)}, u32[]{:S(2)}) collective-permute-start(bf16[72,1024]{1,0:T(8,128)(2,1)S(1)} %slice.9), channel_id=1, source_target_pairs={{0,112},{16,0},{32,16},{48,32},{64,48},{80,64},{96,80},{112,96},{1... | collective-permute-start | bytes 442376 | tf_op jit(solution)/shard_map/ppermute | solution.py:332
  44.9 10.4 %collective-permute-start.13 = (bf16[136,1024]{1,0:T(8,128)(2,1)S(1)}, bf16[136,1024]{1,0:T(8,128)(2,1)}, u32[]{:S(2)}, u32[]{:S(2)}) collective-permute-start(bf16[136,1024]{1,0:T(8,128)(2,1)S(1)} %collective-permute-done.4.refs_4_), channel_id=1, source_target_pairs={{0,1},{1,0},{2,3},{3,2},{4,5},{5,4},{6,7},{7,6},{8,9},{9,8},{10,11... | collective-permute-start | bytes 835592 | tf_op jit(solution)/shard_map/ppermute | solution.py:328
  45.6 10.9 %collective-permute-start.16 = (bf16[136,1024]{1,0:T(8,128)(2,1)S(1)}, bf16[136,1024]{1,0:T(8,128)(2,1)}, u32[]{:S(2)}, u32[]{:S(2)}) collective-permute-start(bf16[136,1024]{1,0:T(8,128)(2,1)S(1)} %collective-permute-done.7.refs_7_), channel_id=1, source_target_pairs={{0,1},{1,0},{2,3},{3,2},{4,5},{5,4},{6,7},{7,6},{8,9},{9,8},{10,11... | collective-permute-start | bytes 835592 | tf_op jit(solution)/shard_map/ppermute | solution.py:328
  46.4 10.1 %collective-permute-start.15 = (bf16[136,1024]{1,0:T(8,128)(2,1)S(1)}, bf16[136,1024]{1,0:T(8,128)(2,1)}, u32[]{:S(2)}, u32[]{:S(2)}) collective-permute-start(bf16[136,1024]{1,0:T(8,128)(2,1)S(1)} %collective-permute-done.6.refs_6_), channel_id=1, source_target_pairs={{0,1},{1,0},{2,3},{3,2},{4,5},{5,4},{6,7},{7,6},{8,9},{9,8},{10,11... | collective-permute-start | bytes 835592 | tf_op jit(solution)/shard_map/ppermute | solution.py:328
  46.4 8.0 %collective-permute-start.8 = (bf16[64,1024]{1,0:T(8,128)(2,1)S(1)}, bf16[64,1024]{1,0:T(8,128)(2,1)}, u32[]{:S(2)}, u32[]{:S(2)}) collective-permute-start(bf16[64,1024]{1,0:T(8,128)(2,1)S(1)} %slice.8), channel_id=1, source_target_pairs={{0,16},{16,32},{32,48},{48,64},{64,80},{80,96},{96,112},{112,0},{1... | collective-permute-start | bytes 393224 | tf_op jit(solution)/shard_map/ppermute | solution.py:332
  53.4 3.2 %collective-permute-start.18 = (bf16[72,1024]{1,0:T(8,128)(2,1)S(1)}, bf16[72,1024]{1,0:T(8,128)(2,1)}, u32[]{:S(2)}, u32[]{:S(2)}) collective-permute-start(bf16[72,1024]{1,0:T(8,128)(2,1)S(1)} %collective-permute-done.9.refs_9_), channel_id=1, source_target_pairs={{0,1},{1,0},{2,3},{3,2},{4,5},{5,4},{6,7},{7,6},{8,9},{9,8},{10,11... | collective-permute-start | bytes 442376 | tf_op jit(solution)/shard_map/ppermute | solution.py:328
  54.4 2.1 %collective-permute-start.17 = (bf16[64,1024]{1,0:T(8,128)(2,1)}, bf16[64,1024]{1,0:T(8,128)(2,1)}, u32[]{:S(2)}, u32[]{:S(2)}) collective-permute-start(bf16[64,1024]{1,0:T(8,128)(2,1)} %collective-permute-done.8.refs_8_), channel_id=1, source_target_pairs={{0,1},{1,0},{2,3},{3,2},{4,5},{5,4},{6,7},{7,6},{8,9},{9,8},{10,11... | collective-permute-start | bytes 393224 | tf_op jit(solution)/shard_map/ppermute | solution.py:328
  56.5 2.8 %copy-start = (bf16[1024,3072]{1,0:T(8,128)(2,1)S(1)}, bf16[1024,3072]{1,0:T(8,128)(2,1)}, u32[]{:S(2)}) copy-start(bf16[1024,3072]{1,0:T(8,128)(2,1)} %w.1) | copy-start | bytes 18874372
  59.3 0.7 copy-start.4
  76.9 6.1 %copy-start.2 = (bf16[128,1024]{1,0:T(8,128)(2,1)}, bf16[128,1024]{1,0:T(8,128)(2,1)S(1)}, u32[]{:S(2)}) copy-start(bf16[128,1024]{1,0:T(8,128)(2,1)S(1)} %get-tuple-element.8.mine) | copy-start | bytes 786436
  76.9 3.1 %collective-permute-start.20 = (bf16[16,320,128]{2,1,0:T(8,128)(2,1)S(1)}, bf16[16,320,128]{2,1,0:T(8,128)(2,1)S(1)}, u32[]{:S(2)}, u32[]{:S(2)}) collective-permute-start(bf16[16,320,128]{2,1,0:T(8,128)(2,1)S(1)} %get-tuple-element.7.part), channel_id=1, source_target_pairs={{0,1},{1,0},{2,3},{3,2},{4,5},{5,4},{6,7},{7,6},{8,9},{9,8},{10,11... | collective-permute-start | bytes 3932168 | tf_op jit(solution)/shard_map/ppermute | solution.py:328
  83.0 35.9 %copy-start.5 = (f32[1024]{0:T(1024)S(1)}, f32[1024]{0:T(1024)}, u32[]{:S(2)}) copy-start(f32[1024]{0:T(1024)} %param.9) | copy-start | bytes 12292
  83.0 35.9 %copy-start.3 = (bf16[128,1024]{1,0:T(8,128)(2,1)S(1)}, bf16[128,1024]{1,0:T(8,128)(2,1)}, u32[]{:S(2)}) copy-start(bf16[128,1024]{1,0:T(8,128)(2,1)} %copy-done.2) | copy-start | bytes 786436
  83.0 8.9 %collective-permute-start.22 = (bf16[8,32,384]{2,1,0:T(8,128)(2,1)S(1)}, bf16[8,32,384]{2,1,0:T(8,128)(2,1)S(1)}, u32[]{:S(2)}, u32[]{:S(2)}) collective-permute-start(bf16[8,32,384]{2,1,0:T(8,128)(2,1)S(1)} %get-tuple-element.10), channel_id=1, source_target_pairs={{0,0},{1,128},{16,16},{17,144},{32,32},{33,160},{48,48},{49,176},{... | collective-permute-start | bytes 589832 | tf_op jit(solution)/shard_map/ppermute | solution.py:341
  86.0 5.9 %collective-permute-start.23 = (bf16[8,32,384]{2,1,0:T(8,128)(2,1)S(1)}, bf16[8,32,384]{2,1,0:T(8,128)(2,1)S(1)}, u32[]{:S(2)}, u32[]{:S(2)}) collective-permute-start(bf16[8,32,384]{2,1,0:T(8,128)(2,1)S(1)} %get-tuple-element.11), channel_id=1, source_target_pairs={{0,1},{1,129},{16,17},{17,145},{32,33},{33,161},{48,49},{49,177},{... | collective-permute-start | bytes 589832 | tf_op jit(solution)/shard_map/ppermute | solution.py:341
  87.7 27.8 %all-to-all-start.1 = ((bf16[8,384,128]{2,1,0:T(8,128)(2,1)}), bf16[8,384,128]{2,1,0:T(8,128)(2,1)S(1)}, u32[]{:S(2)}, u32[]{:S(2)}) async-start(bf16[8,384,128]{2,1,0:T(8,128)(2,1)} %join_pass.1), calls=%async_computation.1 | async-start | bytes 1572864 | tf_op jit(solution)/shard_map/all_to_all | solution.py:382
  92.0 5.6 %collective-permute-start.24 = (bf16[8,32,384]{2,1,0:T(8,128)(2,1)S(1)}, bf16[8,32,384]{2,1,0:T(8,128)(2,1)S(1)}, u32[]{:S(2)}, u32[]{:S(2)}) collective-permute-start(bf16[8,32,384]{2,1,0:T(8,128)(2,1)S(1)} %add_convert_fusion.3), channel_id=1, source_target_pairs={{0,4},{4,0},{8,12},{12,8},{1,5},{5,1},{9,13},{13,9},{2,6},{6,2},{1... | collective-permute-start | bytes 589832 | tf_op jit(solution)/shard_map/ppermute | solution.py:328
  97.6 6.3 %collective-permute-start.25 = (bf16[8,32,384]{2,1,0:T(8,128)(2,1)S(1)}, bf16[8,32,384]{2,1,0:T(8,128)(2,1)S(1)}, u32[]{:S(2)}, u32[]{:S(2)}) collective-permute-start(bf16[8,32,384]{2,1,0:T(8,128)(2,1)S(1)} %add_convert_fusion.2), channel_id=1, source_target_pairs={{0,8},{4,12},{8,0},{12,4},{1,9},{5,13},{9,1},{13,5},{2,10},{6,14},... | collective-permute-start | bytes 589832 | tf_op jit(solution)/shard_map/ppermute | solution.py:328
  103.9 6.1 %collective-permute-start.26 = (bf16[8,32,384]{2,1,0:T(8,128)(2,1)S(1)}, bf16[8,32,384]{2,1,0:T(8,128)(2,1)S(1)}, u32[]{:S(2)}, u32[]{:S(2)}) collective-permute-start(bf16[8,32,384]{2,1,0:T(8,128)(2,1)S(1)} %add_convert_fusion.1), channel_id=1, source_target_pairs={{0,2},{2,0},{1,3},{3,1},{4,6},{6,4},{5,7},{7,5},{8,10},{10,8},{9,1... | collective-permute-start | bytes 589832 | tf_op jit(solution)/shard_map/ppermute | solution.py:328
  115.5 15.5 %all-to-all-start.2 = ((bf16[8,32,384]{2,1,0:T(8,128)(2,1)}), bf16[8,32,384]{2,1,0:T(8,128)(2,1)S(1)}, u32[]{:S(2)}, u32[]{:S(2)}) async-start(bf16[8,32,384]{2,1,0:T(8,128)(2,1)} %add_convert_fusion), calls=%async_computation.2 | async-start | bytes 393216 | tf_op jit(solution)/shard_map/all_to_all | solution.py:390
  118.9 2.8 %copy-start.1 = (bf16[1024,3072]{1,0:T(8,128)(2,1)S(1)}, bf16[1024,3072]{1,0:T(8,128)(2,1)}, u32[]{:S(2)}) copy-start(bf16[1024,3072]{1,0:T(8,128)(2,1)} %w.1) | copy-start | bytes 18874372
  124.7 10.4 %collective-permute-start.21 = (bf16[128,1024]{1,0:T(8,128)(2,1)S(1)}, bf16[128,1024]{1,0:T(8,128)(2,1)S(1)}, u32[]{:S(2)}, u32[]{:S(2)}) collective-permute-start(bf16[128,1024]{1,0:T(8,128)(2,1)S(1)} %rows_pass.1), channel_id=1, source_target_pairs={{0,0},{1,128},{16,16},{17,144},{32,32},{33,160},{48,48},{49,176},{... | collective-permute-start | bytes 786440 | tf_op jit(solution)/shard_map/ppermute | solution.py:341
  131.0 1.5 %collective-permute-start.27 = (bf16[8,32,384]{2,1,0:T(8,128)(2,1)S(1)}, bf16[8,32,384]{2,1,0:T(8,128)(2,1)S(1)}, u32[]{:S(2)}, u32[]{:S(2)}) collective-permute-start(bf16[8,32,384]{2,1,0:T(8,128)(2,1)S(1)} %all-to-all-done.2.own), channel_id=1, source_target_pairs={{0,1},{1,0},{2,3},{3,2},{4,5},{5,4},{6,7},{7,6},{8,9},{9,8},{10,11... | collective-permute-start | bytes 589832 | tf_op jit(solution)/shard_map/ppermute | solution.py:328

commit v2 on v1

--- a/solution.py
+++ b/solution.py
@@ -76,7 +76,7 @@
 
     rows = rows_s[pl.ds(step * 4, 4), 0:BLOCK, :].astype(F32)
     inverse = lax.rsqrt(jnp.mean(rows * rows, axis=-1, keepdims=True) + EPS)
-    nrm = (rows * inverse * gain[...][None]).astype(BF16)
+    nrm = (rows * inverse * gain[0:1, :][None]).astype(BF16)
     normed[...] = nrm
     nrm = nrm.reshape(KROWS, D)
     k_s[step] = dot(nrm, wk[...], 1, 0).astype(BF16)
@@ -99,6 +99,7 @@
         below = jnp.sum(jnp.where((known < number) & real, 1.0, 0.0))
         first = first + jnp.where(mine_docs == number, below, 0.0)
     q_first = first.astype(jnp.int32)
+    low_tile = jnp.min(q_first) // KROWS
 
     def scores(g, total):
         s = dot(k_s[g], q_s[...], 1, 1) * FACTOR
@@ -107,7 +108,7 @@
         e_s[g] = e
         return total + jnp.sum(e, axis=0, keepdims=True)
 
-    total = lax.fori_loop(0, step + 1, scores, jnp.zeros((1, QROWS), F32))
+    total = lax.fori_loop(low_tile, step + 1, scores, jnp.zeros((1, QROWS), F32))
     scale = 1.0 / total
 
     def deltas(g, delta):
@@ -117,14 +118,14 @@
         dv_s[g] += dot(low, do_s[...], 1, 0)
         return delta + jnp.sum(low.astype(F32) * grad, axis=0, keepdims=True)
 
-    delta = lax.fori_loop(0, step + 1, deltas, jnp.zeros((1, QROWS), F32))
+    delta = lax.fori_loop(low_tile, step + 1, deltas, jnp.zeros((1, QROWS), F32))
 
     def grads(g, dq):
         ds = (e_s[g] * scale * (p_s[g] - delta)).astype(BF16)
         dk_s[g] += dot(ds, q_s[...], 1, 0)
         return dq + dot(ds, k_s[g], 0, 0)
 
-    dq = lax.fori_loop(0, step + 1, grads, jnp.zeros((QROWS, HEAD), F32))
+    dq = lax.fori_loop(low_tile, step + 1, grads, jnp.zeros((QROWS, HEAD), F32))
     dq = (dq * FACTOR).astype(BF16)
     part[pl.ds(step * 4, 4), 0:HALF, :] = dq.reshape(4, HALF, HEAD)
 
@@ -134,7 +135,7 @@
         part[:, HALF + BLOCK :, :] = dv_s[...].astype(BF16).reshape(NBLK, BLOCK, HEAD)
 
 
-def head_pass(meta, pieces, others, do, gain, w_qkv):
+def head_pass(meta, pieces, others, do, gain, w_head):
     pack = (NBLK, HALF + 2 * BLOCK, HEAD)
     grid_spec = pltpu.PrefetchScalarGridSpec(
         num_scalar_prefetch=1,
@@ -142,11 +143,9 @@
         in_specs=[pl.BlockSpec(memory_space=pl.ANY)] * (2 * PIECES)
         + [
             pl.BlockSpec((NBLK, HALF, HEAD), lambda i, m: (0, 0, 0)),
-            pl.BlockSpec((1, D), lambda i, m: (0, 0)),
-            pl.BlockSpec((D, HEAD), lambda i, m: (0, m[NBLK])),
-            pl.BlockSpec((D, HEAD), lambda i, m: (0, HEADS + m[NBLK])),
-            pl.BlockSpec((D, HEAD), lambda i, m: (0, 2 * HEADS + m[NBLK])),
-        ],
+            pl.BlockSpec((8, D), lambda i, m: (0, 0)),
+        ]
+        + [pl.BlockSpec((D, HEAD), lambda i, m: (0, 0))] * 3,
         out_specs=[
             pl.BlockSpec((4, BLOCK, D), lambda i, m: (i, 0, 0)),
             pl.BlockSpec((BLOCK, D), lambda i, m: (0, 0)),
@@ -176,7 +175,7 @@
             jax.ShapeDtypeStruct(pack, BF16),
         ],
         name="head_pass", compiler_params=pltpu.CompilerParams(vmem_limit_bytes=26 * 1024 * 1024),
-    )(meta, *pieces, *others, do, gain, w_qkv, w_qkv, w_qkv)
+    )(meta, *pieces, *others, do, gain, *w_head)
 
 
 def total_of(part, came, half, blocks):
@@ -276,7 +275,7 @@
         values = mine[...].astype(F32)
         inverse = lax.rsqrt(jnp.mean(values * values, axis=-1, keepdims=True) + EPS)
         unit = values * inverse
-        gained = d_norm[...].T * gain[...]
+        gained = d_norm[...].T * gain[0:1, :]
         shared = jnp.mean(gained * unit, axis=-1, keepdims=True)
         out[...] = (inverse * (gained - unit * shared)).astype(BF16)
 
@@ -288,7 +287,7 @@
         in_specs=[
             pl.BlockSpec((HEADS, 3 * BLOCK, HEAD), lambda i: (0, 0, 0)),
             pl.BlockSpec((BLOCK, D), lambda i: (0, 0)),
-            pl.BlockSpec((1, D), lambda i: (0, 0)),
+            pl.BlockSpec((8, D), lambda i: (0, 0)),
             pl.BlockSpec((D // STEPS, 3 * D), lambda i: (i, 0)),
         ],
         out_specs=pl.BlockSpec((BLOCK, D), lambda i: (0, 0)),
@@ -352,7 +351,8 @@
     for _ in range(2):
         down, up = ring(down, "z", -1, 8), ring(up, "z", 1, 8)
         made += [down, up]
-    made.append(ring(up[:HALF], "z", 1, 8))
+    far = ring(up[:HALF], "z", 1, 8)
+    made.append(far)
     made.append(ring(down[HALF:], "z", -1, 8))
     return made
 
@@ -370,12 +370,13 @@
     parts = d_attn[0].reshape(2, HALF, HEADS, HEAD).transpose(2, 0, 1, 3)
     parts = turn(parts.reshape(NBLK, HALF, HEAD))
     meta = jnp.concatenate([order, jnp.stack([z, core, y, x]).astype(jnp.int32)])
-    gain = norm_gain[None, :]
+    gain = jnp.broadcast_to(norm_gain[None, :], (8, D))
+    w_head = [lax.dynamic_slice_in_dim(w_qkv, n * D + z * HEAD, HEAD, 1) for n in range(3)]
 
     pieces = relay(payload)
     others = [flip(piece, "core", 1, 2) for piece in pieces]
     do = lax.all_to_all(parts, ("z", "core"), 0, 0, tiled=True)
-    normed, mine, part = head_pass(meta, pieces, others, do, gain, w_qkv)
+    normed, mine, part = head_pass(meta, pieces, others, do, gain, w_head)
     came = flip(part, "core", 1, 2)
     here, there = weight_pass(meta, normed, part, came)
     back = join_pass(meta, part, came)

time: 136 us -> 136 us (level)
  Pallas kernels: 25.9 us -> 21 us
  starting transfers between devices: 61.6 us -> 64.5 us
  waiting for transfers between devices: 36.4 us -> 37.8 us
    pallas_call x1, Pallas kernels: 16.8 us -> 12 us  [head_pass(): pl.pallas_call(head_kernel, grid_spec=grid_spec, out_shape=[jax.ShapeDtyp...]
    ppermute x14, starting transfers between devices: 12.8 us -> 17.4 us  [flip(): return lax.ppermute(x, axis, [(i, i ^ bit) for i in range(size)])]
    ppermute x6, waiting for transfers between devices: 7.05 us -> 9.19 us  [ring(): return lax.ppermute(x, axis, [(i, (i + by) % size) for i in range(size)])]
    unnamed x16 -> x18, local copies, waits for them, and re-layouts: 7.97 us -> 7.11 us
  transfers between devices with their start and end apart: 31 -> 31, of which waited for: 12 -> 14; matrix products, arithmetic and copies ran while one was open for 2% -> 2% of each run, Pallas kernels for 4% -> 4%
where the time goes in v2:
time: 136 us
  starting transfers between devices  64.5 us (47%)
  waiting for transfers between devices  37.8 us (28%)
  Pallas kernels  21 us (15%)
  local copies, waits for them, and re-layouts  8.77 us (6%)
  other arithmetic  2.55 us (2%)
    ppermute x8, starting transfers between devices, turn(): return lax.ppermute(x, ('y_lo', 'z', 'core'), pairs)  25.2 us
    ppermute x14, starting transfers between devices, flip(): return lax.ppermute(x, axis, [(i, i ^ bit) for i in range(size)])  17.4 us
    ppermute x14, waiting for transfers between devices, flip(): return lax.ppermute(x, axis, [(i, i ^ bit) for i in range(size)])  14.9 us
    pallas_call x1, Pallas kernels, head_pass(): pl.pallas_call(head_kernel, grid_spec=grid_spec, out_shape=[jax.ShapeDtyp...  12 us
    ppermute x6, starting transfers between devices, ring(): return lax.ppermute(x, axis, [(i, (i + by) % size) for i in range(size)])  9.93 us
    ppermute x8, waiting for transfers between devices, turn(): return lax.ppermute(x, ('y_lo', 'z', 'core'), pairs)  9.26 us
    ppermute x6, waiting for transfers between devices, ring(): return lax.ppermute(x, axis, [(i, (i + by) % size) for i in range(size)])  9.19 us
    unnamed x18, local copies, waits for them, and re-layouts  7.11 us
  transfers between devices with their start and end apart: 31, of which 14 were waited for; matrix products, arithmetic and copies ran while one was open for 2% of the time, Pallas kernels for 4%

profile of v2, /device:TPU:1, one launch (start us, length us, event | category | flops | bytes accessed | tf_op | source)
XLA Modules:
  0.0 135.5 jit_solution(5053092003726254894)
XLA Ops:
  0.7 0.7 convert_reduce_fusion
  1.7 1.0 fusion.1
  2.7 8.0 %collective-permute-start.2 = (bf16[136,1024]{1,0:T(8,128)(2,1)S(1)}, bf16[136,1024]{1,0:T(8,128)(2,1)S(1)}, u32[]{:S(2)}, u32[]{:S(2)}) collective-permute-start(bf16[136,1024]{1,0:T(8,128)(2,1)S(1)} %fusion.1), channel_id=1, source_target_pairs={{0,112},{1,240},{16,0},{17,128},{32,16},{33,144},{48,32},{49,160},... | collective-permute-start | bytes 835592 | tf_op jit(solution)/shard_map/ppermute | solution.py:340
  10.7 6.0 %collective-permute-done.2.refs_2_ = bf16[136,1024]{1,0:T(8,128)(2,1)S(1)} collective-permute-done((bf16[136,1024]{1,0:T(8,128)(2,1)S(1)}, bf16[136,1024]{1,0:T(8,128)(2,1)S(1)}, u32[]{:S(2)}, u32[]{:S(2)}) %collective-permute-start.2) | collective-permute-done | bytes 278560 | tf_op jit(solution)/shard_map/ppermute | solution.py:340
  16.7 4.0 %collective-permute-start.4 = (bf16[136,1024]{1,0:T(8,128)(2,1)S(1)}, bf16[136,1024]{1,0:T(8,128)(2,1)S(1)}, u32[]{:S(2)}, u32[]{:S(2)}) collective-permute-start(bf16[136,1024]{1,0:T(8,128)(2,1)S(1)} %collective-permute-done.2.refs_2_), channel_id=1, source_target_pairs={{0,112},{16,0},{32,16},{48,32},{64,48},{80,64},{96,80},{112,96},{1... | collective-permute-start | bytes 835592 | tf_op jit(solution)/shard_map/ppermute | solution.py:331
  20.8 3.1 %collective-permute-start.1 = (bf16[136,1024]{1,0:T(8,128)(2,1)S(1)}, bf16[136,1024]{1,0:T(8,128)(2,1)S(1)}, u32[]{:S(2)}, u32[]{:S(2)}) collective-permute-start(bf16[136,1024]{1,0:T(8,128)(2,1)S(1)} %fusion.1), channel_id=1, source_target_pairs={{0,0},{1,128},{16,16},{17,144},{32,32},{33,160},{48,48},{49,176},{... | collective-permute-start | bytes 835592 | tf_op jit(solution)/shard_map/ppermute | solution.py:340
  23.8 3.3 %collective-permute-done.4.refs_4_ = bf16[136,1024]{1,0:T(8,128)(2,1)S(1)} collective-permute-done((bf16[136,1024]{1,0:T(8,128)(2,1)S(1)}, bf16[136,1024]{1,0:T(8,128)(2,1)S(1)}, u32[]{:S(2)}, u32[]{:S(2)}) %collective-permute-start.4) | collective-permute-done | bytes 278560 | tf_op jit(solution)/shard_map/ppermute | solution.py:331
  27.1 3.2 %collective-permute-start.6 = (bf16[136,1024]{1,0:T(8,128)(2,1)S(1)}, bf16[136,1024]{1,0:T(8,128)(2,1)S(1)}, u32[]{:S(2)}, u32[]{:S(2)}) collective-permute-start(bf16[136,1024]{1,0:T(8,128)(2,1)S(1)} %collective-permute-done.4.refs_4_), channel_id=1, source_target_pairs={{0,112},{16,0},{32,16},{48,32},{64,48},{80,64},{96,80},{112,96},{1... | collective-permute-start | bytes 835592 | tf_op jit(solution)/shard_map/ppermute | solution.py:331
  30.3 1.0 copy.9
  31.3 1.9 %collective-permute-start.19 = (bf16[16,64,128]{2,1,0:T(8,128)(2,1)S(1)}, bf16[16,64,128]{2,1,0:T(8,128)(2,1)}, u32[]{:S(2)}, u32[]{:S(2)}) collective-permute-start(bf16[16,64,128]{2,1,0:T(8,128)(2,1)S(1)} %bitcast.18), channel_id=1, source_target_pairs={{0,0},{1,128},{16,16},{17,144},{32,32},{33,160},{48,48},{49,176},{... | collective-permute-start | bytes 786440 | tf_op jit(solution)/shard_map/ppermute | solution.py:340
  33.3 3.6 %collective-permute-start = (s32[16]{0:T(128)}, s32[16]{0:T(128)S(1)}, u32[]{:S(2)}, u32[]{:S(2)}) collective-permute-start(s32[16]{0:T(128)} %bitcast.19), channel_id=1, source_target_pairs={{0,0},{1,128},{16,16},{17,144},{32,32},{33,160},{48,48},{49,176},{... | collective-permute-start | bytes 200 | tf_op jit(solution)/shard_map/ppermute | solution.py:340
  36.9 2.2 %collective-permute-done = s32[16]{0:T(128)S(1)} collective-permute-done((s32[16]{0:T(128)}, s32[16]{0:T(128)S(1)}, u32[]{:S(2)}, u32[]{:S(2)}) %collective-permute-start) | collective-permute-done | bytes 96 | tf_op jit(solution)/shard_map/ppermute | solution.py:340
  40.3 4.5 %all-to-all-start = ((bf16[16,64,128]{2,1,0:T(8,128)(2,1)}), bf16[16,64,128]{2,1,0:T(8,128)(2,1)S(1)}, u32[]{:S(2)}, u32[]{:S(2)}) async-start(bf16[16,64,128]{2,1,0:T(8,128)(2,1)} %collective-permute-done.19), calls=%async_computation | async-start | bytes 524288 | tf_op jit(solution)/shard_map/all_to_all | solution.py:378
  44.8 2.6 %collective-permute-start.9 = (bf16[72,1024]{1,0:T(8,128)(2,1)S(1)}, bf16[72,1024]{1,0:T(8,128)(2,1)S(1)}, u32[]{:S(2)}, u32[]{:S(2)}) collective-permute-start(bf16[72,1024]{1,0:T(8,128)(2,1)S(1)} %slice.9), channel_id=1, source_target_pairs={{0,112},{16,0},{32,16},{48,32},{64,48},{80,64},{96,80},{112,96},{1... | collective-permute-start | bytes 442376 | tf_op jit(solution)/shard_map/ppermute | solution.py:331
  47.5 0.7 collective-permute-start.13
  48.1 0.9 collective-permute-done.7.refs_7_
  49.0 2.6 %collective-permute-start.16 = (bf16[136,1024]{1,0:T(8,128)(2,1)S(1)}, bf16[136,1024]{1,0:T(8,128)(2,1)}, u32[]{:S(2)}, u32[]{:S(2)}) collective-permute-start(bf16[136,1024]{1,0:T(8,128)(2,1)S(1)} %collective-permute-done.7.refs_7_), channel_id=1, source_target_pairs={{0,1},{1,0},{2,3},{3,2},{4,5},{5,4},{6,7},{7,6},{8,9},{9,8},{10,11... | collective-permute-start | bytes 835592 | tf_op jit(solution)/shard_map/ppermute | solution.py:327
  51.6 0.7 copy-done.3
  52.4 3.4 %collective-permute-done.9.refs_9_ = bf16[72,1024]{1,0:T(8,128)(2,1)S(1)} collective-permute-done((bf16[72,1024]{1,0:T(8,128)(2,1)S(1)}, bf16[72,1024]{1,0:T(8,128)(2,1)S(1)}, u32[]{:S(2)}, u32[]{:S(2)}) %collective-permute-start.9) | collective-permute-done | bytes 147488 | tf_op jit(solution)/shard_map/ppermute | solution.py:331
  55.8 1.0 collective-permute-start.18
  56.8 1.6 %collective-permute-done.8.refs_8_ = bf16[64,1024]{1,0:T(8,128)(2,1)} collective-permute-done((bf16[64,1024]{1,0:T(8,128)(2,1)S(1)}, bf16[64,1024]{1,0:T(8,128)(2,1)}, u32[]{:S(2)}, u32[]{:S(2)}) %collective-permute-start.8) | collective-permute-done | bytes 131104 | tf_op jit(solution)/shard_map/ppermute | solution.py:331
  58.4 1.3 collective-permute-start.17
  59.7 1.2 constant_dynamic-slice_fusion
  61.1 0.9 copy-done.2
  62.0 1.0 copy-done.4
  63.0 12.0 %head_pass.1 = (bf16[16,128,1024]{2,1,0:T(8,128)(2,1)S(1)}, bf16[128,1024]{1,0:T(8,128)(2,1)S(1)}, bf16[16,320,128]{2,1,0:T(8,128)(2,1)S(1)}) custom-call(s32[20]{0:T(128)S(1)} %concatenate.6.refs_0_.meta, bf16[136,1024]{1,0:T(8,128)(2,1)S(1)} %collective-permute-done.1.refs_1_, bf16[136,1024]{1,0:T(8,128)(2,1)S(1)} %collective-permute-done.2.refs_2_, ...), custom_call_target="tpu_custom_call" | custom-call | tf_op jit(solution)/shard_map/head_pass/pallas_call | solution.py:169
  75.0 3.3 %collective-permute-start.20 = (bf16[16,320,128]{2,1,0:T(8,128)(2,1)S(1)}, bf16[16,320,128]{2,1,0:T(8,128)(2,1)S(1)}, u32[]{:S(2)}, u32[]{:S(2)}) collective-permute-start(bf16[16,320,128]{2,1,0:T(8,128)(2,1)S(1)} %get-tuple-element.7.part), channel_id=1, source_target_pairs={{0,1},{1,0},{2,3},{3,2},{4,5},{5,4},{6,7},{7,6},{8,9},{9,8},{10,11... | collective-permute-start | bytes 3932168 | tf_op jit(solution)/shard_map/ppermute | solution.py:327
  78.2 2.7 %collective-permute-done.20.came = bf16[16,320,128]{2,1,0:T(8,128)(2,1)S(1)} collective-permute-done((bf16[16,320,128]{2,1,0:T(8,128)(2,1)S(1)}, bf16[16,320,128]{2,1,0:T(8,128)(2,1)S(1)}, u32[]{:S(2)}, u32[]{:S(2)}) %collective-permute-start.20) | collective-permute-done | bytes 1310752 | tf_op jit(solution)/shard_map/ppermute | solution.py:327
  80.9 3.0 %weight_pass.1 = (bf16[8,32,384]{2,1,0:T(8,128)(2,1)S(1)}, bf16[8,32,384]{2,1,0:T(8,128)(2,1)S(1)}) custom-call(s32[20]{0:T(128)S(1)} %concatenate.6.refs_0_.meta, bf16[16,128,1024]{2,1,0:T(8,128)(2,1)S(1)} %get-tuple-element.9.normed, bf16[16,320,128]{2,1,0:T(8,128)(2,1)S(1)} %get-tuple-element.7.part, bf16[16,320,128]{2,1,0:T(8,128)(2,1)S(1)} %collective-permute-done.20.came), custom_call_target="tpu_custom_call" | custom-call | tf_op jit(solution)/shard_map/weight_pass/pallas_call | solution.py:230
  83.9 2.1 %collective-permute-start.22 = (bf16[8,32,384]{2,1,0:T(8,128)(2,1)S(1)}, bf16[8,32,384]{2,1,0:T(8,128)(2,1)S(1)}, u32[]{:S(2)}, u32[]{:S(2)}) collective-permute-start(bf16[8,32,384]{2,1,0:T(8,128)(2,1)S(1)} %get-tuple-element.10), channel_id=1, source_target_pairs={{0,0},{1,128},{16,16},{17,144},{32,32},{33,160},{48,48},{49,176},{... | collective-permute-start | bytes 589832 | tf_op jit(solution)/shard_map/ppermute | solution.py:340
  86.1 1.6 %join_pass.1 = bf16[8,384,128]{2,1,0:T(8,128)(2,1)} custom-call(s32[20]{0:T(128)S(1)} %concatenate.6.refs_0_.meta, bf16[16,320,128]{2,1,0:T(8,128)(2,1)S(1)} %get-tuple-element.7.part, bf16[16,320,128]{2,1,0:T(8,128)(2,1)S(1)} %collective-permute-done.20.came), custom_call_target="tpu_custom_call" | custom-call | tf_op jit(solution)/shard_map/join_pass/pallas_call | solution.py:256
  87.7 4.0 %all-to-all-start.1 = ((bf16[8,384,128]{2,1,0:T(8,128)(2,1)}), bf16[8,384,128]{2,1,0:T(8,128)(2,1)S(1)}, u32[]{:S(2)}, u32[]{:S(2)}) async-start(bf16[8,384,128]{2,1,0:T(8,128)(2,1)} %join_pass.1), calls=%async_computation.1 | async-start | bytes 1572864 | tf_op jit(solution)/shard_map/all_to_all | solution.py:383
  91.7 1.3 collective-permute-start.24
  93.0 3.6 %collective-permute-done.24 = bf16[8,32,384]{2,1,0:T(8,128)(2,1)S(1)} collective-permute-done((bf16[8,32,384]{2,1,0:T(8,128)(2,1)S(1)}, bf16[8,32,384]{2,1,0:T(8,128)(2,1)S(1)}, u32[]{:S(2)}, u32[]{:S(2)}) %collective-permute-start.24) | collective-permute-done | bytes 196640 | tf_op jit(solution)/shard_map/ppermute | solution.py:327
  96.7 2.4 %collective-permute-start.25 = (bf16[8,32,384]{2,1,0:T(8,128)(2,1)S(1)}, bf16[8,32,384]{2,1,0:T(8,128)(2,1)S(1)}, u32[]{:S(2)}, u32[]{:S(2)}) collective-permute-start(bf16[8,32,384]{2,1,0:T(8,128)(2,1)S(1)} %add_convert_fusion.2), channel_id=1, source_target_pairs={{0,8},{4,12},{8,0},{12,4},{1,9},{5,13},{9,1},{13,5},{2,10},{6,14},... | collective-permute-start | bytes 589832 | tf_op jit(solution)/shard_map/ppermute | solution.py:327
  99.1 4.3 %collective-permute-done.25 = bf16[8,32,384]{2,1,0:T(8,128)(2,1)S(1)} collective-permute-done((bf16[8,32,384]{2,1,0:T(8,128)(2,1)S(1)}, bf16[8,32,384]{2,1,0:T(8,128)(2,1)S(1)}, u32[]{:S(2)}, u32[]{:S(2)}) %collective-permute-start.25) | collective-permute-done | bytes 196640 | tf_op jit(solution)/shard_map/ppermute | solution.py:327
  103.5 3.5 %collective-permute-start.26 = (bf16[8,32,384]{2,1,0:T(8,128)(2,1)S(1)}, bf16[8,32,384]{2,1,0:T(8,128)(2,1)S(1)}, u32[]{:S(2)}, u32[]{:S(2)}) collective-permute-start(bf16[8,32,384]{2,1,0:T(8,128)(2,1)S(1)} %add_convert_fusion.1), channel_id=1, source_target_pairs={{0,2},{2,0},{1,3},{3,1},{4,6},{6,4},{5,7},{7,5},{8,10},{10,8},{9,1... | collective-permute-start | bytes 589832 | tf_op jit(solution)/shard_map/ppermute | solution.py:327
  107.0 3.1 %collective-permute-done.26 = bf16[8,32,384]{2,1,0:T(8,128)(2,1)S(1)} collective-permute-done((bf16[8,32,384]{2,1,0:T(8,128)(2,1)S(1)}, bf16[8,32,384]{2,1,0:T(8,128)(2,1)S(1)}, u32[]{:S(2)}, u32[]{:S(2)}) %collective-permute-start.26) | collective-permute-done | bytes 196640 | tf_op jit(solution)/shard_map/ppermute | solution.py:327
  110.0 0.7 add_convert_fusion
  110.8 4.5 %all-to-all-done.1.back = bf16[8,384,128]{2,1,0:T(8,128)(2,1)S(1)} async-done(((bf16[8,384,128]{2,1,0:T(8,128)(2,1)}), bf16[8,384,128]{2,1,0:T(8,128)(2,1)S(1)}, u32[]{:S(2)}, u32[]{:S(2)}) %all-to-all-start.1) | async-done | bytes 786464 | tf_op jit(solution)/shard_map/all_to_all | solution.py:383
  115.2 3.4 %all-to-all-start.2 = ((bf16[8,32,384]{2,1,0:T(8,128)(2,1)}), bf16[8,32,384]{2,1,0:T(8,128)(2,1)S(1)}, u32[]{:S(2)}, u32[]{:S(2)}) async-start(bf16[8,32,384]{2,1,0:T(8,128)(2,1)} %add_convert_fusion), calls=%async_computation.2 | async-start | bytes 393216 | tf_op jit(solution)/shard_map/all_to_all | solution.py:391
  118.7 2.8 %copy-done = bf16[1024,3072]{1,0:T(8,128)(2,1)S(1)} copy-done((bf16[1024,3072]{1,0:T(8,128)(2,1)S(1)}, bf16[1024,3072]{1,0:T(8,128)(2,1)}, u32[]{:S(2)}) %copy-start) | copy-done | bytes 6291480
  121.4 2.9 %rows_pass.1 = bf16[128,1024]{1,0:T(8,128)(2,1)S(1)} custom-call(bf16[8,384,128]{2,1,0:T(8,128)(2,1)S(1)} %all-to-all-done.1.back, bf16[128,1024]{1,0:T(8,128)(2,1)S(1)} %copy-done.6, f32[8,1024]{1,0:T(8,128)S(1)} %broadcast_in_dim.4.refs_20_.gain, bf16[1024,3072]{1,0:T(8,128)(2,1)S(1)} %copy-done), custom_call_target="tpu_custom_call" | custom-call | tf_op jit(solution)/shard_map/rows_pass/pallas_call | solution.py:284
  124.4 6.4 %collective-permute-start.21 = (bf16[128,1024]{1,0:T(8,128)(2,1)S(1)}, bf16[128,1024]{1,0:T(8,128)(2,1)S(1)}, u32[]{:S(2)}, u32[]{:S(2)}) collective-permute-start(bf16[128,1024]{1,0:T(8,128)(2,1)S(1)} %rows_pass.1), channel_id=1, source_target_pairs={{0,0},{1,128},{16,16},{17,144},{32,32},{33,160},{48,48},{49,176},{... | collective-permute-start | bytes 786440 | tf_op jit(solution)/shard_map/ppermute | solution.py:340
  131.2 1.1 collective-permute-done.27.other
  132.3 1.5 %final_pass.1 = f32[64,3072]{1,0:T(8,128)} custom-call(s32[20]{0:T(128)S(1)} %concatenate.6.refs_0_.meta, bf16[8,32,384]{2,1,0:T(8,128)(2,1)S(1)} %all-to-all-done.2.own, bf16[8,32,384]{2,1,0:T(8,128)(2,1)S(1)} %collective-permute-done.27.other), custom_call_target="tpu_custom_call" | custom-call | tf_op jit(solution)/shard_map/final_pass/pallas_call | solution.py:321
  133.8 1.0 collective-permute-done.21
  134.8 0.7 copy.11
  (56 shorter events, 2.5 us)
Async XLA Ops:
  0.6 60.4 %copy-start.7 = (f32[1024]{0:T(1024)S(1)}, f32[1024]{0:T(1024)}, u32[]{:S(2)}) copy-start(f32[1024]{0:T(1024)} %param.9) | copy-start | bytes 12292
  2.7 14.1 %collective-permute-start.2 = (bf16[136,1024]{1,0:T(8,128)(2,1)S(1)}, bf16[136,1024]{1,0:T(8,128)(2,1)S(1)}, u32[]{:S(2)}, u32[]{:S(2)}) collective-permute-start(bf16[136,1024]{1,0:T(8,128)(2,1)S(1)} %fusion.1), channel_id=1, source_target_pairs={{0,112},{1,240},{16,0},{17,128},{32,16},{33,144},{48,32},{49,160},... | collective-permute-start | bytes 835592 | tf_op jit(solution)/shard_map/ppermute | solution.py:340
  10.7 10.0 %collective-permute-start.3 = (bf16[136,1024]{1,0:T(8,128)(2,1)S(1)}, bf16[136,1024]{1,0:T(8,128)(2,1)S(1)}, u32[]{:S(2)}, u32[]{:S(2)}) collective-permute-start(bf16[136,1024]{1,0:T(8,128)(2,1)S(1)} %fusion.1), channel_id=1, source_target_pairs={{0,16},{1,144},{16,32},{17,160},{32,48},{33,176},{48,64},{49,192},... | collective-permute-start | bytes 835592 | tf_op jit(solution)/shard_map/ppermute | solution.py:340
  16.7 10.3 %collective-permute-start.4 = (bf16[136,1024]{1,0:T(8,128)(2,1)S(1)}, bf16[136,1024]{1,0:T(8,128)(2,1)S(1)}, u32[]{:S(2)}, u32[]{:S(2)}) collective-permute-start(bf16[136,1024]{1,0:T(8,128)(2,1)S(1)} %collective-permute-done.2.refs_2_), channel_id=1, source_target_pairs={{0,112},{16,0},{32,16},{48,32},{64,48},{80,64},{96,80},{112,96},{1... | collective-permute-start | bytes 835592 | tf_op jit(solution)/shard_map/ppermute | solution.py:331
  20.7 18.9 %collective-permute-start.5 = (bf16[136,1024]{1,0:T(8,128)(2,1)S(1)}, bf16[136,1024]{1,0:T(8,128)(2,1)S(1)}, u32[]{:S(2)}, u32[]{:S(2)}) collective-permute-start(bf16[136,1024]{1,0:T(8,128)(2,1)S(1)} %collective-permute-done.3.refs_3_), channel_id=1, source_target_pairs={{0,16},{16,32},{32,48},{48,64},{64,80},{80,96},{96,112},{112,0},{1... | collective-permute-start | bytes 835592 | tf_op jit(solution)/shard_map/ppermute | solution.py:331
  20.8 18.9 %collective-permute-start.1 = (bf16[136,1024]{1,0:T(8,128)(2,1)S(1)}, bf16[136,1024]{1,0:T(8,128)(2,1)S(1)}, u32[]{:S(2)}, u32[]{:S(2)}) collective-permute-start(bf16[136,1024]{1,0:T(8,128)(2,1)S(1)} %fusion.1), channel_id=1, source_target_pairs={{0,0},{1,128},{16,16},{17,144},{32,32},{33,160},{48,48},{49,176},{... | collective-permute-start | bytes 835592 | tf_op jit(solution)/shard_map/ppermute | solution.py:340
  27.1 12.8 %collective-permute-start.6 = (bf16[136,1024]{1,0:T(8,128)(2,1)S(1)}, bf16[136,1024]{1,0:T(8,128)(2,1)S(1)}, u32[]{:S(2)}, u32[]{:S(2)}) collective-permute-start(bf16[136,1024]{1,0:T(8,128)(2,1)S(1)} %collective-permute-done.4.refs_4_), channel_id=1, source_target_pairs={{0,112},{16,0},{32,16},{48,32},{64,48},{80,64},{96,80},{112,96},{1... | collective-permute-start | bytes 835592 | tf_op jit(solution)/shard_map/ppermute | solution.py:331
  31.3 7.8 %collective-permute-start.19 = (bf16[16,64,128]{2,1,0:T(8,128)(2,1)S(1)}, bf16[16,64,128]{2,1,0:T(8,128)(2,1)}, u32[]{:S(2)}, u32[]{:S(2)}) collective-permute-start(bf16[16,64,128]{2,1,0:T(8,128)(2,1)S(1)} %bitcast.18), channel_id=1, source_target_pairs={{0,0},{1,128},{16,16},{17,144},{32,32},{33,160},{48,48},{49,176},{... | collective-permute-start | bytes 786440 | tf_op jit(solution)/shard_map/ppermute | solution.py:340
  33.3 5.9 %collective-permute-start = (s32[16]{0:T(128)}, s32[16]{0:T(128)S(1)}, u32[]{:S(2)}, u32[]{:S(2)}) collective-permute-start(s32[16]{0:T(128)} %bitcast.19), channel_id=1, source_target_pairs={{0,0},{1,128},{16,16},{17,144},{32,32},{33,160},{48,48},{49,176},{... | collective-permute-start | bytes 200 | tf_op jit(solution)/shard_map/ppermute | solution.py:340
  39.1 5.7 %collective-permute-start.12 = (bf16[136,1024]{1,0:T(8,128)(2,1)S(1)}, bf16[136,1024]{1,0:T(8,128)(2,1)S(1)}, u32[]{:S(2)}, u32[]{:S(2)}) collective-permute-start(bf16[136,1024]{1,0:T(8,128)(2,1)S(1)} %collective-permute-done.3.refs_3_), channel_id=1, source_target_pairs={{0,1},{1,0},{2,3},{3,2},{4,5},{5,4},{6,7},{7,6},{8,9},{9,8},{10,11... | collective-permute-start | bytes 835592 | tf_op jit(solution)/shard_map/ppermute | solution.py:327
  39.1 8.3 %collective-permute-start.11 = (bf16[136,1024]{1,0:T(8,128)(2,1)S(1)}, bf16[136,1024]{1,0:T(8,128)(2,1)S(1)}, u32[]{:S(2)}, u32[]{:S(2)}) collective-permute-start(bf16[136,1024]{1,0:T(8,128)(2,1)S(1)} %collective-permute-done.2.refs_2_), channel_id=1, source_target_pairs={{0,1},{1,0},{2,3},{3,2},{4,5},{5,4},{6,7},{7,6},{8,9},{9,8},{10,11... | collective-permute-start | bytes 835592 | tf_op jit(solution)/shard_map/ppermute | solution.py:327
  39.7 9.3 %collective-permute-start.7 = (bf16[136,1024]{1,0:T(8,128)(2,1)S(1)}, bf16[136,1024]{1,0:T(8,128)(2,1)S(1)}, u32[]{:S(2)}, u32[]{:S(2)}) collective-permute-start(bf16[136,1024]{1,0:T(8,128)(2,1)S(1)} %collective-permute-done.5.refs_5_), channel_id=1, source_target_pairs={{0,16},{16,32},{32,48},{48,64},{64,80},{80,96},{96,112},{112,0},{1... | collective-permute-start | bytes 835592 | tf_op jit(solution)/shard_map/ppermute | solution.py:331
  39.7 11.9 %collective-permute-start.10 = (bf16[136,1024]{1,0:T(8,128)(2,1)S(1)}, bf16[136,1024]{1,0:T(8,128)(2,1)S(1)}, u32[]{:S(2)}, u32[]{:S(2)}) collective-permute-start(bf16[136,1024]{1,0:T(8,128)(2,1)S(1)} %collective-permute-done.1.refs_1_), channel_id=1, source_target_pairs={{0,1},{1,0},{2,3},{3,2},{4,5},{5,4},{6,7},{7,6},{8,9},{9,8},{10,11... | collective-permute-start | bytes 835592 | tf_op jit(solution)/shard_map/ppermute | solution.py:327
  39.9 12.4 %collective-permute-start.14 = (bf16[136,1024]{1,0:T(8,128)(2,1)S(1)}, bf16[136,1024]{1,0:T(8,128)(2,1)}, u32[]{:S(2)}, u32[]{:S(2)}) collective-permute-start(bf16[136,1024]{1,0:T(8,128)(2,1)S(1)} %collective-permute-done.5.refs_5_), channel_id=1, source_target_pairs={{0,1},{1,0},{2,3},{3,2},{4,5},{5,4},{6,7},{7,6},{8,9},{9,8},{10,11... | collective-permute-start | bytes 835592 | tf_op jit(solution)/shard_map/ppermute | solution.py:327
  40.3 20.7 %all-to-all-start = ((bf16[16,64,128]{2,1,0:T(8,128)(2,1)}), bf16[16,64,128]{2,1,0:T(8,128)(2,1)S(1)}, u32[]{:S(2)}, u32[]{:S(2)}) async-start(bf16[16,64,128]{2,1,0:T(8,128)(2,1)} %collective-permute-done.19), calls=%async_computation | async-start | bytes 524288 | tf_op jit(solution)/shard_map/all_to_all | solution.py:378
  44.8 11.0 %collective-permute-start.9 = (bf16[72,1024]{1,0:T(8,128)(2,1)S(1)}, bf16[72,1024]{1,0:T(8,128)(2,1)S(1)}, u32[]{:S(2)}, u32[]{:S(2)}) collective-permute-start(bf16[72,1024]{1,0:T(8,128)(2,1)S(1)} %slice.9), channel_id=1, source_target_pairs={{0,112},{16,0},{32,16},{48,32},{64,48},{80,64},{96,80},{112,96},{1... | collective-permute-start | bytes 442376 | tf_op jit(solution)/shard_map/ppermute | solution.py:331
  47.5 10.9 %copy-start.1 = (bf16[136,1024]{1,0:T(8,128)(2,1)}, bf16[136,1024]{1,0:T(8,128)(2,1)S(1)}, u32[]{:S(2)}) copy-start(bf16[136,1024]{1,0:T(8,128)(2,1)S(1)} %collective-permute-done.11.refs_11_) | copy-start | bytes 835588
  47.5 13.5 %collective-permute-start.13 = (bf16[136,1024]{1,0:T(8,128)(2,1)S(1)}, bf16[136,1024]{1,0:T(8,128)(2,1)}, u32[]{:S(2)}, u32[]{:S(2)}) collective-permute-start(bf16[136,1024]{1,0:T(8,128)(2,1)S(1)} %collective-permute-done.4.refs_4_), channel_id=1, source_target_pairs={{0,1},{1,0},{2,3},{3,2},{4,5},{5,4},{6,7},{7,6},{8,9},{9,8},{10,11... | collective-permute-start | bytes 835592 | tf_op jit(solution)/shard_map/ppermute | solution.py:327
  49.0 12.0 %collective-permute-start.16 = (bf16[136,1024]{1,0:T(8,128)(2,1)S(1)}, bf16[136,1024]{1,0:T(8,128)(2,1)}, u32[]{:S(2)}, u32[]{:S(2)}) collective-permute-start(bf16[136,1024]{1,0:T(8,128)(2,1)S(1)} %collective-permute-done.7.refs_7_), channel_id=1, source_target_pairs={{0,1},{1,0},{2,3},{3,2},{4,5},{5,4},{6,7},{7,6},{8,9},{9,8},{10,11... | collective-permute-start | bytes 835592 | tf_op jit(solution)/shard_map/ppermute | solution.py:327
  51.6 0.7 copy-start.3
  52.3 8.8 %collective-permute-start.15 = (bf16[136,1024]{1,0:T(8,128)(2,1)S(1)}, bf16[136,1024]{1,0:T(8,128)(2,1)}, u32[]{:S(2)}, u32[]{:S(2)}) collective-permute-start(bf16[136,1024]{1,0:T(8,128)(2,1)S(1)} %collective-permute-done.6.refs_6_), channel_id=1, source_target_pairs={{0,1},{1,0},{2,3},{3,2},{4,5},{5,4},{6,7},{7,6},{8,9},{9,8},{10,11... | collective-permute-start | bytes 835592 | tf_op jit(solution)/shard_map/ppermute | solution.py:327
  52.3 6.1 %collective-permute-start.8 = (bf16[64,1024]{1,0:T(8,128)(2,1)S(1)}, bf16[64,1024]{1,0:T(8,128)(2,1)}, u32[]{:S(2)}, u32[]{:S(2)}) collective-permute-start(bf16[64,1024]{1,0:T(8,128)(2,1)S(1)} %slice.8), channel_id=1, source_target_pairs={{0,16},{16,32},{32,48},{48,64},{64,80},{80,96},{96,112},{112,0},{1... | collective-permute-start | bytes 393224 | tf_op jit(solution)/shard_map/ppermute | solution.py:331
  55.8 5.2 %collective-permute-start.18 = (bf16[72,1024]{1,0:T(8,128)(2,1)S(1)}, bf16[72,1024]{1,0:T(8,128)(2,1)}, u32[]{:S(2)}, u32[]{:S(2)}) collective-permute-start(bf16[72,1024]{1,0:T(8,128)(2,1)S(1)} %collective-permute-done.9.refs_9_), channel_id=1, source_target_pairs={{0,1},{1,0},{2,3},{3,2},{4,5},{5,4},{6,7},{7,6},{8,9},{9,8},{10,11... | collective-permute-start | bytes 442376 | tf_op jit(solution)/shard_map/ppermute | solution.py:327
  58.4 2.6 %collective-permute-start.17 = (bf16[64,1024]{1,0:T(8,128)(2,1)}, bf16[64,1024]{1,0:T(8,128)(2,1)}, u32[]{:S(2)}, u32[]{:S(2)}) collective-permute-start(bf16[64,1024]{1,0:T(8,128)(2,1)} %collective-permute-done.8.refs_8_), channel_id=1, source_target_pairs={{0,1},{1,0},{2,3},{3,2},{4,5},{5,4},{6,7},{7,6},{8,9},{9,8},{10,11... | collective-permute-start | bytes 393224 | tf_op jit(solution)/shard_map/ppermute | solution.py:327
  61.0 1.0 copy-start.2
  62.0 1.0 copy-start.4
  75.0 8.9 %copy-start.5 = (bf16[128,1024]{1,0:T(8,128)(2,1)}, bf16[128,1024]{1,0:T(8,128)(2,1)S(1)}, u32[]{:S(2)}) copy-start(bf16[128,1024]{1,0:T(8,128)(2,1)S(1)} %get-tuple-element.8.mine) | copy-start | bytes 786436
  75.0 5.9 %collective-permute-start.20 = (bf16[16,320,128]{2,1,0:T(8,128)(2,1)S(1)}, bf16[16,320,128]{2,1,0:T(8,128)(2,1)S(1)}, u32[]{:S(2)}, u32[]{:S(2)}) collective-permute-start(bf16[16,320,128]{2,1,0:T(8,128)(2,1)S(1)} %get-tuple-element.7.part), channel_id=1, source_target_pairs={{0,1},{1,0},{2,3},{3,2},{4,5},{5,4},{6,7},{7,6},{8,9},{9,8},{10,11... | collective-permute-start | bytes 3932168 | tf_op jit(solution)/shard_map/ppermute | solution.py:327
  83.9 34.7 %copy-start.6 = (bf16[128,1024]{1,0:T(8,128)(2,1)S(1)}, bf16[128,1024]{1,0:T(8,128)(2,1)}, u32[]{:S(2)}) copy-start(bf16[128,1024]{1,0:T(8,128)(2,1)} %copy-done.5) | copy-start | bytes 786436
  83.9 7.7 %collective-permute-start.22 = (bf16[8,32,384]{2,1,0:T(8,128)(2,1)S(1)}, bf16[8,32,384]{2,1,0:T(8,128)(2,1)S(1)}, u32[]{:S(2)}, u32[]{:S(2)}) collective-permute-start(bf16[8,32,384]{2,1,0:T(8,128)(2,1)S(1)} %get-tuple-element.10), channel_id=1, source_target_pairs={{0,0},{1,128},{16,16},{17,144},{32,32},{33,160},{48,48},{49,176},{... | collective-permute-start | bytes 589832 | tf_op jit(solution)/shard_map/ppermute | solution.py:340
  86.0 5.7 %collective-permute-start.23 = (bf16[8,32,384]{2,1,0:T(8,128)(2,1)S(1)}, bf16[8,32,384]{2,1,0:T(8,128)(2,1)S(1)}, u32[]{:S(2)}, u32[]{:S(2)}) collective-permute-start(bf16[8,32,384]{2,1,0:T(8,128)(2,1)S(1)} %get-tuple-element.11), channel_id=1, source_target_pairs={{0,1},{1,129},{16,17},{17,145},{32,33},{33,161},{48,49},{49,177},{... | collective-permute-start | bytes 589832 | tf_op jit(solution)/shard_map/ppermute | solution.py:340
  87.7 27.6 %all-to-all-start.1 = ((bf16[8,384,128]{2,1,0:T(8,128)(2,1)}), bf16[8,384,128]{2,1,0:T(8,128)(2,1)S(1)}, u32[]{:S(2)}, u32[]{:S(2)}) async-start(bf16[8,384,128]{2,1,0:T(8,128)(2,1)} %join_pass.1), calls=%async_computation.1 | async-start | bytes 1572864 | tf_op jit(solution)/shard_map/all_to_all | solution.py:383
  91.7 4.9 %collective-permute-start.24 = (bf16[8,32,384]{2,1,0:T(8,128)(2,1)S(1)}, bf16[8,32,384]{2,1,0:T(8,128)(2,1)S(1)}, u32[]{:S(2)}, u32[]{:S(2)}) collective-permute-start(bf16[8,32,384]{2,1,0:T(8,128)(2,1)S(1)} %add_convert_fusion.3), channel_id=1, source_target_pairs={{0,4},{4,0},{8,12},{12,8},{1,5},{5,1},{9,13},{13,9},{2,6},{6,2},{1... | collective-permute-start | bytes 589832 | tf_op jit(solution)/shard_map/ppermute | solution.py:327
  96.7 6.7 %collective-permute-start.25 = (bf16[8,32,384]{2,1,0:T(8,128)(2,1)S(1)}, bf16[8,32,384]{2,1,0:T(8,128)(2,1)S(1)}, u32[]{:S(2)}, u32[]{:S(2)}) collective-permute-start(bf16[8,32,384]{2,1,0:T(8,128)(2,1)S(1)} %add_convert_fusion.2), channel_id=1, source_target_pairs={{0,8},{4,12},{8,0},{12,4},{1,9},{5,13},{9,1},{13,5},{2,10},{6,14},... | collective-permute-start | bytes 589832 | tf_op jit(solution)/shard_map/ppermute | solution.py:327
  103.5 6.5 %collective-permute-start.26 = (bf16[8,32,384]{2,1,0:T(8,128)(2,1)S(1)}, bf16[8,32,384]{2,1,0:T(8,128)(2,1)S(1)}, u32[]{:S(2)}, u32[]{:S(2)}) collective-permute-start(bf16[8,32,384]{2,1,0:T(8,128)(2,1)S(1)} %add_convert_fusion.1), channel_id=1, source_target_pairs={{0,2},{2,0},{1,3},{3,1},{4,6},{6,4},{5,7},{7,5},{8,10},{10,8},{9,1... | collective-permute-start | bytes 589832 | tf_op jit(solution)/shard_map/ppermute | solution.py:327
  115.2 15.6 %all-to-all-start.2 = ((bf16[8,32,384]{2,1,0:T(8,128)(2,1)}), bf16[8,32,384]{2,1,0:T(8,128)(2,1)S(1)}, u32[]{:S(2)}, u32[]{:S(2)}) async-start(bf16[8,32,384]{2,1,0:T(8,128)(2,1)} %add_convert_fusion), calls=%async_computation.2 | async-start | bytes 393216 | tf_op jit(solution)/shard_map/all_to_all | solution.py:391
  118.6 2.8 %copy-start = (bf16[1024,3072]{1,0:T(8,128)(2,1)S(1)}, bf16[1024,3072]{1,0:T(8,128)(2,1)}, u32[]{:S(2)}) copy-start(bf16[1024,3072]{1,0:T(8,128)(2,1)} %w.1) | copy-start | bytes 18874372
  124.4 10.4 %collective-permute-start.21 = (bf16[128,1024]{1,0:T(8,128)(2,1)S(1)}, bf16[128,1024]{1,0:T(8,128)(2,1)S(1)}, u32[]{:S(2)}, u32[]{:S(2)}) collective-permute-start(bf16[128,1024]{1,0:T(8,128)(2,1)S(1)} %rows_pass.1), channel_id=1, source_target_pairs={{0,0},{1,128},{16,16},{17,144},{32,32},{33,160},{48,48},{49,176},{... | collective-permute-start | bytes 786440 | tf_op jit(solution)/shard_map/ppermute | solution.py:340
  130.8 1.5 %collective-permute-start.27 = (bf16[8,32,384]{2,1,0:T(8,128)(2,1)S(1)}, bf16[8,32,384]{2,1,0:T(8,128)(2,1)S(1)}, u32[]{:S(2)}, u32[]{:S(2)}) collective-permute-start(bf16[8,32,384]{2,1,0:T(8,128)(2,1)S(1)} %all-to-all-done.2.own), channel_id=1, source_target_pairs={{0,1},{1,0},{2,3},{3,2},{4,5},{5,4},{6,7},{7,6},{8,9},{9,8},{10,11... | collective-permute-start | bytes 589832 | tf_op jit(solution)/shard_map/ppermute | solution.py:327

commit v3 on v2

--- a/solution.py
+++ b/solution.py
@@ -32,63 +32,122 @@
     return (p % 8) * 2 + p // 8
 
 
-PIECES = 9
+EARLY = (0, 1, 7, 2, 6)
+LATE = (3, 5, 4)
+
+
+def block_at(meta, n, offsets):
+    half = meta[NBLK + 1]
+    side = half if n < len(offsets) else 1 - half
+    return side * 8 + (meta[NBLK] + offsets[n % len(offsets)]) % 8
+
+
+def project(meta, n, rows, gain, wq, wk, wv, normed):
+    values = rows.astype(F32)
+    inverse = lax.rsqrt(jnp.mean(values * values, axis=-1, keepdims=True) + EPS)
+    nrm = (values * inverse * gain[0:1, :]).astype(BF16)
+    normed[n : n + 2] = nrm.reshape(2, BLOCK, D)
+    own = pl.multiple_of(meta[NBLK + 1] * HALF, HALF)
+    qn = normed[n : n + 2, pl.ds(own, HALF), :].reshape(BLOCK, D)
+    q = dot(qn, wq[...], 1, 0).astype(BF16).reshape(2, HALF, HEAD)
+    k = dot(nrm, wk[...], 1, 0).astype(BF16).reshape(2, BLOCK, HEAD)
+    v = dot(nrm, wv[...], 1, 0).astype(BF16).reshape(2, BLOCK, HEAD)
+    return q, k, v
+
+
+def early_kernel(*refs):
+    meta, pieces = refs[0], refs[1:11]
+    gain, wq, wk, wv, normed, q_o, k_o, v_o, info, mine = refs[11:]
+    target = meta[meta[NBLK + 1] * 8 + meta[NBLK]]
+    mine[...] = jnp.zeros(mine.shape, BF16)
+    for n in range(0, 10, 2):
+        rows = jnp.concatenate([pieces[n][0:BLOCK, :], pieces[n + 1][0:BLOCK, :]], axis=0)
+        q_o[n : n + 2], k_o[n : n + 2], v_o[n : n + 2] = project(meta, n, rows, gain, wq, wk, wv, normed)
+    for n in range(10):
+        info[n] = pieces[n][BLOCK : BLOCK + EXTRA, 0:QROWS].astype(F32)
+
+        @pl.when(block_at(meta, n, EARLY) == target)
+        def _():
+            mine[...] = pieces[n][0:BLOCK, :]
+
+
+def early_pass(meta, pieces, gain, w_head):
+    made = [
+        ((10, BLOCK, D), BF16),
+        ((10, HALF, HEAD), BF16),
+        ((10, BLOCK, HEAD), BF16),
+        ((10, BLOCK, HEAD), BF16),
+        ((10, EXTRA, QROWS), F32),
+        ((BLOCK, D), BF16),
+    ]
+    return pl.pallas_call(
+        early_kernel,
+        grid_spec=pltpu.PrefetchScalarGridSpec(
+            num_scalar_prefetch=1,
+            grid=(1,),
+            in_specs=[pl.BlockSpec((BLOCK + EXTRA, D), lambda i, m: (0, 0))] * 10
+            + [pl.BlockSpec((8, D), lambda i, m: (0, 0))]
+            + [pl.BlockSpec((D, HEAD), lambda i, m: (0, 0))] * 3,
+            out_specs=[pl.BlockSpec(x, lambda i, m, r=len(x): (0,) * r) for x, t in made],
+        ),
+        out_shape=[jax.ShapeDtypeStruct(x, t) for x, t in made],
+        name="early_pass",
+        compiler_params=pltpu.CompilerParams(vmem_limit_bytes=20 * 1024 * 1024),
+    )(meta, *pieces, gain, *w_head)
 
 
 def head_kernel(*refs):
-    meta, pieces, others, rest = refs[0], refs[1 : 1 + PIECES], refs[1 + PIECES : 1 + 2 * PIECES], refs[1 + 2 * PIECES :]
+    meta, pieces = refs[0], refs[1:9]
     (
-        do, gain, wq, wk, wv,
+        q_i, k_i, v_i, info_i, mine_i, do, gain, wq, wk, wv,
         normed, mine, part,
-        rows_s, q_s, do_s, k_s, v_s, dk_s, dv_s, e_s, p_s, docs, inv, sems,
-    ) = rest
+        q_s, do_s, k_s, v_s, dk_s, dv_s, e_s, p_s, docs, inv,
+    ) = refs[9:]
     step = pl.program_id(0)
-    z = meta[NBLK]
     half = meta[NBLK + 1]
 
     @pl.when(step == 0)
     def _():
-        copies = []
-        for c, group in enumerate((pieces, others)):
-            side = half if c == 0 else 1 - half
-            for n, ref in enumerate(group):
-                offset = (0, 1, 7, 2, 6, 3, 5, 4, 4)[n]
-                target = rows_s.at[side * 8 + (z + offset) % 8]
-                if n == 7:
-                    target = target.at[0:HALF]
-                elif n == 8:
-                    target = target.at[HALF : BLOCK + EXTRA]
-                copies.append(pltpu.make_async_copy(ref, target, sems.at[c * PIECES + n]))
-        for copy in copies:
-            copy.start()
-
         def put(p, carry):
             inv[meta[p]] = p
             return carry
 
         lax.fori_loop(0, NBLK, put, 0)
-        docs[...] = jnp.full(docs.shape, 1000.0, F32)
+        docs[...] = jnp.zeros(docs.shape, F32)
         dk_s[...] = jnp.zeros(dk_s.shape, F32)
         dv_s[...] = jnp.zeros(dv_s.shape, F32)
-        for copy in copies:
-            copy.wait()
-        mine[...] = rows_s[meta[half * 8 + z], 0:BLOCK, :]
-
-    rows = rows_s[pl.ds(step * 4, 4), 0:BLOCK, :].astype(F32)
-    inverse = lax.rsqrt(jnp.mean(rows * rows, axis=-1, keepdims=True) + EPS)
-    nrm = (rows * inverse * gain[0:1, :][None]).astype(BF16)
-    normed[...] = nrm
-    nrm = nrm.reshape(KROWS, D)
-    k_s[step] = dot(nrm, wk[...], 1, 0).astype(BF16)
-    v_s[step] = dot(nrm, wv[...], 1, 0).astype(BF16)
-    own = pl.multiple_of(half * HALF, HALF)
-    qn = normed[:, pl.ds(own, HALF), :].reshape(QROWS, D)
-    q_s[...] = dot(qn, wq[...], 1, 0).astype(BF16)
+        mine[...] = mine_i[...]
+        for n in range(10):
+            b = block_at(meta, n, EARLY)
+            q_s[b] = q_i[n]
+            k_s[b] = k_i[n]
+            v_s[b] = v_i[n]
+            docs[b // 4] += info_i[n]
+        raw = []
+        for c in range(2):
+            down, up, top, low = pieces[c * 4 : c * 4 + 4]
+            raw.append((down[0:BLOCK, :], down[BLOCK : BLOCK + EXTRA, 0:QROWS]))
+            raw.append((up[0:BLOCK, :], up[BLOCK : BLOCK + EXTRA, 0:QROWS]))
+            raw.append((jnp.concatenate([top[...], low[0:HALF, :]], axis=0), low[HALF : HALF + EXTRA, 0:QROWS]))
+        target = meta[half * 8 + meta[NBLK]]
+        for n in range(0, 6, 2):
+            rows = jnp.concatenate([raw[n][0], raw[n + 1][0]], axis=0)
+            q, k, v = project(meta, n, rows, gain, wq, wk, wv, normed)
+            for i in range(2):
+                b = block_at(meta, n + i, LATE)
+                q_s[b] = q[i]
+                k_s[b] = k[i]
+                v_s[b] = v[i]
+                docs[b // 4] += raw[n + i][1].astype(F32)
+
+                @pl.when(b == target)
+                def _():
+                    mine[...] = raw[n + i][0]
+
+    q = q_s[pl.ds(step * 4, 4)].reshape(QROWS, HEAD)
     for t in range(4):
         do_s[t * HALF : (t + 1) * HALF, :] = do[place_of(inv[step * 4 + t])]
-
-    info = jnp.sum(rows_s[pl.ds(step * 4, 4), BLOCK : BLOCK + EXTRA, 0:QROWS].astype(F32), axis=0)
-    docs[step] = info
+    info = docs[step]
     mine_docs = jnp.where(half == 0, info[0:1, :], info[1:2, :])
     lane = lax.broadcasted_iota(jnp.int32, (1, QROWS), 1)
     q_pos = step * KROWS + (lane // HALF) * BLOCK + half * HALF + lane % HALF
@@ -102,7 +161,7 @@
     low_tile = jnp.min(q_first) // KROWS
 
     def scores(g, total):
-        s = dot(k_s[g], q_s[...], 1, 1) * FACTOR
+        s = dot(k_s[pl.ds(g * 4, 4)].reshape(KROWS, HEAD), q, 1, 1) * FACTOR
         j = g * KROWS + lax.broadcasted_iota(jnp.int32, (KROWS, QROWS), 0)
         e = jnp.where((j >= q_first) & (j <= q_pos), jnp.exp(s), 0.0)
         e_s[g] = e
@@ -112,7 +171,7 @@
     scale = 1.0 / total
 
     def deltas(g, delta):
-        grad = dot(v_s[g], do_s[...], 1, 1)
+        grad = dot(v_s[pl.ds(g * 4, 4)].reshape(KROWS, HEAD), do_s[...], 1, 1)
         p_s[g] = grad
         low = (e_s[g] * scale).astype(BF16)
         dv_s[g] += dot(low, do_s[...], 1, 0)
@@ -122,8 +181,8 @@
 
     def grads(g, dq):
         ds = (e_s[g] * scale * (p_s[g] - delta)).astype(BF16)
-        dk_s[g] += dot(ds, q_s[...], 1, 0)
-        return dq + dot(ds, k_s[g], 0, 0)
+        dk_s[g] += dot(ds, q, 1, 0)
+        return dq + dot(ds, k_s[pl.ds(g * 4, 4)].reshape(KROWS, HEAD), 0, 0)
 
     dq = lax.fori_loop(low_tile, step + 1, grads, jnp.zeros((QROWS, HEAD), F32))
     dq = (dq * FACTOR).astype(BF16)
@@ -135,47 +194,34 @@
         part[:, HALF + BLOCK :, :] = dv_s[...].astype(BF16).reshape(NBLK, BLOCK, HEAD)
 
 
-def head_pass(meta, pieces, others, do, gain, w_head):
+def head_pass(meta, pieces, made, do, gain, w_head):
     pack = (NBLK, HALF + 2 * BLOCK, HEAD)
-    grid_spec = pltpu.PrefetchScalarGridSpec(
-        num_scalar_prefetch=1,
-        grid=(STEPS,),
-        in_specs=[pl.BlockSpec(memory_space=pl.ANY)] * (2 * PIECES)
-        + [
-            pl.BlockSpec((NBLK, HALF, HEAD), lambda i, m: (0, 0, 0)),
-            pl.BlockSpec((8, D), lambda i, m: (0, 0)),
-        ]
-        + [pl.BlockSpec((D, HEAD), lambda i, m: (0, 0))] * 3,
-        out_specs=[
-            pl.BlockSpec((4, BLOCK, D), lambda i, m: (i, 0, 0)),
-            pl.BlockSpec((BLOCK, D), lambda i, m: (0, 0)),
-            pl.BlockSpec(pack, lambda i, m: (0, 0, 0)),
-        ],
-        scratch_shapes=[
-            pltpu.VMEM((NBLK, BLOCK + EXTRA, D), BF16),
-            pltpu.VMEM((QROWS, HEAD), BF16),
-            pltpu.VMEM((QROWS, HEAD), BF16),
-            pltpu.VMEM((STEPS, KROWS, HEAD), BF16),
-            pltpu.VMEM((STEPS, KROWS, HEAD), BF16),
-            pltpu.VMEM((STEPS, KROWS, HEAD), F32),
-            pltpu.VMEM((STEPS, KROWS, HEAD), F32),
-            pltpu.VMEM((STEPS, KROWS, QROWS), F32),
-            pltpu.VMEM((STEPS, KROWS, QROWS), F32),
-            pltpu.VMEM((STEPS, EXTRA, QROWS), F32),
-            pltpu.SMEM((NBLK,), jnp.int32),
-            pltpu.SemaphoreType.DMA((2 * PIECES,)),
-        ],
-    )
+    given = [*pieces, *made, do, gain, *w_head]
+    outs = [(6, BLOCK, D), (BLOCK, D), pack]
     return pl.pallas_call(
         head_kernel,
-        grid_spec=grid_spec,
-        out_shape=[
-            jax.ShapeDtypeStruct((NBLK, BLOCK, D), BF16),
-            jax.ShapeDtypeStruct((BLOCK, D), BF16),
-            jax.ShapeDtypeStruct(pack, BF16),
-        ],
-        name="head_pass", compiler_params=pltpu.CompilerParams(vmem_limit_bytes=26 * 1024 * 1024),
-    )(meta, *pieces, *others, do, gain, *w_head)
+        grid_spec=pltpu.PrefetchScalarGridSpec(
+            num_scalar_prefetch=1,
+            grid=(STEPS,),
+            in_specs=[pl.BlockSpec(x.shape, lambda i, m, r=x.ndim: (0,) * r) for x in given],
+            out_specs=[pl.BlockSpec(x, lambda i, m, r=len(x): (0,) * r) for x in outs],
+            scratch_shapes=[
+                pltpu.VMEM((NBLK, HALF, HEAD), BF16),
+                pltpu.VMEM((QROWS, HEAD), BF16),
+                pltpu.VMEM((NBLK, BLOCK, HEAD), BF16),
+                pltpu.VMEM((NBLK, BLOCK, HEAD), BF16),
+                pltpu.VMEM((STEPS, KROWS, HEAD), F32),
+                pltpu.VMEM((STEPS, KROWS, HEAD), F32),
+                pltpu.VMEM((STEPS, KROWS, QROWS), F32),
+                pltpu.VMEM((STEPS, KROWS, QROWS), F32),
+                pltpu.VMEM((STEPS, EXTRA, QROWS), F32),
+                pltpu.SMEM((NBLK,), jnp.int32),
+            ],
+        ),
+        out_shape=[jax.ShapeDtypeStruct(x, BF16) for x in outs],
+        name="head_pass",
+        compiler_params=pltpu.CompilerParams(vmem_limit_bytes=26 * 1024 * 1024),
+    )(meta, *given)
 
 
 def total_of(part, came, half, blocks):
@@ -187,52 +233,45 @@
     return first, second, both.astype(BF16)
 
 
-def weight_kernel(meta, normed, part, came, here, there, dw_s):
-    step = pl.program_id(0)
+def weight_kernel(meta, n_early, n_late, part, came, here, there, grads):
     half = meta[NBLK + 1]
     y = meta[NBLK + 2]
-    first, second, both = total_of(part, came, half, slice(None))
-    dq = jnp.concatenate([first, second], axis=1).reshape(KROWS, HEAD)
-    dk = both[:, 0:BLOCK, :].reshape(KROWS, HEAD)
-    dv = both[:, BLOCK:, :].reshape(KROWS, HEAD)
-    grads = jnp.concatenate([dq, dk, dv], axis=1)
-    made = dot(normed[...].reshape(KROWS, D // 2), grads, 0, 0)
-
-    @pl.when(step == 0)
-    def _():
-        dw_s[...] = made
-
-    @pl.when(step > 0)
-    def _():
-        dw_s[...] += made
-
-    @pl.when(step == STEPS - 1)
-    def _():
-        every = dw_s[...].reshape(8, 2, 32, 3 * HEAD)
-        here[...] = jnp.where(y == 0, every[:, 0], every[:, 1]).astype(BF16)
-        there[...] = jnp.where(y == 0, every[:, 1], every[:, 0]).astype(BF16)
-
-
-def weight_pass(meta, normed, part, came):
-    pack = (4, HALF + 2 * BLOCK, HEAD)
+    for n in range(NBLK):
+        b = block_at(meta, n, EARLY) if n < 10 else block_at(meta, n - 10, LATE)
+        first, second, both = total_of(part, came, half, b)
+        grads[n, 0:HALF, 0:HEAD] = first
+        grads[n, HALF:BLOCK, 0:HEAD] = second
+        grads[n, :, HEAD : 2 * HEAD] = both[0:BLOCK]
+        grads[n, :, 2 * HEAD :] = both[BLOCK:]
+    made = dot(n_early[...].reshape(10 * BLOCK, D // 2), grads[0:10].reshape(10 * BLOCK, 3 * HEAD), 0, 0)
+    made = made + dot(n_late[...].reshape(6 * BLOCK, D // 2), grads[10:16].reshape(6 * BLOCK, 3 * HEAD), 0, 0)
+    every = made.reshape(8, 2, 32, 3 * HEAD)
+    here[...] = jnp.where(y == 0, every[:, 0], every[:, 1]).astype(BF16)
+    there[...] = jnp.where(y == 0, every[:, 1], every[:, 0]).astype(BF16)
+
+
+def weight_pass(meta, n_early, n_late, part, came):
+    pack = (NBLK, HALF + 2 * BLOCK, HEAD)
     shape = (8, 32, 3 * HEAD)
     grid_spec = pltpu.PrefetchScalarGridSpec(
         num_scalar_prefetch=1,
-        grid=(STEPS,),
+        grid=(1,),
         in_specs=[
-            pl.BlockSpec((4, BLOCK, D // 2), lambda i, m: (i, 0, m[NBLK + 1])),
-            pl.BlockSpec(pack, lambda i, m: (i, 0, 0)),
-            pl.BlockSpec(pack, lambda i, m: (i, 0, 0)),
+            pl.BlockSpec((10, BLOCK, D // 2), lambda i, m: (0, 0, m[NBLK + 1])),
+            pl.BlockSpec((6, BLOCK, D // 2), lambda i, m: (0, 0, m[NBLK + 1])),
+            pl.BlockSpec(pack, lambda i, m: (0, 0, 0)),
+            pl.BlockSpec(pack, lambda i, m: (0, 0, 0)),
         ],
         out_specs=[pl.BlockSpec(shape, lambda i, m: (0, 0, 0))] * 2,
-        scratch_shapes=[pltpu.VMEM((D // 2, 3 * HEAD), F32)],
+        scratch_shapes=[pltpu.VMEM((NBLK, BLOCK, 3 * HEAD), BF16)],
     )
     return pl.pallas_call(
         weight_kernel,
         grid_spec=grid_spec,
         out_shape=[jax.ShapeDtypeStruct(shape, BF16)] * 2,
-        name="weight_pass", compiler_params=pltpu.CompilerParams(vmem_limit_bytes=10 * 1024 * 1024),
-    )(meta, normed, part, came)
+        name="weight_pass",
+        compiler_params=pltpu.CompilerParams(vmem_limit_bytes=18 * 1024 * 1024),
+    )(meta, n_early, n_late, part, came)
 
 
 def join_kernel(meta, part, came, out):
@@ -353,7 +392,8 @@
         made += [down, up]
     far = ring(up[:HALF], "z", 1, 8)
     made.append(far)
-    made.append(ring(down[HALF:], "z", -1, 8))
+    far = ring(down[HALF:], "z", -1, 8)
+    made.append(far)
     return made
 
 
@@ -375,10 +415,11 @@
 
     pieces = relay(payload)
     others = [flip(piece, "core", 1, 2) for piece in pieces]
+    early, *made = early_pass(meta, pieces[:5] + others[:5], gain, w_head)
     do = lax.all_to_all(parts, ("z", "core"), 0, 0, tiled=True)
-    normed, mine, part = head_pass(meta, pieces, others, do, gain, w_head)
+    late, mine, part = head_pass(meta, pieces[5:] + others[5:], made, do, gain, w_head)
     came = flip(part, "core", 1, 2)
-    here, there = weight_pass(meta, normed, part, came)
+    here, there = weight_pass(meta, early, late, part, came)
     back = join_pass(meta, part, came)
     back = lax.all_to_all(back, "z", 0, 0, tiled=True)
 

time: 136 us -> 152 us (1.12)
  local copies, waits for them, and re-layouts: 8.77 us -> 23.2 us
  starting transfers between devices: 64.5 us -> 61.5 us
  Pallas kernels: 21 us -> 23.7 us
    unnamed x18 -> x62, local copies, waits for them, and re-layouts: 7.11 us -> 19.7 us
    ppermute x14, starting transfers between devices: 17.4 us -> 13.6 us  [flip(): return lax.ppermute(x, axis, [(i, i ^ bit) for i in range(size)])]
    pallas_call x1 -> x2, Pallas kernels: 12 us -> 15.7 us  [the longest x1 11.2 us: head_pass(): pl.pallas_call(head_kernel, grid_spec=pltpu.PrefetchScalarGridSpec(num_sc...]
    ppermute x14, waiting for transfers between devices: 14.9 us -> 17.9 us  [flip(): return lax.ppermute(x, axis, [(i, i ^ bit) for i in range(size)])]
  transfers between devices with their start and end apart: 31 -> 31, of which waited for: 14 -> 11; matrix products, arithmetic and copies ran while one was open for 2% -> 3% of each run, Pallas kernels for 4% -> 7%
where the time goes in v3:
time: 152 us; the launch traced here: 151 us
  starting transfers between devices  61.5 us (40%)
  waiting for transfers between devices  38.9 us (26%)
  Pallas kernels  23.7 us (16%)
  local copies, waits for them, and re-layouts  23.2 us (15%)
  other arithmetic  2.56 us (2%)
    ppermute x8, starting transfers between devices, turn(): return lax.ppermute(x, ('y_lo', 'z', 'core'), pairs)  25.9 us
    unnamed x62, local copies, waits for them, and re-layouts  19.7 us
    ppermute x14, waiting for transfers between devices, flip(): return lax.ppermute(x, axis, [(i, i ^ bit) for i in range(size)])  17.9 us
    ppermute x14, starting transfers between devices, flip(): return lax.ppermute(x, axis, [(i, i ^ bit) for i in range(size)])  13.6 us
    pallas_call x1, Pallas kernels, head_pass(): pl.pallas_call(head_kernel, grid_spec=pltpu.PrefetchScalarGridSpec(num_sc...  11.2 us
    ppermute x6, starting transfers between devices, ring(): return lax.ppermute(x, axis, [(i, (i + by) % size) for i in range(size)])  10.1 us
    ppermute x6, waiting for transfers between devices, ring(): return lax.ppermute(x, axis, [(i, (i + by) % size) for i in range(size)])  8.71 us
    ppermute x8, waiting for transfers between devices, turn(): return lax.ppermute(x, ('y_lo', 'z', 'core'), pairs)  8.14 us
  transfers between devices with their start and end apart: 31, of which 11 were waited for; matrix products, arithmetic and copies ran while one was open for 3% of the time, Pallas kernels for 7%

profile of v3, /device:TPU:1, one launch (start us, length us, event | category | flops | bytes accessed | tf_op | source)
XLA Modules:
  0.0 151.0 jit_solution(7246654137268576654)
XLA Ops:
  1.7 1.0 fusion.1
  2.7 8.0 %collective-permute-start.1 = (bf16[136,1024]{1,0:T(8,128)(2,1)S(1)}, bf16[136,1024]{1,0:T(8,128)(2,1)S(1)}, u32[]{:S(2)}, u32[]{:S(2)}) collective-permute-start(bf16[136,1024]{1,0:T(8,128)(2,1)S(1)} %fusion.1), channel_id=1, source_target_pairs={{0,112},{1,240},{16,0},{17,128},{32,16},{33,144},{48,32},{49,160},... | collective-permute-start | bytes 835592 | tf_op jit(solution)/shard_map/ppermute | solution.py:379
  10.7 6.0 %collective-permute-done.1.refs_2_ = bf16[136,1024]{1,0:T(8,128)(2,1)S(1)} collective-permute-done((bf16[136,1024]{1,0:T(8,128)(2,1)S(1)}, bf16[136,1024]{1,0:T(8,128)(2,1)S(1)}, u32[]{:S(2)}, u32[]{:S(2)}) %collective-permute-start.1) | collective-permute-done | bytes 278560 | tf_op jit(solution)/shard_map/ppermute | solution.py:379
  16.7 4.0 %collective-permute-start.2 = (bf16[136,1024]{1,0:T(8,128)(2,1)S(1)}, bf16[136,1024]{1,0:T(8,128)(2,1)S(1)}, u32[]{:S(2)}, u32[]{:S(2)}) collective-permute-start(bf16[136,1024]{1,0:T(8,128)(2,1)S(1)} %collective-permute-done.1.refs_2_), channel_id=1, source_target_pairs={{0,112},{16,0},{32,16},{48,32},{64,48},{80,64},{96,80},{112,96},{1... | collective-permute-start | bytes 835592 | tf_op jit(solution)/shard_map/ppermute | solution.py:370
  20.7 3.1 %collective-permute-start.13 = (bf16[136,1024]{1,0:T(8,128)(2,1)S(1)}, bf16[136,1024]{1,0:T(8,128)(2,1)S(1)}, u32[]{:S(2)}, u32[]{:S(2)}) collective-permute-start(bf16[136,1024]{1,0:T(8,128)(2,1)S(1)} %fusion.1), channel_id=1, source_target_pairs={{0,0},{1,128},{16,16},{17,144},{32,32},{33,160},{48,48},{49,176},{... | collective-permute-start | bytes 835592 | tf_op jit(solution)/shard_map/ppermute | solution.py:379
  23.9 3.2 %collective-permute-done.2.refs_4_ = bf16[136,1024]{1,0:T(8,128)(2,1)S(1)} collective-permute-done((bf16[136,1024]{1,0:T(8,128)(2,1)S(1)}, bf16[136,1024]{1,0:T(8,128)(2,1)S(1)}, u32[]{:S(2)}, u32[]{:S(2)}) %collective-permute-start.2) | collective-permute-done | bytes 278560 | tf_op jit(solution)/shard_map/ppermute | solution.py:370
  27.1 3.2 %collective-permute-start.3 = (bf16[136,1024]{1,0:T(8,128)(2,1)S(1)}, bf16[136,1024]{1,0:T(8,128)(2,1)}, u32[]{:S(2)}, u32[]{:S(2)}) collective-permute-start(bf16[136,1024]{1,0:T(8,128)(2,1)S(1)} %collective-permute-done.2.refs_4_), channel_id=1, source_target_pairs={{0,112},{16,0},{32,16},{48,32},{64,48},{80,64},{96,80},{112,96},{1... | collective-permute-start | bytes 835592 | tf_op jit(solution)/shard_map/ppermute | solution.py:370
  30.3 1.0 copy.9
  31.3 1.9 %collective-permute-start.19 = (bf16[16,64,128]{2,1,0:T(8,128)(2,1)S(1)}, bf16[16,64,128]{2,1,0:T(8,128)(2,1)}, u32[]{:S(2)}, u32[]{:S(2)}) collective-permute-start(bf16[16,64,128]{2,1,0:T(8,128)(2,1)S(1)} %bitcast.17), channel_id=1, source_target_pairs={{0,0},{1,128},{16,16},{17,144},{32,32},{33,160},{48,48},{49,176},{... | collective-permute-start | bytes 786440 | tf_op jit(solution)/shard_map/ppermute | solution.py:379
  33.4 3.6 %collective-permute-start = (s32[16]{0:T(128)}, s32[16]{0:T(128)S(1)}, u32[]{:S(2)}, u32[]{:S(2)}) collective-permute-start(s32[16]{0:T(128)} %bitcast.19), channel_id=1, source_target_pairs={{0,0},{1,128},{16,16},{17,144},{32,32},{33,160},{48,48},{49,176},{... | collective-permute-start | bytes 200 | tf_op jit(solution)/shard_map/ppermute | solution.py:379
  37.0 2.1 %collective-permute-done = s32[16]{0:T(128)S(1)} collective-permute-done((s32[16]{0:T(128)}, s32[16]{0:T(128)S(1)}, u32[]{:S(2)}, u32[]{:S(2)}) %collective-permute-start) | collective-permute-done | bytes 96 | tf_op jit(solution)/shard_map/ppermute | solution.py:379
  39.9 4.8 %all-to-all-start = ((bf16[16,64,128]{2,1,0:T(8,128)(2,1)}), bf16[16,64,128]{2,1,0:T(8,128)(2,1)}, u32[]{:S(2)}, u32[]{:S(2)}) async-start(bf16[16,64,128]{2,1,0:T(8,128)(2,1)} %collective-permute-done.19), calls=%async_computation | async-start | bytes 524288 | tf_op jit(solution)/shard_map/all_to_all | solution.py:419
  45.6 2.6 %collective-permute-start.8 = (bf16[72,1024]{1,0:T(8,128)(2,1)S(1)}, bf16[72,1024]{1,0:T(8,128)(2,1)}, u32[]{:S(2)}, u32[]{:S(2)}) collective-permute-start(bf16[72,1024]{1,0:T(8,128)(2,1)S(1)} %slice.9), channel_id=1, source_target_pairs={{0,112},{16,0},{32,16},{48,32},{64,48},{80,64},{96,80},{112,96},{1... | collective-permute-start | bytes 442376 | tf_op jit(solution)/shard_map/ppermute | solution.py:370
  49.0 1.0 collective-permute-start.10
  51.2 4.6 %collective-permute-done.8.refs_4_ = bf16[72,1024]{1,0:T(8,128)(2,1)} collective-permute-done((bf16[72,1024]{1,0:T(8,128)(2,1)S(1)}, bf16[72,1024]{1,0:T(8,128)(2,1)}, u32[]{:S(2)}, u32[]{:S(2)}) %collective-permute-start.8) | collective-permute-done | bytes 147488 | tf_op jit(solution)/shard_map/ppermute | solution.py:370
  55.8 1.0 collective-permute-start.12
  57.7 1.0 collective-permute-start.11
  58.7 1.2 constant_dynamic-slice_fusion
  61.0 1.0 copy-done.8
  62.0 1.0 copy-done.10
  63.0 1.0 copy-done.12
  63.9 1.0 copy-done.14
  64.9 1.0 copy-done.16
  65.8 1.0 copy-done.18
  66.8 1.0 copy-done.20
  68.7 4.5 %early_pass.1 = (bf16[10,128,1024]{2,1,0:T(8,128)(2,1)S(1)}, bf16[10,64,128]{2,1,0:T(8,128)(2,1)S(1)}, bf16[10,128,128]{2,1,0:T(8,128)(2,1)S(1)}, bf16[10,128,12...) custom-call(s32[20]{0:T(128)S(1)} %concatenate.6.refs_0_.meta, ...), custom_call_target="tpu_custom_call" | custom-call | tf_op jit(solution)/shard_map/early_pass/pallas_call | solution.py:83
  76.1 1.0 copy-done.2
  77.0 1.0 copy-done.4
  79.9 11.2 %head_pass.1 = (bf16[6,128,1024]{2,1,0:T(8,128)(2,1)S(1)}, bf16[128,1024]{1,0:T(8,128)(2,1)S(1)}, bf16[16,320,128]{2,1,0:T(8,128)(2,1)S(1)}) custom-call(s32[20]{0:T(128)S(1)} %concatenate.6.refs_0_.meta, bf16[136,1024]{1,0:T(8,128)(2,1)} %collective-permute-done.3.refs_1_, bf16[136,1024]{1,0:T(8,128)(2,1)} %collective-permute-done.6.refs_2_, ...), custom_call_target="tpu_custom_call" | custom-call | tf_op jit(solution)/shard_map/head_pass/pallas_call | solution.py:201
  91.1 2.9 %collective-permute-start.20 = (bf16[16,320,128]{2,1,0:T(8,128)(2,1)S(1)}, bf16[16,320,128]{2,1,0:T(8,128)(2,1)S(1)}, u32[]{:S(2)}, u32[]{:S(2)}) collective-permute-start(bf16[16,320,128]{2,1,0:T(8,128)(2,1)S(1)} %get-tuple-element.18.part), channel_id=1, source_target_pairs={{0,1},{1,0},{2,3},{3,2},{4,5},{5,4},{6,7},{7,6},{8,9},{9,8},{10,11... | collective-permute-start | bytes 3932168 | tf_op jit(solution)/shard_map/ppermute | solution.py:366
  94.0 2.7 %collective-permute-done.20.came = bf16[16,320,128]{2,1,0:T(8,128)(2,1)S(1)} collective-permute-done((bf16[16,320,128]{2,1,0:T(8,128)(2,1)S(1)}, bf16[16,320,128]{2,1,0:T(8,128)(2,1)S(1)}, u32[]{:S(2)}, u32[]{:S(2)}) %collective-permute-start.20) | collective-permute-done | bytes 1310752 | tf_op jit(solution)/shard_map/ppermute | solution.py:366
  96.7 2.0 %weight_pass.1 = (bf16[8,32,384]{2,1,0:T(8,128)(2,1)S(1)}, bf16[8,32,384]{2,1,0:T(8,128)(2,1)S(1)}) custom-call(s32[20]{0:T(128)S(1)} %concatenate.6.refs_0_.meta, bf16[10,128,1024]{2,1,0:T(8,128)(2,1)S(1)} %get-tuple-element.20.n_early, bf16[6,128,1024]{2,1,0:T(8,128)(2,1)S(1)} %get-tuple-element.21.n_late, ...), custom_call_target="tpu_custom_call" | custom-call | tf_op jit(solution)/shard_map/weight_pass/pallas_call | solution.py:268
  98.7 4.2 %collective-permute-start.22 = (bf16[8,32,384]{2,1,0:T(8,128)(2,1)S(1)}, bf16[8,32,384]{2,1,0:T(8,128)(2,1)S(1)}, u32[]{:S(2)}, u32[]{:S(2)}) collective-permute-start(bf16[8,32,384]{2,1,0:T(8,128)(2,1)S(1)} %get-tuple-element.22), channel_id=1, source_target_pairs={{0,0},{1,128},{16,16},{17,144},{32,32},{33,160},{48,48},{49,176},{... | collective-permute-start | bytes 589832 | tf_op jit(solution)/shard_map/ppermute | solution.py:379
  103.0 1.6 %join_pass.1 = bf16[8,384,128]{2,1,0:T(8,128)(2,1)} custom-call(s32[20]{0:T(128)S(1)} %concatenate.6.refs_0_.meta, bf16[16,320,128]{2,1,0:T(8,128)(2,1)S(1)} %get-tuple-element.18.part, bf16[16,320,128]{2,1,0:T(8,128)(2,1)S(1)} %collective-permute-done.20.came), custom_call_target="tpu_custom_call" | custom-call | tf_op jit(solution)/shard_map/join_pass/pallas_call | solution.py:295
  104.6 3.7 %all-to-all-start.1 = ((bf16[8,384,128]{2,1,0:T(8,128)(2,1)}), bf16[8,384,128]{2,1,0:T(8,128)(2,1)S(1)}, u32[]{:S(2)}, u32[]{:S(2)}) async-start(bf16[8,384,128]{2,1,0:T(8,128)(2,1)} %join_pass.1), calls=%async_computation.1 | async-start | bytes 1572864 | tf_op jit(solution)/shard_map/all_to_all | solution.py:424
  108.4 1.3 collective-permute-start.24
  109.7 4.5 %collective-permute-done.24 = bf16[8,32,384]{2,1,0:T(8,128)(2,1)S(1)} collective-permute-done((bf16[8,32,384]{2,1,0:T(8,128)(2,1)S(1)}, bf16[8,32,384]{2,1,0:T(8,128)(2,1)S(1)}, u32[]{:S(2)}, u32[]{:S(2)}) %collective-permute-start.24) | collective-permute-done | bytes 196640 | tf_op jit(solution)/shard_map/ppermute | solution.py:366
  114.3 6.3 %collective-permute-done.25 = bf16[8,32,384]{2,1,0:T(8,128)(2,1)S(1)} collective-permute-done((bf16[8,32,384]{2,1,0:T(8,128)(2,1)S(1)}, bf16[8,32,384]{2,1,0:T(8,128)(2,1)S(1)}, u32[]{:S(2)}, u32[]{:S(2)}) %collective-permute-start.25) | collective-permute-done | bytes 196640 | tf_op jit(solution)/shard_map/ppermute | solution.py:366
  120.7 2.8 %collective-permute-start.26 = (bf16[8,32,384]{2,1,0:T(8,128)(2,1)S(1)}, bf16[8,32,384]{2,1,0:T(8,128)(2,1)S(1)}, u32[]{:S(2)}, u32[]{:S(2)}) collective-permute-start(bf16[8,32,384]{2,1,0:T(8,128)(2,1)S(1)} %add_convert_fusion.1), channel_id=1, source_target_pairs={{0,2},{2,0},{1,3},{3,1},{4,6},{6,4},{5,7},{7,5},{8,10},{10,8},{9,1... | collective-permute-start | bytes 589832 | tf_op jit(solution)/shard_map/ppermute | solution.py:366
  123.5 3.3 %collective-permute-done.26 = bf16[8,32,384]{2,1,0:T(8,128)(2,1)S(1)} collective-permute-done((bf16[8,32,384]{2,1,0:T(8,128)(2,1)S(1)}, bf16[8,32,384]{2,1,0:T(8,128)(2,1)S(1)}, u32[]{:S(2)}, u32[]{:S(2)}) %collective-permute-start.26) | collective-permute-done | bytes 196640 | tf_op jit(solution)/shard_map/ppermute | solution.py:366
  127.5 4.2 %all-to-all-done.1.back = bf16[8,384,128]{2,1,0:T(8,128)(2,1)S(1)} async-done(((bf16[8,384,128]{2,1,0:T(8,128)(2,1)}), bf16[8,384,128]{2,1,0:T(8,128)(2,1)S(1)}, u32[]{:S(2)}, u32[]{:S(2)}) %all-to-all-start.1) | async-done | bytes 786464 | tf_op jit(solution)/shard_map/all_to_all | solution.py:424
  131.8 3.4 %all-to-all-start.2 = ((bf16[8,32,384]{2,1,0:T(8,128)(2,1)}), bf16[8,32,384]{2,1,0:T(8,128)(2,1)S(1)}, u32[]{:S(2)}, u32[]{:S(2)}) async-start(bf16[8,32,384]{2,1,0:T(8,128)(2,1)} %add_convert_fusion), calls=%async_computation.2 | async-start | bytes 393216 | tf_op jit(solution)/shard_map/all_to_all | solution.py:432
  135.2 2.8 %copy-done = bf16[1024,3072]{1,0:T(8,128)(2,1)S(1)} copy-done((bf16[1024,3072]{1,0:T(8,128)(2,1)S(1)}, bf16[1024,3072]{1,0:T(8,128)(2,1)}, u32[]{:S(2)}) %copy-start) | copy-done | bytes 6291480
  138.0 2.9 %rows_pass.1 = bf16[128,1024]{1,0:T(8,128)(2,1)S(1)} custom-call(bf16[8,384,128]{2,1,0:T(8,128)(2,1)S(1)} %all-to-all-done.1.back, bf16[128,1024]{1,0:T(8,128)(2,1)S(1)} %copy-done.26, f32[8,1024]{1,0:T(8,128)S(1)} %broadcast_in_dim.4.refs_11_.refs_15_.gain, bf16[1024,3072]{1,0:T(8,128)(2,1)S(1)} %copy-done), custom_call_target="tpu_custom_call" | custom-call | tf_op jit(solution)/shard_map/rows_pass/pallas_call | solution.py:323
  140.9 4.9 %collective-permute-start.21 = (bf16[128,1024]{1,0:T(8,128)(2,1)S(1)}, bf16[128,1024]{1,0:T(8,128)(2,1)S(1)}, u32[]{:S(2)}, u32[]{:S(2)}) collective-permute-start(bf16[128,1024]{1,0:T(8,128)(2,1)S(1)} %rows_pass.1), channel_id=1, source_target_pairs={{0,0},{1,128},{16,16},{17,144},{32,32},{33,160},{48,48},{49,176},{... | collective-permute-start | bytes 786440 | tf_op jit(solution)/shard_map/ppermute | solution.py:379
  145.9 1.9 %collective-permute-start.27 = (bf16[8,32,384]{2,1,0:T(8,128)(2,1)S(1)}, bf16[8,32,384]{2,1,0:T(8,128)(2,1)S(1)}, u32[]{:S(2)}, u32[]{:S(2)}) collective-permute-start(bf16[8,32,384]{2,1,0:T(8,128)(2,1)S(1)} %all-to-all-done.2.own), channel_id=1, source_target_pairs={{0,1},{1,0},{2,3},{3,2},{4,5},{5,4},{6,7},{7,6},{8,9},{9,8},{10,11... | collective-permute-start | bytes 589832 | tf_op jit(solution)/shard_map/ppermute | solution.py:366
  147.8 1.1 collective-permute-done.27.other
  148.8 1.5 final_pass.1
  (101 shorter events, 14.1 us)
Async XLA Ops:
  0.6 59.3 %copy-start.29 = (f32[1024]{0:T(1024)S(1)}, f32[1024]{0:T(1024)}, u32[]{:S(2)}) copy-start(f32[1024]{0:T(1024)} %param.9) | copy-start | bytes 12292
  2.7 14.1 %collective-permute-start.1 = (bf16[136,1024]{1,0:T(8,128)(2,1)S(1)}, bf16[136,1024]{1,0:T(8,128)(2,1)S(1)}, u32[]{:S(2)}, u32[]{:S(2)}) collective-permute-start(bf16[136,1024]{1,0:T(8,128)(2,1)S(1)} %fusion.1), channel_id=1, source_target_pairs={{0,112},{1,240},{16,0},{17,128},{32,16},{33,144},{48,32},{49,160},... | collective-permute-start | bytes 835592 | tf_op jit(solution)/shard_map/ppermute | solution.py:379
  10.7 13.1 %collective-permute-start.4 = (bf16[136,1024]{1,0:T(8,128)(2,1)S(1)}, bf16[136,1024]{1,0:T(8,128)(2,1)S(1)}, u32[]{:S(2)}, u32[]{:S(2)}) collective-permute-start(bf16[136,1024]{1,0:T(8,128)(2,1)S(1)} %fusion.1), channel_id=1, source_target_pairs={{0,16},{1,144},{16,32},{17,160},{32,48},{33,176},{48,64},{49,192},... | collective-permute-start | bytes 835592 | tf_op jit(solution)/shard_map/ppermute | solution.py:379
  16.7 43.2 %copy-start.5 = (bf16[136,1024]{1,0:T(8,128)(2,1)}, bf16[136,1024]{1,0:T(8,128)(2,1)S(1)}, u32[]{:S(2)}) copy-start(bf16[136,1024]{1,0:T(8,128)(2,1)S(1)} %collective-permute-done.1.refs_2_) | copy-start | bytes 835588
  16.7 10.3 %collective-permute-start.2 = (bf16[136,1024]{1,0:T(8,128)(2,1)S(1)}, bf16[136,1024]{1,0:T(8,128)(2,1)S(1)}, u32[]{:S(2)}, u32[]{:S(2)}) collective-permute-start(bf16[136,1024]{1,0:T(8,128)(2,1)S(1)} %collective-permute-done.1.refs_2_), channel_id=1, source_target_pairs={{0,112},{16,0},{32,16},{48,32},{64,48},{80,64},{96,80},{112,96},{1... | collective-permute-start | bytes 835592 | tf_op jit(solution)/shard_map/ppermute | solution.py:370
  20.7 12.5 %collective-permute-start.13 = (bf16[136,1024]{1,0:T(8,128)(2,1)S(1)}, bf16[136,1024]{1,0:T(8,128)(2,1)S(1)}, u32[]{:S(2)}, u32[]{:S(2)}) collective-permute-start(bf16[136,1024]{1,0:T(8,128)(2,1)S(1)} %fusion.1), channel_id=1, source_target_pairs={{0,0},{1,128},{16,16},{17,144},{32,32},{33,160},{48,48},{49,176},{... | collective-permute-start | bytes 835592 | tf_op jit(solution)/shard_map/ppermute | solution.py:379
  23.8 36.2 %copy-start.7 = (bf16[136,1024]{1,0:T(8,128)(2,1)}, bf16[136,1024]{1,0:T(8,128)(2,1)S(1)}, u32[]{:S(2)}) copy-start(bf16[136,1024]{1,0:T(8,128)(2,1)S(1)} %collective-permute-done.4.refs_3_) | copy-start | bytes 835588
  23.8 15.3 %collective-permute-start.5 = (bf16[136,1024]{1,0:T(8,128)(2,1)S(1)}, bf16[136,1024]{1,0:T(8,128)(2,1)S(1)}, u32[]{:S(2)}, u32[]{:S(2)}) collective-permute-start(bf16[136,1024]{1,0:T(8,128)(2,1)S(1)} %collective-permute-done.4.refs_3_), channel_id=1, source_target_pairs={{0,16},{16,32},{32,48},{48,64},{64,80},{80,96},{96,112},{112,0},{1... | collective-permute-start | bytes 835592 | tf_op jit(solution)/shard_map/ppermute | solution.py:370
  27.1 32.9 %copy-start.9 = (bf16[136,1024]{1,0:T(8,128)(2,1)}, bf16[136,1024]{1,0:T(8,128)(2,1)S(1)}, u32[]{:S(2)}) copy-start(bf16[136,1024]{1,0:T(8,128)(2,1)S(1)} %collective-permute-done.2.refs_4_) | copy-start | bytes 835588
  27.1 12.7 %collective-permute-start.3 = (bf16[136,1024]{1,0:T(8,128)(2,1)S(1)}, bf16[136,1024]{1,0:T(8,128)(2,1)}, u32[]{:S(2)}, u32[]{:S(2)}) collective-permute-start(bf16[136,1024]{1,0:T(8,128)(2,1)S(1)} %collective-permute-done.2.refs_4_), channel_id=1, source_target_pairs={{0,112},{16,0},{32,16},{48,32},{64,48},{80,64},{96,80},{112,96},{1... | collective-permute-start | bytes 835592 | tf_op jit(solution)/shard_map/ppermute | solution.py:370
  31.3 7.9 %collective-permute-start.19 = (bf16[16,64,128]{2,1,0:T(8,128)(2,1)S(1)}, bf16[16,64,128]{2,1,0:T(8,128)(2,1)}, u32[]{:S(2)}, u32[]{:S(2)}) collective-permute-start(bf16[16,64,128]{2,1,0:T(8,128)(2,1)S(1)} %bitcast.17), channel_id=1, source_target_pairs={{0,0},{1,128},{16,16},{17,144},{32,32},{33,160},{48,48},{49,176},{... | collective-permute-start | bytes 786440 | tf_op jit(solution)/shard_map/ppermute | solution.py:379
  33.3 26.7 %copy-start.11 = (bf16[136,1024]{1,0:T(8,128)(2,1)}, bf16[136,1024]{1,0:T(8,128)(2,1)S(1)}, u32[]{:S(2)}) copy-start(bf16[136,1024]{1,0:T(8,128)(2,1)S(1)} %collective-permute-done.13.refs_1_) | copy-start | bytes 835588
  33.3 12.3 %collective-permute-start.14 = (bf16[136,1024]{1,0:T(8,128)(2,1)S(1)}, bf16[136,1024]{1,0:T(8,128)(2,1)S(1)}, u32[]{:S(2)}, u32[]{:S(2)}) collective-permute-start(bf16[136,1024]{1,0:T(8,128)(2,1)S(1)} %collective-permute-done.13.refs_1_), channel_id=1, source_target_pairs={{0,1},{1,0},{2,3},{3,2},{4,5},{5,4},{6,7},{7,6},{8,9},{9,8},{10,11... | collective-permute-start | bytes 835592 | tf_op jit(solution)/shard_map/ppermute | solution.py:366
  33.4 5.7 %collective-permute-start = (s32[16]{0:T(128)}, s32[16]{0:T(128)S(1)}, u32[]{:S(2)}, u32[]{:S(2)}) collective-permute-start(s32[16]{0:T(128)} %bitcast.19), channel_id=1, source_target_pairs={{0,0},{1,128},{16,16},{17,144},{32,32},{33,160},{48,48},{49,176},{... | collective-permute-start | bytes 200 | tf_op jit(solution)/shard_map/ppermute | solution.py:379
  39.1 9.2 %collective-permute-start.16 = (bf16[136,1024]{1,0:T(8,128)(2,1)S(1)}, bf16[136,1024]{1,0:T(8,128)(2,1)S(1)}, u32[]{:S(2)}, u32[]{:S(2)}) collective-permute-start(bf16[136,1024]{1,0:T(8,128)(2,1)S(1)} %collective-permute-done.4.refs_3_), channel_id=1, source_target_pairs={{0,1},{1,0},{2,3},{3,2},{4,5},{5,4},{6,7},{7,6},{8,9},{9,8},{10,11... | collective-permute-start | bytes 835592 | tf_op jit(solution)/shard_map/ppermute | solution.py:366
  39.1 20.9 %copy-start.13 = (bf16[136,1024]{1,0:T(8,128)(2,1)}, bf16[136,1024]{1,0:T(8,128)(2,1)S(1)}, u32[]{:S(2)}) copy-start(bf16[136,1024]{1,0:T(8,128)(2,1)S(1)} %collective-permute-done.5.refs_5_) | copy-start | bytes 835588
  39.2 9.8 %collective-permute-start.6 = (bf16[136,1024]{1,0:T(8,128)(2,1)S(1)}, bf16[136,1024]{1,0:T(8,128)(2,1)}, u32[]{:S(2)}, u32[]{:S(2)}) collective-permute-start(bf16[136,1024]{1,0:T(8,128)(2,1)S(1)} %collective-permute-done.5.refs_5_), channel_id=1, source_target_pairs={{0,16},{16,32},{32,48},{48,64},{64,80},{80,96},{96,112},{112,0},{1... | collective-permute-start | bytes 835592 | tf_op jit(solution)/shard_map/ppermute | solution.py:370
  39.3 10.8 %collective-permute-start.15 = (bf16[136,1024]{1,0:T(8,128)(2,1)S(1)}, bf16[136,1024]{1,0:T(8,128)(2,1)S(1)}, u32[]{:S(2)}, u32[]{:S(2)}) collective-permute-start(bf16[136,1024]{1,0:T(8,128)(2,1)S(1)} %collective-permute-done.1.refs_2_), channel_id=1, source_target_pairs={{0,1},{1,0},{2,3},{3,2},{4,5},{5,4},{6,7},{7,6},{8,9},{9,8},{10,11... | collective-permute-start | bytes 835592 | tf_op jit(solution)/shard_map/ppermute | solution.py:366
  39.8 11.3 %collective-permute-start.18 = (bf16[136,1024]{1,0:T(8,128)(2,1)S(1)}, bf16[136,1024]{1,0:T(8,128)(2,1)S(1)}, u32[]{:S(2)}, u32[]{:S(2)}) collective-permute-start(bf16[136,1024]{1,0:T(8,128)(2,1)S(1)} %collective-permute-done.5.refs_5_), channel_id=1, source_target_pairs={{0,1},{1,0},{2,3},{3,2},{4,5},{5,4},{6,7},{7,6},{8,9},{9,8},{10,11... | collective-permute-start | bytes 835592 | tf_op jit(solution)/shard_map/ppermute | solution.py:366
  39.9 36.2 %all-to-all-start = ((bf16[16,64,128]{2,1,0:T(8,128)(2,1)}), bf16[16,64,128]{2,1,0:T(8,128)(2,1)}, u32[]{:S(2)}, u32[]{:S(2)}) async-start(bf16[16,64,128]{2,1,0:T(8,128)(2,1)} %collective-permute-done.19), calls=%async_computation | async-start | bytes 524288 | tf_op jit(solution)/shard_map/all_to_all | solution.py:419
  45.6 14.4 %copy-start.15 = (bf16[136,1024]{1,0:T(8,128)(2,1)}, bf16[136,1024]{1,0:T(8,128)(2,1)S(1)}, u32[]{:S(2)}) copy-start(bf16[136,1024]{1,0:T(8,128)(2,1)S(1)} %collective-permute-done.14.refs_6_) | copy-start | bytes 835588
  45.6 10.2 %collective-permute-start.8 = (bf16[72,1024]{1,0:T(8,128)(2,1)S(1)}, bf16[72,1024]{1,0:T(8,128)(2,1)}, u32[]{:S(2)}, u32[]{:S(2)}) collective-permute-start(bf16[72,1024]{1,0:T(8,128)(2,1)S(1)} %slice.9), channel_id=1, source_target_pairs={{0,112},{16,0},{32,16},{48,32},{64,48},{80,64},{96,80},{112,96},{1... | collective-permute-start | bytes 442376 | tf_op jit(solution)/shard_map/ppermute | solution.py:370
  48.3 11.8 %copy-start.17 = (bf16[136,1024]{1,0:T(8,128)(2,1)}, bf16[136,1024]{1,0:T(8,128)(2,1)S(1)}, u32[]{:S(2)}) copy-start(bf16[136,1024]{1,0:T(8,128)(2,1)S(1)} %collective-permute-done.16.refs_8_) | copy-start | bytes 835588
  48.3 11.7 %collective-permute-start.17 = (bf16[136,1024]{1,0:T(8,128)(2,1)S(1)}, bf16[136,1024]{1,0:T(8,128)(2,1)}, u32[]{:S(2)}, u32[]{:S(2)}) collective-permute-start(bf16[136,1024]{1,0:T(8,128)(2,1)S(1)} %collective-permute-done.2.refs_4_), channel_id=1, source_target_pairs={{0,1},{1,0},{2,3},{3,2},{4,5},{5,4},{6,7},{7,6},{8,9},{9,8},{10,11... | collective-permute-start | bytes 835592 | tf_op jit(solution)/shard_map/ppermute | solution.py:366
  49.0 27.1 %collective-permute-start.10 = (bf16[136,1024]{1,0:T(8,128)(2,1)}, bf16[136,1024]{1,0:T(8,128)(2,1)}, u32[]{:S(2)}, u32[]{:S(2)}) collective-permute-start(bf16[136,1024]{1,0:T(8,128)(2,1)} %collective-permute-done.6.refs_2_), channel_id=1, source_target_pairs={{0,1},{1,0},{2,3},{3,2},{4,5},{5,4},{6,7},{7,6},{8,9},{9,8},{10,11... | collective-permute-start | bytes 835592 | tf_op jit(solution)/shard_map/ppermute | solution.py:366
  50.0 10.0 %copy-start.19 = (bf16[136,1024]{1,0:T(8,128)(2,1)}, bf16[136,1024]{1,0:T(8,128)(2,1)S(1)}, u32[]{:S(2)}) copy-start(bf16[136,1024]{1,0:T(8,128)(2,1)S(1)} %collective-permute-done.15.refs_7_) | copy-start | bytes 835588
  50.0 26.0 %collective-permute-start.9 = (bf16[136,1024]{1,0:T(8,128)(2,1)}, bf16[136,1024]{1,0:T(8,128)(2,1)}, u32[]{:S(2)}, u32[]{:S(2)}) collective-permute-start(bf16[136,1024]{1,0:T(8,128)(2,1)} %collective-permute-done.3.refs_1_), channel_id=1, source_target_pairs={{0,1},{1,0},{2,3},{3,2},{4,5},{5,4},{6,7},{7,6},{8,9},{9,8},{10,11... | collective-permute-start | bytes 835592 | tf_op jit(solution)/shard_map/ppermute | solution.py:366
  51.1 9.0 %copy-start.21 = (bf16[136,1024]{1,0:T(8,128)(2,1)}, bf16[136,1024]{1,0:T(8,128)(2,1)S(1)}, u32[]{:S(2)}) copy-start(bf16[136,1024]{1,0:T(8,128)(2,1)S(1)} %collective-permute-done.18.refs_10_) | copy-start | bytes 835588
  51.1 6.6 %collective-permute-start.7 = (bf16[64,1024]{1,0:T(8,128)(2,1)S(1)}, bf16[64,1024]{1,0:T(8,128)(2,1)}, u32[]{:S(2)}, u32[]{:S(2)}) collective-permute-start(bf16[64,1024]{1,0:T(8,128)(2,1)S(1)} %slice.8), channel_id=1, source_target_pairs={{0,16},{16,32},{32,48},{48,64},{64,80},{80,96},{96,112},{112,0},{1... | collective-permute-start | bytes 393224 | tf_op jit(solution)/shard_map/ppermute | solution.py:370
  55.8 20.2 %collective-permute-start.12 = (bf16[72,1024]{1,0:T(8,128)(2,1)}, bf16[72,1024]{1,0:T(8,128)(2,1)}, u32[]{:S(2)}, u32[]{:S(2)}) collective-permute-start(bf16[72,1024]{1,0:T(8,128)(2,1)} %collective-permute-done.8.refs_4_), channel_id=1, source_target_pairs={{0,1},{1,0},{2,3},{3,2},{4,5},{5,4},{6,7},{7,6},{8,9},{9,8},{10,11... | collective-permute-start | bytes 442376 | tf_op jit(solution)/shard_map/ppermute | solution.py:366
  57.7 18.4 %collective-permute-start.11 = (bf16[64,1024]{1,0:T(8,128)(2,1)}, bf16[64,1024]{1,0:T(8,128)(2,1)}, u32[]{:S(2)}, u32[]{:S(2)}) collective-permute-start(bf16[64,1024]{1,0:T(8,128)(2,1)} %collective-permute-done.7.refs_3_), channel_id=1, source_target_pairs={{0,1},{1,0},{2,3},{3,2},{4,5},{5,4},{6,7},{7,6},{8,9},{9,8},{10,11... | collective-permute-start | bytes 393224 | tf_op jit(solution)/shard_map/ppermute | solution.py:366
  60.1 1.0 copy-start.6
  61.0 1.0 copy-start.8
  76.1 1.0 copy-start.2
  77.0 1.0 copy-start.4
  91.1 7.6 %copy-start.25 = (bf16[128,1024]{1,0:T(8,128)(2,1)}, bf16[128,1024]{1,0:T(8,128)(2,1)S(1)}, u32[]{:S(2)}) copy-start(bf16[128,1024]{1,0:T(8,128)(2,1)S(1)} %get-tuple-element.19.mine) | copy-start | bytes 786436
  91.1 5.6 %collective-permute-start.20 = (bf16[16,320,128]{2,1,0:T(8,128)(2,1)S(1)}, bf16[16,320,128]{2,1,0:T(8,128)(2,1)S(1)}, u32[]{:S(2)}, u32[]{:S(2)}) collective-permute-start(bf16[16,320,128]{2,1,0:T(8,128)(2,1)S(1)} %get-tuple-element.18.part), channel_id=1, source_target_pairs={{0,1},{1,0},{2,3},{3,2},{4,5},{5,4},{6,7},{7,6},{8,9},{9,8},{10,11... | collective-permute-start | bytes 3932168 | tf_op jit(solution)/shard_map/ppermute | solution.py:366
  98.7 9.6 %collective-permute-start.22 = (bf16[8,32,384]{2,1,0:T(8,128)(2,1)S(1)}, bf16[8,32,384]{2,1,0:T(8,128)(2,1)S(1)}, u32[]{:S(2)}, u32[]{:S(2)}) collective-permute-start(bf16[8,32,384]{2,1,0:T(8,128)(2,1)S(1)} %get-tuple-element.22), channel_id=1, source_target_pairs={{0,0},{1,128},{16,16},{17,144},{32,32},{33,160},{48,48},{49,176},{... | collective-permute-start | bytes 589832 | tf_op jit(solution)/shard_map/ppermute | solution.py:379
  102.9 5.4 %collective-permute-start.23 = (bf16[8,32,384]{2,1,0:T(8,128)(2,1)S(1)}, bf16[8,32,384]{2,1,0:T(8,128)(2,1)S(1)}, u32[]{:S(2)}, u32[]{:S(2)}) collective-permute-start(bf16[8,32,384]{2,1,0:T(8,128)(2,1)S(1)} %get-tuple-element.23), channel_id=1, source_target_pairs={{0,1},{1,129},{16,17},{17,145},{32,33},{33,161},{48,49},{49,177},{... | collective-permute-start | bytes 589832 | tf_op jit(solution)/shard_map/ppermute | solution.py:379
  104.6 30.6 %copy-start.26 = (bf16[128,1024]{1,0:T(8,128)(2,1)S(1)}, bf16[128,1024]{1,0:T(8,128)(2,1)}, u32[]{:S(2)}) copy-start(bf16[128,1024]{1,0:T(8,128)(2,1)} %copy-done.25) | copy-start | bytes 786436
  104.6 27.2 %all-to-all-start.1 = ((bf16[8,384,128]{2,1,0:T(8,128)(2,1)}), bf16[8,384,128]{2,1,0:T(8,128)(2,1)S(1)}, u32[]{:S(2)}, u32[]{:S(2)}) async-start(bf16[8,384,128]{2,1,0:T(8,128)(2,1)} %join_pass.1), calls=%async_computation.1 | async-start | bytes 1572864 | tf_op jit(solution)/shard_map/all_to_all | solution.py:424
  108.4 5.8 %collective-permute-start.24 = (bf16[8,32,384]{2,1,0:T(8,128)(2,1)S(1)}, bf16[8,32,384]{2,1,0:T(8,128)(2,1)S(1)}, u32[]{:S(2)}, u32[]{:S(2)}) collective-permute-start(bf16[8,32,384]{2,1,0:T(8,128)(2,1)S(1)} %add_convert_fusion.3), channel_id=1, source_target_pairs={{0,4},{4,0},{8,12},{12,8},{1,5},{5,1},{9,13},{13,9},{2,6},{6,2},{1... | collective-permute-start | bytes 589832 | tf_op jit(solution)/shard_map/ppermute | solution.py:366
  114.2 6.4 %collective-permute-start.25 = (bf16[8,32,384]{2,1,0:T(8,128)(2,1)S(1)}, bf16[8,32,384]{2,1,0:T(8,128)(2,1)S(1)}, u32[]{:S(2)}, u32[]{:S(2)}) collective-permute-start(bf16[8,32,384]{2,1,0:T(8,128)(2,1)S(1)} %add_convert_fusion.2), channel_id=1, source_target_pairs={{0,8},{4,12},{8,0},{12,4},{1,9},{5,13},{9,1},{13,5},{2,10},{6,14},... | collective-permute-start | bytes 589832 | tf_op jit(solution)/shard_map/ppermute | solution.py:366
  120.7 6.1 %collective-permute-start.26 = (bf16[8,32,384]{2,1,0:T(8,128)(2,1)S(1)}, bf16[8,32,384]{2,1,0:T(8,128)(2,1)S(1)}, u32[]{:S(2)}, u32[]{:S(2)}) collective-permute-start(bf16[8,32,384]{2,1,0:T(8,128)(2,1)S(1)} %add_convert_fusion.1), channel_id=1, source_target_pairs={{0,2},{2,0},{1,3},{3,1},{4,6},{6,4},{5,7},{7,5},{8,10},{10,8},{9,1... | collective-permute-start | bytes 589832 | tf_op jit(solution)/shard_map/ppermute | solution.py:366
  131.8 14.1 %all-to-all-start.2 = ((bf16[8,32,384]{2,1,0:T(8,128)(2,1)}), bf16[8,32,384]{2,1,0:T(8,128)(2,1)S(1)}, u32[]{:S(2)}, u32[]{:S(2)}) async-start(bf16[8,32,384]{2,1,0:T(8,128)(2,1)} %add_convert_fusion), calls=%async_computation.2 | async-start | bytes 393216 | tf_op jit(solution)/shard_map/all_to_all | solution.py:432
  135.2 2.8 %copy-start = (bf16[1024,3072]{1,0:T(8,128)(2,1)S(1)}, bf16[1024,3072]{1,0:T(8,128)(2,1)}, u32[]{:S(2)}) copy-start(bf16[1024,3072]{1,0:T(8,128)(2,1)} %w.1) | copy-start | bytes 18874372
  140.9 9.4 %collective-permute-start.21 = (bf16[128,1024]{1,0:T(8,128)(2,1)S(1)}, bf16[128,1024]{1,0:T(8,128)(2,1)S(1)}, u32[]{:S(2)}, u32[]{:S(2)}) collective-permute-start(bf16[128,1024]{1,0:T(8,128)(2,1)S(1)} %rows_pass.1), channel_id=1, source_target_pairs={{0,0},{1,128},{16,16},{17,144},{32,32},{33,160},{48,48},{49,176},{... | collective-permute-start | bytes 786440 | tf_op jit(solution)/shard_map/ppermute | solution.py:379
  145.9 3.0 %collective-permute-start.27 = (bf16[8,32,384]{2,1,0:T(8,128)(2,1)S(1)}, bf16[8,32,384]{2,1,0:T(8,128)(2,1)S(1)}, u32[]{:S(2)}, u32[]{:S(2)}) collective-permute-start(bf16[8,32,384]{2,1,0:T(8,128)(2,1)S(1)} %all-to-all-done.2.own), channel_id=1, source_target_pairs={{0,1},{1,0},{2,3},{3,2},{4,5},{5,4},{6,7},{7,6},{8,9},{9,8},{10,11... | collective-permute-start | bytes 589832 | tf_op jit(solution)/shard_map/ppermute | solution.py:366
  (13 other events, 11.4 us)

commit v4 on v3

--- a/solution.py
+++ b/solution.py
@@ -92,7 +92,7 @@
         ),
         out_shape=[jax.ShapeDtypeStruct(x, t) for x, t in made],
         name="early_pass",
-        compiler_params=pltpu.CompilerParams(vmem_limit_bytes=20 * 1024 * 1024),
+        compiler_params=pltpu.CompilerParams(vmem_limit_bytes=58 * 1024 * 1024),
     )(meta, *pieces, gain, *w_head)
 
 
@@ -125,10 +125,11 @@
             docs[b // 4] += info_i[n]
         raw = []
         for c in range(2):
-            down, up, top, low = pieces[c * 4 : c * 4 + 4]
+            down, up, first, second = pieces[c * 4 : c * 4 + 4]
+            far = jnp.where(half == c, first[...], second[...])
             raw.append((down[0:BLOCK, :], down[BLOCK : BLOCK + EXTRA, 0:QROWS]))
             raw.append((up[0:BLOCK, :], up[BLOCK : BLOCK + EXTRA, 0:QROWS]))
-            raw.append((jnp.concatenate([top[...], low[0:HALF, :]], axis=0), low[HALF : HALF + EXTRA, 0:QROWS]))
+            raw.append((far[0:BLOCK, :], far[BLOCK : BLOCK + EXTRA, 0:QROWS]))
         target = meta[half * 8 + meta[NBLK]]
         for n in range(0, 6, 2):
             rows = jnp.concatenate([raw[n][0], raw[n + 1][0]], axis=0)
@@ -220,7 +221,7 @@
         ),
         out_shape=[jax.ShapeDtypeStruct(x, BF16) for x in outs],
         name="head_pass",
-        compiler_params=pltpu.CompilerParams(vmem_limit_bytes=26 * 1024 * 1024),
+        compiler_params=pltpu.CompilerParams(vmem_limit_bytes=58 * 1024 * 1024),
     )(meta, *given)
 
 
@@ -390,10 +391,8 @@
     for _ in range(2):
         down, up = ring(down, "z", -1, 8), ring(up, "z", 1, 8)
         made += [down, up]
-    far = ring(up[:HALF], "z", 1, 8)
-    made.append(far)
-    far = ring(down[HALF:], "z", -1, 8)
-    made.append(far)
+    made.append(lax.ppermute(up, ("z", "core"), [(2 * n, 2 * ((n + 1) % 8)) for n in range(8)]))
+    made.append(lax.ppermute(down, ("z", "core"), [(2 * n + 1, 2 * ((n + 7) % 8) + 1) for n in range(8)]))
     return made
 
 
@@ -414,7 +413,9 @@
     w_head = [lax.dynamic_slice_in_dim(w_qkv, n * D + z * HEAD, HEAD, 1) for n in range(3)]
 
     pieces = relay(payload)
-    others = [flip(piece, "core", 1, 2) for piece in pieces]
+    others = [flip(piece, "core", 1, 2) for piece in pieces[:7]]
+    others.append(lax.ppermute(pieces[7], "core", [(0, 1)]))
+    others.append(lax.ppermute(pieces[8], "core", [(1, 0)]))
     early, *made = early_pass(meta, pieces[:5] + others[:5], gain, w_head)
     do = lax.all_to_all(parts, ("z", "core"), 0, 0, tiled=True)
     late, mine, part = head_pass(meta, pieces[5:] + others[5:], made, do, gain, w_head)

time: 152 us -> 148 us (0.974)
  local copies, waits for them, and re-layouts: 23.2 us -> 11.5 us
  starting transfers between devices: 61.5 us -> 68.1 us
  Pallas kernels: 23.7 us -> 29.4 us
  waiting for transfers between devices: 38.9 us -> 34.6 us
    unnamed x62 -> x42, local copies, waits for them, and re-layouts: 19.7 us -> 7.92 us
    ppermute x0 -> x4, starting transfers between devices: none -> 9.31 us  [the longest x1 4.46 us: work(): others.append(lax.ppermute(pieces[8], 'core', [(1, 0)]))]
    ppermute x6 -> x4, starting transfers between devices: 10.1 us -> 5.33 us  [ring(): return lax.ppermute(x, axis, [(i, (i + by) % size) for i in range(size)])]
    ppermute x14 -> x12, starting transfers between devices: 13.6 us -> 10.3 us  [flip(): return lax.ppermute(x, axis, [(i, i ^ bit) for i in range(size)])]
    all_to_all x1, starting transfers between devices: 3.68 us -> 6.96 us  [work(): back = lax.all_to_all(back, 'z', 0, 0, tiled=True)]
    pallas_call x1, Pallas kernels: 4.52 us -> 7.52 us  [early_pass(): pl.pallas_call(early_kernel, grid_spec=pltpu.PrefetchScalarGridSpec(num_s...]
    pallas_call x1, Pallas kernels: 11.2 us -> 13.9 us  [head_pass(): pl.pallas_call(head_kernel, grid_spec=pltpu.PrefetchScalarGridSpec(num_sc...]
    ppermute x6 -> x4, waiting for transfers between devices: 8.71 us -> 6.38 us  [ring(): return lax.ppermute(x, axis, [(i, (i + by) % size) for i in range(size)])]
  transfers between devices with their start and end apart: 31 -> 31, of which waited for: 11 -> 11; matrix products, arithmetic and copies ran while one was open for 3% -> 3% of each run, Pallas kernels for 7% -> 9%
where the time goes in v4:
time: 148 us; the launch traced here: 147 us
  starting transfers between devices  68.1 us (46%)
  waiting for transfers between devices  34.6 us (23%)
  Pallas kernels  29.4 us (20%)
  local copies, waits for them, and re-layouts  11.5 us (8%)
  other arithmetic  2.55 us (2%)
    ppermute x8, starting transfers between devices, turn(): return lax.ppermute(x, ('y_lo', 'z', 'core'), pairs)  25.8 us
    ppermute x12, waiting for transfers between devices, flip(): return lax.ppermute(x, axis, [(i, i ^ bit) for i in range(size)])  15.7 us
    pallas_call x1, Pallas kernels, head_pass(): pl.pallas_call(head_kernel, grid_spec=pltpu.PrefetchScalarGridSpec(num_sc...  13.9 us
    ppermute x12, starting transfers between devices, flip(): return lax.ppermute(x, axis, [(i, i ^ bit) for i in range(size)])  10.3 us
    ppermute x8, waiting for transfers between devices, turn(): return lax.ppermute(x, ('y_lo', 'z', 'core'), pairs)  8.11 us
    unnamed x42, local copies, waits for them, and re-layouts  7.92 us
    pallas_call x1, Pallas kernels, early_pass(): pl.pallas_call(early_kernel, grid_spec=pltpu.PrefetchScalarGridSpec(num_s...  7.52 us
    all_to_all x1, starting transfers between devices, work(): do = lax.all_to_all(parts, ('z', 'core'), 0, 0, tiled=True)  7.07 us
  transfers between devices with their start and end apart: 31, of which 11 were waited for; matrix products, arithmetic and copies ran while one was open for 3% of the time, Pallas kernels for 9%

profile of v4, /device:TPU:1, one launch (start us, length us, event | category | flops | bytes accessed | tf_op | source)
XLA Modules:
  0.0 147.2 jit_solution(6035779393040300646)
XLA Ops:
  0.7 0.7 convert_reduce_fusion
  1.7 1.0 fusion.1
  2.7 4.1 %collective-permute-start.4 = (bf16[136,1024]{1,0:T(8,128)(2,1)S(1)}, bf16[136,1024]{1,0:T(8,128)(2,1)S(1)}, u32[]{:S(2)}, u32[]{:S(2)}) collective-permute-start(bf16[136,1024]{1,0:T(8,128)(2,1)S(1)} %fusion.1), channel_id=1, source_target_pairs={{0,16},{1,144},{16,32},{17,160},{32,48},{33,176},{48,64},{49,192},... | collective-permute-start | bytes 835592 | tf_op jit(solution)/shard_map/ppermute | solution.py:380
  6.8 4.0 %collective-permute-start.1 = (bf16[136,1024]{1,0:T(8,128)(2,1)S(1)}, bf16[136,1024]{1,0:T(8,128)(2,1)S(1)}, u32[]{:S(2)}, u32[]{:S(2)}) collective-permute-start(bf16[136,1024]{1,0:T(8,128)(2,1)S(1)} %fusion.1), channel_id=1, source_target_pairs={{0,112},{1,240},{16,0},{17,128},{32,16},{33,144},{48,32},{49,160},... | collective-permute-start | bytes 835592 | tf_op jit(solution)/shard_map/ppermute | solution.py:380
  10.8 1.9 %collective-permute-start.13 = (bf16[136,1024]{1,0:T(8,128)(2,1)S(1)}, bf16[136,1024]{1,0:T(8,128)(2,1)S(1)}, u32[]{:S(2)}, u32[]{:S(2)}) collective-permute-start(bf16[136,1024]{1,0:T(8,128)(2,1)S(1)} %fusion.1), channel_id=1, source_target_pairs={{0,0},{1,128},{16,16},{17,144},{32,32},{33,160},{48,48},{49,176},{... | collective-permute-start | bytes 835592 | tf_op jit(solution)/shard_map/ppermute | solution.py:380
  12.7 4.7 %collective-permute-done.4.refs_3_ = bf16[136,1024]{1,0:T(8,128)(2,1)S(1)} collective-permute-done((bf16[136,1024]{1,0:T(8,128)(2,1)S(1)}, bf16[136,1024]{1,0:T(8,128)(2,1)S(1)}, u32[]{:S(2)}, u32[]{:S(2)}) %collective-permute-start.4) | collective-permute-done | bytes 278560 | tf_op jit(solution)/shard_map/ppermute | solution.py:380
  17.4 2.7 %collective-permute-start.2 = (bf16[136,1024]{1,0:T(8,128)(2,1)S(1)}, bf16[136,1024]{1,0:T(8,128)(2,1)S(1)}, u32[]{:S(2)}, u32[]{:S(2)}) collective-permute-start(bf16[136,1024]{1,0:T(8,128)(2,1)S(1)} %collective-permute-done.1.refs_2_), channel_id=1, source_target_pairs={{0,112},{16,0},{32,16},{48,32},{64,48},{80,64},{96,80},{112,96},{1... | collective-permute-start | bytes 835592 | tf_op jit(solution)/shard_map/ppermute | solution.py:371
  20.6 6.4 %collective-permute-done.5.refs_5_ = bf16[136,1024]{1,0:T(8,128)(2,1)S(1)} collective-permute-done((bf16[136,1024]{1,0:T(8,128)(2,1)S(1)}, bf16[136,1024]{1,0:T(8,128)(2,1)S(1)}, u32[]{:S(2)}, u32[]{:S(2)}) %collective-permute-start.5) | collective-permute-done | bytes 278560 | tf_op jit(solution)/shard_map/ppermute | solution.py:371
  26.9 2.7 %collective-permute-start.3 = (bf16[136,1024]{1,0:T(8,128)(2,1)S(1)}, bf16[136,1024]{1,0:T(8,128)(2,1)S(1)}, u32[]{:S(2)}, u32[]{:S(2)}) collective-permute-start(bf16[136,1024]{1,0:T(8,128)(2,1)S(1)} %collective-permute-done.2.refs_4_), channel_id=1, source_target_pairs={{0,112},{16,0},{32,16},{48,32},{64,48},{80,64},{96,80},{112,96},{1... | collective-permute-start | bytes 835592 | tf_op jit(solution)/shard_map/ppermute | solution.py:371
  29.6 1.0 copy.9
  30.7 2.7 %collective-permute-start.19 = (bf16[16,64,128]{2,1,0:T(8,128)(2,1)S(1)}, bf16[16,64,128]{2,1,0:T(8,128)(2,1)}, u32[]{:S(2)}, u32[]{:S(2)}) collective-permute-start(bf16[16,64,128]{2,1,0:T(8,128)(2,1)S(1)} %bitcast.18), channel_id=1, source_target_pairs={{0,0},{1,128},{16,16},{17,144},{32,32},{33,160},{48,48},{49,176},{... | collective-permute-start | bytes 786440 | tf_op jit(solution)/shard_map/ppermute | solution.py:380
  33.4 2.9 %collective-permute-start = (s32[16]{0:T(128)}, s32[16]{0:T(128)S(1)}, u32[]{:S(2)}, u32[]{:S(2)}) collective-permute-start(s32[16]{0:T(128)} %bitcast.19), channel_id=1, source_target_pairs={{0,0},{1,128},{16,16},{17,144},{32,32},{33,160},{48,48},{49,176},{... | collective-permute-start | bytes 200 | tf_op jit(solution)/shard_map/ppermute | solution.py:380
  36.2 2.2 %collective-permute-done = s32[16]{0:T(128)S(1)} collective-permute-done((s32[16]{0:T(128)}, s32[16]{0:T(128)S(1)}, u32[]{:S(2)}, u32[]{:S(2)}) %collective-permute-start) | collective-permute-done | bytes 96 | tf_op jit(solution)/shard_map/ppermute | solution.py:380
  39.1 1.4 collective-permute-start.7
  40.5 2.2 %collective-permute-start.8 = (bf16[136,1024]{1,0:T(8,128)(2,1)S(1)}, bf16[136,1024]{1,0:T(8,128)(2,1)}, u32[]{:S(2)}, u32[]{:S(2)}) collective-permute-start(bf16[136,1024]{1,0:T(8,128)(2,1)S(1)} %collective-permute-done.3.refs_1_), channel_id=1, source_target_pairs={{1,113},{17,1},{33,17},{49,33},{65,49},{81,65},{97,81},{113,97},{3... | collective-permute-start | bytes 835592 | tf_op jit(solution)/shard_map/ppermute | solution.py:395
  42.7 7.1 %all-to-all-start = ((bf16[16,64,128]{2,1,0:T(8,128)(2,1)}), bf16[16,64,128]{2,1,0:T(8,128)(2,1)S(1)}, u32[]{:S(2)}, u32[]{:S(2)}) async-start(bf16[16,64,128]{2,1,0:T(8,128)(2,1)} %collective-permute-done.19), calls=%async_computation | async-start | bytes 524288 | tf_op jit(solution)/shard_map/all_to_all | solution.py:420
  50.5 1.3 collective-permute-start.11
  51.8 4.5 %collective-permute-start.12 = (bf16[136,1024]{1,0:T(8,128)(2,1)}, bf16[136,1024]{1,0:T(8,128)(2,1)}, u32[]{:S(2)}, u32[]{:S(2)}) collective-permute-start(bf16[136,1024]{1,0:T(8,128)(2,1)} %collective-permute-done.8.refs_4_), channel_id=1, source_target_pairs={{1,0},{3,2},{5,4},{7,6},{9,8},{11,10},{13,12},{15,14},{17,16},{19,... | collective-permute-start | bytes 835592 | tf_op jit(solution)/shard_map/ppermute | solution.py:418
  56.3 2.0 %constant_dynamic-slice_fusion = (bf16[1024,128]{1,0:T(8,128)(2,1)}, bf16[1024,128]{1,0:T(8,128)(2,1)}, bf16[1024,128]{1,0:T(8,128)(2,1)}) fusion(bf16[1024,3072]{1,0:T(8,128)(2,1)} %w.1, s32[]{:T(128)S(6)} %select_n.19, s32[]{:T(128)S(6)} %select_n.18, s32[]{:T(128)S(6)} %select_n.17), kind=kLoop, calls=%fused_computation.8 | loop fusion | bytes 1572876 | tf_op jit(solution)/shard_map/dynamic_slice | solution.py:413
  58.9 0.6 broadcast_in_dim.4.refs_11_.refs_15_.gain
  59.5 7.5 %early_pass.1 = (bf16[10,128,1024]{2,1,0:T(8,128)(2,1)}, bf16[10,64,128]{2,1,0:T(8,128)(2,1)}, bf16[10,128,128]{2,1,0:T(8,128)(2,1)}, bf16[10,128,128]{2,1,0:T(8...) custom-call(s32[20]{0:T(128)} %concatenate.6.refs_0_.meta, bf16[136,1024]{1,0:T(8,128)(2,1)} %copy-done.12, ...), custom_call_target="tpu_custom_call" | custom-call | tf_op jit(solution)/shard_map/early_pass/pallas_call | solution.py:83
  67.2 0.7 copy-done.7
  67.8 13.9 %head_pass.1 = (bf16[6,128,1024]{2,1,0:T(8,128)(2,1)}, bf16[128,1024]{1,0:T(8,128)(2,1)}, bf16[16,320,128]{2,1,0:T(8,128)(2,1)}) custom-call(s32[20]{0:T(128)} %concatenate.6.refs_0_.meta, bf16[136,1024]{1,0:T(8,128)(2,1)} %copy-done.9, bf16[136,1024]{1,0:T(8,128)(2,1)} %copy-done.8, bf16[136,1024]{1,0:T(8,128)(2,1)} %collective-permute-done.7.refs_3_, ...), custom_call_target="tpu_custom_call" | custom-call | tf_op jit(solution)/shard_map/head_pass/pallas_call | solution.py:202
  81.7 1.7 %collective-permute-start.20 = (bf16[16,320,128]{2,1,0:T(8,128)(2,1)}, bf16[16,320,128]{2,1,0:T(8,128)(2,1)S(1)}, u32[]{:S(2)}, u32[]{:S(2)}) collective-permute-start(bf16[16,320,128]{2,1,0:T(8,128)(2,1)} %get-tuple-element.18.part), channel_id=1, source_target_pairs={{0,1},{1,0},{2,3},{3,2},{4,5},{5,4},{6,7},{7,6},{8,9},{9,8},{10,11... | collective-permute-start | bytes 3932168 | tf_op jit(solution)/shard_map/ppermute | solution.py:367
  83.4 2.9 %collective-permute-done.20.came = bf16[16,320,128]{2,1,0:T(8,128)(2,1)S(1)} collective-permute-done((bf16[16,320,128]{2,1,0:T(8,128)(2,1)}, bf16[16,320,128]{2,1,0:T(8,128)(2,1)S(1)}, u32[]{:S(2)}, u32[]{:S(2)}) %collective-permute-start.20) | collective-permute-done | bytes 1310752 | tf_op jit(solution)/shard_map/ppermute | solution.py:367
  86.3 1.3 copy-done.1
  87.6 1.4 copy-done.3
  89.0 2.0 %weight_pass.1 = (bf16[8,32,384]{2,1,0:T(8,128)(2,1)S(1)}, bf16[8,32,384]{2,1,0:T(8,128)(2,1)S(1)}) custom-call(s32[20]{0:T(128)S(1)} %copy-done.6, bf16[10,128,1024]{2,1,0:T(8,128)(2,1)S(1)} %copy-done.2, bf16[6,128,1024]{2,1,0:T(8,128)(2,1)S(1)} %copy-done.3, bf16[16,320,128]{2,1,0:T(8,128)(2,1)S(1)} %copy-done.1, ...), custom_call_target="tpu_custom_call" | custom-call | tf_op jit(solution)/shard_map/weight_pass/pallas_call | solution.py:269
  91.0 4.0 %collective-permute-start.22 = (bf16[8,32,384]{2,1,0:T(8,128)(2,1)S(1)}, bf16[8,32,384]{2,1,0:T(8,128)(2,1)S(1)}, u32[]{:S(2)}, u32[]{:S(2)}) collective-permute-start(bf16[8,32,384]{2,1,0:T(8,128)(2,1)S(1)} %get-tuple-element.22), channel_id=1, source_target_pairs={{0,0},{1,128},{16,16},{17,144},{32,32},{33,160},{48,48},{49,176},{... | collective-permute-start | bytes 589832 | tf_op jit(solution)/shard_map/ppermute | solution.py:380
  95.1 1.6 %join_pass.1 = bf16[8,384,128]{2,1,0:T(8,128)(2,1)} custom-call(s32[20]{0:T(128)S(1)} %copy-done.6, bf16[16,320,128]{2,1,0:T(8,128)(2,1)S(1)} %copy-done.1, bf16[16,320,128]{2,1,0:T(8,128)(2,1)S(1)} %collective-permute-done.20.came), custom_call_target="tpu_custom_call" | custom-call | tf_op jit(solution)/shard_map/join_pass/pallas_call | solution.py:296
  96.7 7.0 %all-to-all-start.1 = ((bf16[8,384,128]{2,1,0:T(8,128)(2,1)}), bf16[8,384,128]{2,1,0:T(8,128)(2,1)S(1)}, u32[]{:S(2)}, u32[]{:S(2)}) async-start(bf16[8,384,128]{2,1,0:T(8,128)(2,1)} %join_pass.1), calls=%async_computation.1 | async-start | bytes 1572864 | tf_op jit(solution)/shard_map/all_to_all | solution.py:425
  103.8 1.3 collective-permute-start.24
  105.1 4.5 %collective-permute-done.24 = bf16[8,32,384]{2,1,0:T(8,128)(2,1)S(1)} collective-permute-done((bf16[8,32,384]{2,1,0:T(8,128)(2,1)S(1)}, bf16[8,32,384]{2,1,0:T(8,128)(2,1)S(1)}, u32[]{:S(2)}, u32[]{:S(2)}) %collective-permute-start.24) | collective-permute-done | bytes 196640 | tf_op jit(solution)/shard_map/ppermute | solution.py:367
  109.6 2.2 %collective-permute-start.25 = (bf16[8,32,384]{2,1,0:T(8,128)(2,1)S(1)}, bf16[8,32,384]{2,1,0:T(8,128)(2,1)S(1)}, u32[]{:S(2)}, u32[]{:S(2)}) collective-permute-start(bf16[8,32,384]{2,1,0:T(8,128)(2,1)S(1)} %add_convert_fusion.2), channel_id=1, source_target_pairs={{0,8},{4,12},{8,0},{12,4},{1,9},{5,13},{9,1},{13,5},{2,10},{6,14},... | collective-permute-start | bytes 589832 | tf_op jit(solution)/shard_map/ppermute | solution.py:367
  111.8 4.2 %collective-permute-done.25 = bf16[8,32,384]{2,1,0:T(8,128)(2,1)S(1)} collective-permute-done((bf16[8,32,384]{2,1,0:T(8,128)(2,1)S(1)}, bf16[8,32,384]{2,1,0:T(8,128)(2,1)S(1)}, u32[]{:S(2)}, u32[]{:S(2)}) %collective-permute-start.25) | collective-permute-done | bytes 196640 | tf_op jit(solution)/shard_map/ppermute | solution.py:367
  116.1 3.0 %collective-permute-start.26 = (bf16[8,32,384]{2,1,0:T(8,128)(2,1)S(1)}, bf16[8,32,384]{2,1,0:T(8,128)(2,1)S(1)}, u32[]{:S(2)}, u32[]{:S(2)}) collective-permute-start(bf16[8,32,384]{2,1,0:T(8,128)(2,1)S(1)} %add_convert_fusion.1), channel_id=1, source_target_pairs={{0,2},{2,0},{1,3},{3,1},{4,6},{6,4},{5,7},{7,5},{8,10},{10,8},{9,1... | collective-permute-start | bytes 589832 | tf_op jit(solution)/shard_map/ppermute | solution.py:367
  119.1 3.1 %collective-permute-done.26 = bf16[8,32,384]{2,1,0:T(8,128)(2,1)S(1)} collective-permute-done((bf16[8,32,384]{2,1,0:T(8,128)(2,1)S(1)}, bf16[8,32,384]{2,1,0:T(8,128)(2,1)S(1)}, u32[]{:S(2)}, u32[]{:S(2)}) %collective-permute-start.26) | collective-permute-done | bytes 196640 | tf_op jit(solution)/shard_map/ppermute | solution.py:367
  122.2 0.7 add_convert_fusion
  122.9 4.3 %all-to-all-done.1.back = bf16[8,384,128]{2,1,0:T(8,128)(2,1)S(1)} async-done(((bf16[8,384,128]{2,1,0:T(8,128)(2,1)}), bf16[8,384,128]{2,1,0:T(8,128)(2,1)S(1)}, u32[]{:S(2)}, u32[]{:S(2)}) %all-to-all-start.1) | async-done | bytes 786464 | tf_op jit(solution)/shard_map/all_to_all | solution.py:425
  127.3 3.4 %all-to-all-start.2 = ((bf16[8,32,384]{2,1,0:T(8,128)(2,1)}), bf16[8,32,384]{2,1,0:T(8,128)(2,1)S(1)}, u32[]{:S(2)}, u32[]{:S(2)}) async-start(bf16[8,32,384]{2,1,0:T(8,128)(2,1)} %add_convert_fusion), calls=%async_computation.2 | async-start | bytes 393216 | tf_op jit(solution)/shard_map/all_to_all | solution.py:433
  130.7 2.8 %copy-done = bf16[1024,3072]{1,0:T(8,128)(2,1)S(1)} copy-done((bf16[1024,3072]{1,0:T(8,128)(2,1)S(1)}, bf16[1024,3072]{1,0:T(8,128)(2,1)}, u32[]{:S(2)}) %copy-start) | copy-done | bytes 6291480
  133.5 2.9 %rows_pass.1 = bf16[128,1024]{1,0:T(8,128)(2,1)S(1)} custom-call(bf16[8,384,128]{2,1,0:T(8,128)(2,1)S(1)} %all-to-all-done.1.back, bf16[128,1024]{1,0:T(8,128)(2,1)S(1)} %copy-done.5, f32[8,1024]{1,0:T(8,128)S(1)} %copy-done.4, bf16[1024,3072]{1,0:T(8,128)(2,1)S(1)} %copy-done), custom_call_target="tpu_custom_call" | custom-call | tf_op jit(solution)/shard_map/rows_pass/pallas_call | solution.py:324
  136.4 6.1 %collective-permute-start.21 = (bf16[128,1024]{1,0:T(8,128)(2,1)S(1)}, bf16[128,1024]{1,0:T(8,128)(2,1)S(1)}, u32[]{:S(2)}, u32[]{:S(2)}) collective-permute-start(bf16[128,1024]{1,0:T(8,128)(2,1)S(1)} %rows_pass.1), channel_id=1, source_target_pairs={{0,0},{1,128},{16,16},{17,144},{32,32},{33,160},{48,48},{49,176},{... | collective-permute-start | bytes 786440 | tf_op jit(solution)/shard_map/ppermute | solution.py:380
  142.5 0.7 collective-permute-start.27
  143.2 1.1 collective-permute-done.27.other
  144.3 1.5 %final_pass.1 = f32[64,3072]{1,0:T(8,128)} custom-call(s32[20]{0:T(128)S(1)} %copy-done.6, bf16[8,32,384]{2,1,0:T(8,128)(2,1)S(1)} %all-to-all-done.2.own, bf16[8,32,384]{2,1,0:T(8,128)(2,1)S(1)} %collective-permute-done.27.other), custom_call_target="tpu_custom_call" | custom-call | tf_op jit(solution)/shard_map/final_pass/pallas_call | solution.py:361
  145.8 0.7 collective-permute-done.21
  146.5 0.7 copy.11
  (79 shorter events, 3.2 us)
Async XLA Ops:
  0.6 58.2 %copy-start.19 = (f32[1024]{0:T(1024)S(1)}, f32[1024]{0:T(1024)}, u32[]{:S(2)}) copy-start(f32[1024]{0:T(1024)} %param.9) | copy-start | bytes 12292
  2.7 14.7 %collective-permute-start.4 = (bf16[136,1024]{1,0:T(8,128)(2,1)S(1)}, bf16[136,1024]{1,0:T(8,128)(2,1)S(1)}, u32[]{:S(2)}, u32[]{:S(2)}) collective-permute-start(bf16[136,1024]{1,0:T(8,128)(2,1)S(1)} %fusion.1), channel_id=1, source_target_pairs={{0,16},{1,144},{16,32},{17,160},{32,48},{33,176},{48,64},{49,192},... | collective-permute-start | bytes 835592 | tf_op jit(solution)/shard_map/ppermute | solution.py:380
  6.8 10.6 %collective-permute-start.1 = (bf16[136,1024]{1,0:T(8,128)(2,1)S(1)}, bf16[136,1024]{1,0:T(8,128)(2,1)S(1)}, u32[]{:S(2)}, u32[]{:S(2)}) collective-permute-start(bf16[136,1024]{1,0:T(8,128)(2,1)S(1)} %fusion.1), channel_id=1, source_target_pairs={{0,112},{1,240},{16,0},{17,128},{32,16},{33,144},{48,32},{49,160},... | collective-permute-start | bytes 835592 | tf_op jit(solution)/shard_map/ppermute | solution.py:380
  10.8 9.8 %collective-permute-start.13 = (bf16[136,1024]{1,0:T(8,128)(2,1)S(1)}, bf16[136,1024]{1,0:T(8,128)(2,1)S(1)}, u32[]{:S(2)}, u32[]{:S(2)}) collective-permute-start(bf16[136,1024]{1,0:T(8,128)(2,1)S(1)} %fusion.1), channel_id=1, source_target_pairs={{0,0},{1,128},{16,16},{17,144},{32,32},{33,160},{48,48},{49,176},{... | collective-permute-start | bytes 835592 | tf_op jit(solution)/shard_map/ppermute | solution.py:380
  17.4 42.1 %copy-start.10 = (bf16[136,1024]{1,0:T(8,128)(2,1)}, bf16[136,1024]{1,0:T(8,128)(2,1)S(1)}, u32[]{:S(2)}) copy-start(bf16[136,1024]{1,0:T(8,128)(2,1)S(1)} %collective-permute-done.4.refs_3_) | copy-start | bytes 835588
  17.4 9.6 %collective-permute-start.5 = (bf16[136,1024]{1,0:T(8,128)(2,1)S(1)}, bf16[136,1024]{1,0:T(8,128)(2,1)S(1)}, u32[]{:S(2)}, u32[]{:S(2)}) collective-permute-start(bf16[136,1024]{1,0:T(8,128)(2,1)S(1)} %collective-permute-done.4.refs_3_), channel_id=1, source_target_pairs={{0,16},{16,32},{32,48},{48,64},{64,80},{80,96},{96,112},{112,0},{1... | collective-permute-start | bytes 835592 | tf_op jit(solution)/shard_map/ppermute | solution.py:371
  17.4 42.1 %copy-start.11 = (bf16[136,1024]{1,0:T(8,128)(2,1)}, bf16[136,1024]{1,0:T(8,128)(2,1)S(1)}, u32[]{:S(2)}) copy-start(bf16[136,1024]{1,0:T(8,128)(2,1)S(1)} %collective-permute-done.1.refs_2_) | copy-start | bytes 835588
  17.4 9.5 %collective-permute-start.2 = (bf16[136,1024]{1,0:T(8,128)(2,1)S(1)}, bf16[136,1024]{1,0:T(8,128)(2,1)S(1)}, u32[]{:S(2)}, u32[]{:S(2)}) collective-permute-start(bf16[136,1024]{1,0:T(8,128)(2,1)S(1)} %collective-permute-done.1.refs_2_), channel_id=1, source_target_pairs={{0,112},{16,0},{32,16},{48,32},{64,48},{80,64},{96,80},{112,96},{1... | collective-permute-start | bytes 835592 | tf_op jit(solution)/shard_map/ppermute | solution.py:371
  20.6 38.9 %copy-start.12 = (bf16[136,1024]{1,0:T(8,128)(2,1)}, bf16[136,1024]{1,0:T(8,128)(2,1)S(1)}, u32[]{:S(2)}) copy-start(bf16[136,1024]{1,0:T(8,128)(2,1)S(1)} %collective-permute-done.13.refs_1_) | copy-start | bytes 835588
  20.6 18.4 %collective-permute-start.14 = (bf16[136,1024]{1,0:T(8,128)(2,1)S(1)}, bf16[136,1024]{1,0:T(8,128)(2,1)S(1)}, u32[]{:S(2)}, u32[]{:S(2)}) collective-permute-start(bf16[136,1024]{1,0:T(8,128)(2,1)S(1)} %collective-permute-done.13.refs_1_), channel_id=1, source_target_pairs={{0,1},{1,0},{2,3},{3,2},{4,5},{5,4},{6,7},{7,6},{8,9},{9,8},{10,11... | collective-permute-start | bytes 835592 | tf_op jit(solution)/shard_map/ppermute | solution.py:367
  26.9 32.6 %copy-start.13 = (bf16[136,1024]{1,0:T(8,128)(2,1)}, bf16[136,1024]{1,0:T(8,128)(2,1)S(1)}, u32[]{:S(2)}) copy-start(bf16[136,1024]{1,0:T(8,128)(2,1)S(1)} %collective-permute-done.5.refs_5_) | copy-start | bytes 835588
  26.9 12.2 %collective-permute-start.6 = (bf16[136,1024]{1,0:T(8,128)(2,1)S(1)}, bf16[136,1024]{1,0:T(8,128)(2,1)S(1)}, u32[]{:S(2)}, u32[]{:S(2)}) collective-permute-start(bf16[136,1024]{1,0:T(8,128)(2,1)S(1)} %collective-permute-done.5.refs_5_), channel_id=1, source_target_pairs={{0,16},{16,32},{32,48},{48,64},{64,80},{80,96},{96,112},{112,0},{1... | collective-permute-start | bytes 835592 | tf_op jit(solution)/shard_map/ppermute | solution.py:371
  26.9 32.6 %copy-start.14 = (bf16[136,1024]{1,0:T(8,128)(2,1)}, bf16[136,1024]{1,0:T(8,128)(2,1)S(1)}, u32[]{:S(2)}) copy-start(bf16[136,1024]{1,0:T(8,128)(2,1)S(1)} %collective-permute-done.2.refs_4_) | copy-start | bytes 835588
  26.9 13.5 %collective-permute-start.3 = (bf16[136,1024]{1,0:T(8,128)(2,1)S(1)}, bf16[136,1024]{1,0:T(8,128)(2,1)S(1)}, u32[]{:S(2)}, u32[]{:S(2)}) collective-permute-start(bf16[136,1024]{1,0:T(8,128)(2,1)S(1)} %collective-permute-done.2.refs_4_), channel_id=1, source_target_pairs={{0,112},{16,0},{32,16},{48,32},{64,48},{80,64},{96,80},{112,96},{1... | collective-permute-start | bytes 835592 | tf_op jit(solution)/shard_map/ppermute | solution.py:371
  30.7 7.8 %collective-permute-start.19 = (bf16[16,64,128]{2,1,0:T(8,128)(2,1)S(1)}, bf16[16,64,128]{2,1,0:T(8,128)(2,1)}, u32[]{:S(2)}, u32[]{:S(2)}) collective-permute-start(bf16[16,64,128]{2,1,0:T(8,128)(2,1)S(1)} %bitcast.18), channel_id=1, source_target_pairs={{0,0},{1,128},{16,16},{17,144},{32,32},{33,160},{48,48},{49,176},{... | collective-permute-start | bytes 786440 | tf_op jit(solution)/shard_map/ppermute | solution.py:380
  33.4 5.1 %collective-permute-start = (s32[16]{0:T(128)}, s32[16]{0:T(128)S(1)}, u32[]{:S(2)}, u32[]{:S(2)}) collective-permute-start(s32[16]{0:T(128)} %bitcast.19), channel_id=1, source_target_pairs={{0,0},{1,128},{16,16},{17,144},{32,32},{33,160},{48,48},{49,176},{... | collective-permute-start | bytes 200 | tf_op jit(solution)/shard_map/ppermute | solution.py:380
  38.5 11.3 %collective-permute-start.16 = (bf16[136,1024]{1,0:T(8,128)(2,1)S(1)}, bf16[136,1024]{1,0:T(8,128)(2,1)S(1)}, u32[]{:S(2)}, u32[]{:S(2)}) collective-permute-start(bf16[136,1024]{1,0:T(8,128)(2,1)S(1)} %collective-permute-done.4.refs_3_), channel_id=1, source_target_pairs={{0,1},{1,0},{2,3},{3,2},{4,5},{5,4},{6,7},{7,6},{8,9},{9,8},{10,11... | collective-permute-start | bytes 835592 | tf_op jit(solution)/shard_map/ppermute | solution.py:367
  38.5 11.5 %collective-permute-start.15 = (bf16[136,1024]{1,0:T(8,128)(2,1)S(1)}, bf16[136,1024]{1,0:T(8,128)(2,1)S(1)}, u32[]{:S(2)}, u32[]{:S(2)}) collective-permute-start(bf16[136,1024]{1,0:T(8,128)(2,1)S(1)} %collective-permute-done.1.refs_2_), channel_id=1, source_target_pairs={{0,1},{1,0},{2,3},{3,2},{4,5},{5,4},{6,7},{7,6},{8,9},{9,8},{10,11... | collective-permute-start | bytes 835592 | tf_op jit(solution)/shard_map/ppermute | solution.py:367
  39.0 20.5 %copy-start.15 = (bf16[136,1024]{1,0:T(8,128)(2,1)}, bf16[136,1024]{1,0:T(8,128)(2,1)S(1)}, u32[]{:S(2)}) copy-start(bf16[136,1024]{1,0:T(8,128)(2,1)S(1)} %collective-permute-done.14.refs_6_) | copy-start | bytes 835588
  39.0 11.4 %collective-permute-start.18 = (bf16[136,1024]{1,0:T(8,128)(2,1)S(1)}, bf16[136,1024]{1,0:T(8,128)(2,1)S(1)}, u32[]{:S(2)}, u32[]{:S(2)}) collective-permute-start(bf16[136,1024]{1,0:T(8,128)(2,1)S(1)} %collective-permute-done.5.refs_5_), channel_id=1, source_target_pairs={{0,1},{1,0},{2,3},{3,2},{4,5},{5,4},{6,7},{7,6},{8,9},{9,8},{10,11... | collective-permute-start | bytes 835592 | tf_op jit(solution)/shard_map/ppermute | solution.py:367
  39.1 28.0 %copy-start.8 = (bf16[136,1024]{1,0:T(8,128)(2,1)}, bf16[136,1024]{1,0:T(8,128)(2,1)S(1)}, u32[]{:S(2)}) copy-start(bf16[136,1024]{1,0:T(8,128)(2,1)S(1)} %collective-permute-done.6.refs_2_) | copy-start | bytes 835588
  39.1 11.4 %collective-permute-start.7 = (bf16[136,1024]{1,0:T(8,128)(2,1)S(1)}, bf16[136,1024]{1,0:T(8,128)(2,1)}, u32[]{:S(2)}, u32[]{:S(2)}) collective-permute-start(bf16[136,1024]{1,0:T(8,128)(2,1)S(1)} %collective-permute-done.6.refs_2_), channel_id=1, source_target_pairs={{0,16},{16,32},{32,48},{48,64},{64,80},{80,96},{96,112},{112,0},{2... | collective-permute-start | bytes 835592 | tf_op jit(solution)/shard_map/ppermute | solution.py:394
  40.5 26.6 %copy-start.9 = (bf16[136,1024]{1,0:T(8,128)(2,1)}, bf16[136,1024]{1,0:T(8,128)(2,1)S(1)}, u32[]{:S(2)}) copy-start(bf16[136,1024]{1,0:T(8,128)(2,1)S(1)} %collective-permute-done.3.refs_1_) | copy-start | bytes 835588
  40.5 11.3 %collective-permute-start.8 = (bf16[136,1024]{1,0:T(8,128)(2,1)S(1)}, bf16[136,1024]{1,0:T(8,128)(2,1)}, u32[]{:S(2)}, u32[]{:S(2)}) collective-permute-start(bf16[136,1024]{1,0:T(8,128)(2,1)S(1)} %collective-permute-done.3.refs_1_), channel_id=1, source_target_pairs={{1,113},{17,1},{33,17},{49,33},{65,49},{81,65},{97,81},{113,97},{3... | collective-permute-start | bytes 835592 | tf_op jit(solution)/shard_map/ppermute | solution.py:395
  42.7 24.4 %all-to-all-start = ((bf16[16,64,128]{2,1,0:T(8,128)(2,1)}), bf16[16,64,128]{2,1,0:T(8,128)(2,1)S(1)}, u32[]{:S(2)}, u32[]{:S(2)}) async-start(bf16[16,64,128]{2,1,0:T(8,128)(2,1)} %collective-permute-done.19), calls=%async_computation | async-start | bytes 524288 | tf_op jit(solution)/shard_map/all_to_all | solution.py:420
  49.8 9.8 %copy-start.16 = (bf16[136,1024]{1,0:T(8,128)(2,1)}, bf16[136,1024]{1,0:T(8,128)(2,1)S(1)}, u32[]{:S(2)}) copy-start(bf16[136,1024]{1,0:T(8,128)(2,1)S(1)} %collective-permute-done.16.refs_8_) | copy-start | bytes 835588
  49.8 9.1 %collective-permute-start.17 = (bf16[136,1024]{1,0:T(8,128)(2,1)S(1)}, bf16[136,1024]{1,0:T(8,128)(2,1)}, u32[]{:S(2)}, u32[]{:S(2)}) collective-permute-start(bf16[136,1024]{1,0:T(8,128)(2,1)S(1)} %collective-permute-done.2.refs_4_), channel_id=1, source_target_pairs={{0,1},{1,0},{2,3},{3,2},{4,5},{5,4},{6,7},{7,6},{8,9},{9,8},{10,11... | collective-permute-start | bytes 835592 | tf_op jit(solution)/shard_map/ppermute | solution.py:367
  50.0 9.6 %copy-start.17 = (bf16[136,1024]{1,0:T(8,128)(2,1)}, bf16[136,1024]{1,0:T(8,128)(2,1)S(1)}, u32[]{:S(2)}) copy-start(bf16[136,1024]{1,0:T(8,128)(2,1)S(1)} %collective-permute-done.15.refs_7_) | copy-start | bytes 835588
  50.0 17.1 %collective-permute-start.10 = (bf16[136,1024]{1,0:T(8,128)(2,1)S(1)}, bf16[136,1024]{1,0:T(8,128)(2,1)}, u32[]{:S(2)}, u32[]{:S(2)}) collective-permute-start(bf16[136,1024]{1,0:T(8,128)(2,1)S(1)} %collective-permute-done.6.refs_2_), channel_id=1, source_target_pairs={{0,1},{1,0},{2,3},{3,2},{4,5},{5,4},{6,7},{7,6},{8,9},{9,8},{10,11... | collective-permute-start | bytes 835592 | tf_op jit(solution)/shard_map/ppermute | solution.py:367
  50.4 9.2 %copy-start.18 = (bf16[136,1024]{1,0:T(8,128)(2,1)}, bf16[136,1024]{1,0:T(8,128)(2,1)S(1)}, u32[]{:S(2)}) copy-start(bf16[136,1024]{1,0:T(8,128)(2,1)S(1)} %collective-permute-done.18.refs_10_) | copy-start | bytes 835588
  50.4 16.7 %collective-permute-start.9 = (bf16[136,1024]{1,0:T(8,128)(2,1)S(1)}, bf16[136,1024]{1,0:T(8,128)(2,1)}, u32[]{:S(2)}, u32[]{:S(2)}) collective-permute-start(bf16[136,1024]{1,0:T(8,128)(2,1)S(1)} %collective-permute-done.3.refs_1_), channel_id=1, source_target_pairs={{0,1},{1,0},{2,3},{3,2},{4,5},{5,4},{6,7},{7,6},{8,9},{9,8},{10,11... | collective-permute-start | bytes 835592 | tf_op jit(solution)/shard_map/ppermute | solution.py:367
  50.5 16.6 %collective-permute-start.11 = (bf16[136,1024]{1,0:T(8,128)(2,1)}, bf16[136,1024]{1,0:T(8,128)(2,1)}, u32[]{:S(2)}, u32[]{:S(2)}) collective-permute-start(bf16[136,1024]{1,0:T(8,128)(2,1)} %collective-permute-done.7.refs_3_), channel_id=1, source_target_pairs={{0,1},{2,3},{4,5},{6,7},{8,9},{10,11},{12,13},{14,15},{16,17},{18,... | collective-permute-start | bytes 835592 | tf_op jit(solution)/shard_map/ppermute | solution.py:417
  51.8 15.3 %collective-permute-start.12 = (bf16[136,1024]{1,0:T(8,128)(2,1)}, bf16[136,1024]{1,0:T(8,128)(2,1)}, u32[]{:S(2)}, u32[]{:S(2)}) collective-permute-start(bf16[136,1024]{1,0:T(8,128)(2,1)} %collective-permute-done.8.refs_4_), channel_id=1, source_target_pairs={{1,0},{3,2},{5,4},{7,6},{9,8},{11,10},{13,12},{15,14},{17,16},{19,... | collective-permute-start | bytes 835592 | tf_op jit(solution)/shard_map/ppermute | solution.py:418
  67.1 19.2 %copy-start.2 = (bf16[10,128,1024]{2,1,0:T(8,128)(2,1)S(1)}, bf16[10,128,1024]{2,1,0:T(8,128)(2,1)}, u32[]{:S(2)}) copy-start(bf16[10,128,1024]{2,1,0:T(8,128)(2,1)} %get-tuple-element.20.n_early) | copy-start | bytes 7864324
  67.1 19.2 %copy-start.6 = (s32[20]{0:T(128)S(1)}, s32[20]{0:T(128)}, u32[]{:S(2)}) copy-start(s32[20]{0:T(128)} %concatenate.6.refs_0_.meta) | copy-start | bytes 244
  81.7 4.6 %collective-permute-start.20 = (bf16[16,320,128]{2,1,0:T(8,128)(2,1)}, bf16[16,320,128]{2,1,0:T(8,128)(2,1)S(1)}, u32[]{:S(2)}, u32[]{:S(2)}) collective-permute-start(bf16[16,320,128]{2,1,0:T(8,128)(2,1)} %get-tuple-element.18.part), channel_id=1, source_target_pairs={{0,1},{1,0},{2,3},{3,2},{4,5},{5,4},{6,7},{7,6},{8,9},{9,8},{10,11... | collective-permute-start | bytes 3932168 | tf_op jit(solution)/shard_map/ppermute | solution.py:367
  91.0 12.7 %collective-permute-start.22 = (bf16[8,32,384]{2,1,0:T(8,128)(2,1)S(1)}, bf16[8,32,384]{2,1,0:T(8,128)(2,1)S(1)}, u32[]{:S(2)}, u32[]{:S(2)}) collective-permute-start(bf16[8,32,384]{2,1,0:T(8,128)(2,1)S(1)} %get-tuple-element.22), channel_id=1, source_target_pairs={{0,0},{1,128},{16,16},{17,144},{32,32},{33,160},{48,48},{49,176},{... | collective-permute-start | bytes 589832 | tf_op jit(solution)/shard_map/ppermute | solution.py:380
  95.0 8.7 %collective-permute-start.23 = (bf16[8,32,384]{2,1,0:T(8,128)(2,1)S(1)}, bf16[8,32,384]{2,1,0:T(8,128)(2,1)S(1)}, u32[]{:S(2)}, u32[]{:S(2)}) collective-permute-start(bf16[8,32,384]{2,1,0:T(8,128)(2,1)S(1)} %get-tuple-element.23), channel_id=1, source_target_pairs={{0,1},{1,129},{16,17},{17,145},{32,33},{33,161},{48,49},{49,177},{... | collective-permute-start | bytes 589832 | tf_op jit(solution)/shard_map/ppermute | solution.py:380
  96.7 33.9 %copy-start.4 = (f32[8,1024]{1,0:T(8,128)S(1)}, f32[8,1024]{1,0:T(8,128)}, u32[]{:S(2)}) copy-start(f32[8,1024]{1,0:T(8,128)} %broadcast_in_dim.4.refs_11_.refs_15_.gain) | copy-start | bytes 98308
  96.7 33.9 %copy-start.5 = (bf16[128,1024]{1,0:T(8,128)(2,1)S(1)}, bf16[128,1024]{1,0:T(8,128)(2,1)}, u32[]{:S(2)}) copy-start(bf16[128,1024]{1,0:T(8,128)(2,1)} %get-tuple-element.19.mine) | copy-start | bytes 786436
  96.7 30.5 %all-to-all-start.1 = ((bf16[8,384,128]{2,1,0:T(8,128)(2,1)}), bf16[8,384,128]{2,1,0:T(8,128)(2,1)S(1)}, u32[]{:S(2)}, u32[]{:S(2)}) async-start(bf16[8,384,128]{2,1,0:T(8,128)(2,1)} %join_pass.1), calls=%async_computation.1 | async-start | bytes 1572864 | tf_op jit(solution)/shard_map/all_to_all | solution.py:425
  103.8 5.8 %collective-permute-start.24 = (bf16[8,32,384]{2,1,0:T(8,128)(2,1)S(1)}, bf16[8,32,384]{2,1,0:T(8,128)(2,1)S(1)}, u32[]{:S(2)}, u32[]{:S(2)}) collective-permute-start(bf16[8,32,384]{2,1,0:T(8,128)(2,1)S(1)} %add_convert_fusion.3), channel_id=1, source_target_pairs={{0,4},{4,0},{8,12},{12,8},{1,5},{5,1},{9,13},{13,9},{2,6},{6,2},{1... | collective-permute-start | bytes 589832 | tf_op jit(solution)/shard_map/ppermute | solution.py:367
  109.6 6.4 %collective-permute-start.25 = (bf16[8,32,384]{2,1,0:T(8,128)(2,1)S(1)}, bf16[8,32,384]{2,1,0:T(8,128)(2,1)S(1)}, u32[]{:S(2)}, u32[]{:S(2)}) collective-permute-start(bf16[8,32,384]{2,1,0:T(8,128)(2,1)S(1)} %add_convert_fusion.2), channel_id=1, source_target_pairs={{0,8},{4,12},{8,0},{12,4},{1,9},{5,13},{9,1},{13,5},{2,10},{6,14},... | collective-permute-start | bytes 589832 | tf_op jit(solution)/shard_map/ppermute | solution.py:367
  116.1 6.1 %collective-permute-start.26 = (bf16[8,32,384]{2,1,0:T(8,128)(2,1)S(1)}, bf16[8,32,384]{2,1,0:T(8,128)(2,1)S(1)}, u32[]{:S(2)}, u32[]{:S(2)}) collective-permute-start(bf16[8,32,384]{2,1,0:T(8,128)(2,1)S(1)} %add_convert_fusion.1), channel_id=1, source_target_pairs={{0,2},{2,0},{1,3},{3,1},{4,6},{6,4},{5,7},{7,5},{8,10},{10,8},{9,1... | collective-permute-start | bytes 589832 | tf_op jit(solution)/shard_map/ppermute | solution.py:367
  127.3 15.2 %all-to-all-start.2 = ((bf16[8,32,384]{2,1,0:T(8,128)(2,1)}), bf16[8,32,384]{2,1,0:T(8,128)(2,1)S(1)}, u32[]{:S(2)}, u32[]{:S(2)}) async-start(bf16[8,32,384]{2,1,0:T(8,128)(2,1)} %add_convert_fusion), calls=%async_computation.2 | async-start | bytes 393216 | tf_op jit(solution)/shard_map/all_to_all | solution.py:433
  130.7 2.8 %copy-start = (bf16[1024,3072]{1,0:T(8,128)(2,1)S(1)}, bf16[1024,3072]{1,0:T(8,128)(2,1)}, u32[]{:S(2)}) copy-start(bf16[1024,3072]{1,0:T(8,128)(2,1)} %w.1) | copy-start | bytes 18874372
  136.4 10.1 %collective-permute-start.21 = (bf16[128,1024]{1,0:T(8,128)(2,1)S(1)}, bf16[128,1024]{1,0:T(8,128)(2,1)S(1)}, u32[]{:S(2)}, u32[]{:S(2)}) collective-permute-start(bf16[128,1024]{1,0:T(8,128)(2,1)S(1)} %rows_pass.1), channel_id=1, source_target_pairs={{0,0},{1,128},{16,16},{17,144},{32,32},{33,160},{48,48},{49,176},{... | collective-permute-start | bytes 786440 | tf_op jit(solution)/shard_map/ppermute | solution.py:380
  142.5 1.8 %collective-permute-start.27 = (bf16[8,32,384]{2,1,0:T(8,128)(2,1)S(1)}, bf16[8,32,384]{2,1,0:T(8,128)(2,1)S(1)}, u32[]{:S(2)}, u32[]{:S(2)}) collective-permute-start(bf16[8,32,384]{2,1,0:T(8,128)(2,1)S(1)} %all-to-all-done.2.own), channel_id=1, source_target_pairs={{0,1},{1,0},{2,3},{3,2},{4,5},{5,4},{6,7},{7,6},{8,9},{9,8},{10,11... | collective-permute-start | bytes 589832 | tf_op jit(solution)/shard_map/ppermute | solution.py:367
  (3 other events, 3.4 us)

commit v5 on v2

--- a/solution.py
+++ b/solution.py
@@ -51,16 +51,22 @@
         copies = []
         for c, group in enumerate((pieces, others)):
             side = half if c == 0 else 1 - half
-            for n, ref in enumerate(group):
-                offset = (0, 1, 7, 2, 6, 3, 5, 4, 4)[n]
+            for n, ref in enumerate(group[:7]):
+                offset = (0, 1, 7, 2, 6, 3, 5)[n]
                 target = rows_s.at[side * 8 + (z + offset) % 8]
-                if n == 7:
-                    target = target.at[0:HALF]
-                elif n == 8:
-                    target = target.at[HALF : BLOCK + EXTRA]
                 copies.append(pltpu.make_async_copy(ref, target, sems.at[c * PIECES + n]))
         for copy in copies:
             copy.start()
+
+        for c, group in enumerate((pieces, others)):
+            far = rows_s.at[(half if c == 0 else 1 - half) * 8 + (z + 4) % 8]
+            for n in range(2):
+
+                @pl.when(half == (n if c == 0 else 1 - n))
+                def _():
+                    copy = pltpu.make_async_copy(group[7 + n], far, sems.at[c * PIECES + 7 + n])
+                    copy.start()
+                    copy.wait()
 
         def put(p, carry):
             inv[meta[p]] = p
@@ -351,9 +357,8 @@
     for _ in range(2):
         down, up = ring(down, "z", -1, 8), ring(up, "z", 1, 8)
         made += [down, up]
-    far = ring(up[:HALF], "z", 1, 8)
-    made.append(far)
-    made.append(ring(down[HALF:], "z", -1, 8))
+    made.append(lax.ppermute(up, ("z", "core"), [(2 * n, 2 * ((n + 1) % 8)) for n in range(8)]))
+    made.append(lax.ppermute(down, ("z", "core"), [(2 * n + 1, 2 * ((n + 7) % 8) + 1) for n in range(8)]))
     return made
 
 
@@ -374,7 +379,9 @@
     w_head = [lax.dynamic_slice_in_dim(w_qkv, n * D + z * HEAD, HEAD, 1) for n in range(3)]
 
     pieces = relay(payload)
-    others = [flip(piece, "core", 1, 2) for piece in pieces]
+    others = [flip(piece, "core", 1, 2) for piece in pieces[:7]]
+    others.append(lax.ppermute(pieces[7], "core", [(0, 1)]))
+    others.append(lax.ppermute(pieces[8], "core", [(1, 0)]))
     do = lax.all_to_all(parts, ("z", "core"), 0, 0, tiled=True)
     normed, mine, part = head_pass(meta, pieces, others, do, gain, w_head)
     came = flip(part, "core", 1, 2)

time: 136 us -> 143 us (1.051)
  starting transfers between devices: 64.5 us -> 67.8 us
    ppermute x0 -> x4, starting transfers between devices: none -> 9.01 us  [the longest x1 4.45 us: work(): others.append(lax.ppermute(pieces[8], 'core', [(1, 0)]))]
    ppermute x6 -> x4, waiting for transfers between devices: 9.19 us -> 3.04 us  [ring(): return lax.ppermute(x, axis, [(i, (i + by) % size) for i in range(size)])]
    ppermute x14 -> x12, starting transfers between devices: 17.4 us -> 12.1 us  [flip(): return lax.ppermute(x, axis, [(i, i ^ bit) for i in range(size)])]
    ppermute x8, waiting for transfers between devices: 9.26 us -> 14.6 us  [turn(): return lax.ppermute(x, ('y_lo', 'z', 'core'), pairs)]
    ppermute x6 -> x4, starting transfers between devices: 9.93 us -> 5.35 us  [ring(): return lax.ppermute(x, axis, [(i, (i + by) % size) for i in range(size)])]
    all_to_all x1, starting transfers between devices: 4.52 us -> 7.19 us  [work(): do = lax.all_to_all(parts, ('z', 'core'), 0, 0, tiled=True)]
    all_to_all x1, waiting for transfers between devices: 0.01 us -> 2.5 us  [work(): do = lax.all_to_all(parts, ('z', 'core'), 0, 0, tiled=True)]
    unnamed x18 -> x16, local copies, waits for them, and re-layouts: 7.11 us -> 7.83 us
  transfers between devices with their start and end apart: 31 -> 31, of which waited for: 14 -> 12; matrix products, arithmetic and copies ran while one was open for 2% -> 2% of each run, Pallas kernels for 4% -> 4%
where the time goes in v5:
time: 143 us; the launch traced here: 142 us
  starting transfers between devices  67.8 us (47%)
  waiting for transfers between devices  39 us (27%)
  Pallas kernels  21.9 us (15%)
  local copies, waits for them, and re-layouts  10.2 us (7%)
  other arithmetic  2.54 us (2%)
    ppermute x8, starting transfers between devices, turn(): return lax.ppermute(x, ('y_lo', 'z', 'core'), pairs)  26.5 us
    ppermute x8, waiting for transfers between devices, turn(): return lax.ppermute(x, ('y_lo', 'z', 'core'), pairs)  14.6 us
    ppermute x12, waiting for transfers between devices, flip(): return lax.ppermute(x, axis, [(i, i ^ bit) for i in range(size)])  14.2 us
    pallas_call x1, Pallas kernels, head_pass(): pl.pallas_call(head_kernel, grid_spec=grid_spec, out_shape=[jax.ShapeDtyp...  12.9 us
    ppermute x12, starting transfers between devices, flip(): return lax.ppermute(x, axis, [(i, i ^ bit) for i in range(size)])  12.1 us
    unnamed x16, local copies, waits for them, and re-layouts  7.83 us
    all_to_all x1, starting transfers between devices, work(): do = lax.all_to_all(parts, ('z', 'core'), 0, 0, tiled=True)  7.19 us
    ppermute x4, starting transfers between devices, ring(): return lax.ppermute(x, axis, [(i, (i + by) % size) for i in range(size)])  5.35 us
  transfers between devices with their start and end apart: 31, of which 12 were waited for; matrix products, arithmetic and copies ran while one was open for 2% of the time, Pallas kernels for 4%

profile of v5, /device:TPU:1, one launch (start us, length us, event | category | flops | bytes accessed | tf_op | source)
XLA Modules:
  0.0 142.4 jit_solution(6501667088877938274)
XLA Ops:
  1.7 1.0 fusion.1
  2.7 4.1 %collective-permute-start.3 = (bf16[136,1024]{1,0:T(8,128)(2,1)S(1)}, bf16[136,1024]{1,0:T(8,128)(2,1)S(1)}, u32[]{:S(2)}, u32[]{:S(2)}) collective-permute-start(bf16[136,1024]{1,0:T(8,128)(2,1)S(1)} %fusion.1), channel_id=1, source_target_pairs={{0,16},{1,144},{16,32},{17,160},{32,48},{33,176},{48,64},{49,192},... | collective-permute-start | bytes 835592 | tf_op jit(solution)/shard_map/ppermute | solution.py:346
  6.8 4.0 %collective-permute-start.2 = (bf16[136,1024]{1,0:T(8,128)(2,1)S(1)}, bf16[136,1024]{1,0:T(8,128)(2,1)S(1)}, u32[]{:S(2)}, u32[]{:S(2)}) collective-permute-start(bf16[136,1024]{1,0:T(8,128)(2,1)S(1)} %fusion.1), channel_id=1, source_target_pairs={{0,112},{1,240},{16,0},{17,128},{32,16},{33,144},{48,32},{49,160},... | collective-permute-start | bytes 835592 | tf_op jit(solution)/shard_map/ppermute | solution.py:346
  10.8 6.5 %collective-permute-done.3.refs_3_ = bf16[136,1024]{1,0:T(8,128)(2,1)S(1)} collective-permute-done((bf16[136,1024]{1,0:T(8,128)(2,1)S(1)}, bf16[136,1024]{1,0:T(8,128)(2,1)S(1)}, u32[]{:S(2)}, u32[]{:S(2)}) %collective-permute-start.3) | collective-permute-done | bytes 278560 | tf_op jit(solution)/shard_map/ppermute | solution.py:346
  17.3 2.7 %collective-permute-start.4 = (bf16[136,1024]{1,0:T(8,128)(2,1)S(1)}, bf16[136,1024]{1,0:T(8,128)(2,1)S(1)}, u32[]{:S(2)}, u32[]{:S(2)}) collective-permute-start(bf16[136,1024]{1,0:T(8,128)(2,1)S(1)} %collective-permute-done.2.refs_2_), channel_id=1, source_target_pairs={{0,112},{16,0},{32,16},{48,32},{64,48},{80,64},{96,80},{112,96},{1... | collective-permute-start | bytes 835592 | tf_op jit(solution)/shard_map/ppermute | solution.py:337
  19.9 3.9 %collective-permute-start.1 = (bf16[136,1024]{1,0:T(8,128)(2,1)S(1)}, bf16[136,1024]{1,0:T(8,128)(2,1)S(1)}, u32[]{:S(2)}, u32[]{:S(2)}) collective-permute-start(bf16[136,1024]{1,0:T(8,128)(2,1)S(1)} %fusion.1), channel_id=1, source_target_pairs={{0,0},{1,128},{16,16},{17,144},{32,32},{33,160},{48,48},{49,176},{... | collective-permute-start | bytes 835592 | tf_op jit(solution)/shard_map/ppermute | solution.py:346
  24.0 3.0 %collective-permute-done.5.refs_5_ = bf16[136,1024]{1,0:T(8,128)(2,1)S(1)} collective-permute-done((bf16[136,1024]{1,0:T(8,128)(2,1)S(1)}, bf16[136,1024]{1,0:T(8,128)(2,1)S(1)}, u32[]{:S(2)}, u32[]{:S(2)}) %collective-permute-start.5) | collective-permute-done | bytes 278560 | tf_op jit(solution)/shard_map/ppermute | solution.py:337
  27.0 2.7 %collective-permute-start.6 = (bf16[136,1024]{1,0:T(8,128)(2,1)S(1)}, bf16[136,1024]{1,0:T(8,128)(2,1)S(1)}, u32[]{:S(2)}, u32[]{:S(2)}) collective-permute-start(bf16[136,1024]{1,0:T(8,128)(2,1)S(1)} %collective-permute-done.4.refs_4_), channel_id=1, source_target_pairs={{0,112},{16,0},{32,16},{48,32},{64,48},{80,64},{96,80},{112,96},{1... | collective-permute-start | bytes 835592 | tf_op jit(solution)/shard_map/ppermute | solution.py:337
  29.7 2.6 %collective-permute-start = (s32[16]{0:T(128)}, s32[16]{0:T(128)S(1)}, u32[]{:S(2)}, u32[]{:S(2)}) collective-permute-start(s32[16]{0:T(128)} %bitcast.19), channel_id=1, source_target_pairs={{0,0},{1,128},{16,16},{17,144},{32,32},{33,160},{48,48},{49,176},{... | collective-permute-start | bytes 200 | tf_op jit(solution)/shard_map/ppermute | solution.py:346
  32.3 1.0 copy.9
  33.3 1.7 %collective-permute-done = s32[16]{0:T(128)S(1)} collective-permute-done((s32[16]{0:T(128)}, s32[16]{0:T(128)S(1)}, u32[]{:S(2)}, u32[]{:S(2)}) %collective-permute-start) | collective-permute-done | bytes 96 | tf_op jit(solution)/shard_map/ppermute | solution.py:346
  35.0 2.3 %collective-permute-start.19 = (bf16[16,64,128]{2,1,0:T(8,128)(2,1)S(1)}, bf16[16,64,128]{2,1,0:T(8,128)(2,1)}, u32[]{:S(2)}, u32[]{:S(2)}) collective-permute-start(bf16[16,64,128]{2,1,0:T(8,128)(2,1)S(1)} %bitcast.18), channel_id=1, source_target_pairs={{0,0},{1,128},{16,16},{17,144},{32,32},{33,160},{48,48},{49,176},{... | collective-permute-start | bytes 786440 | tf_op jit(solution)/shard_map/ppermute | solution.py:346
  37.3 5.5 %collective-permute-done.19 = bf16[16,64,128]{2,1,0:T(8,128)(2,1)} collective-permute-done((bf16[16,64,128]{2,1,0:T(8,128)(2,1)S(1)}, bf16[16,64,128]{2,1,0:T(8,128)(2,1)}, u32[]{:S(2)}, u32[]{:S(2)}) %collective-permute-start.19) | collective-permute-done | bytes 262176 | tf_op jit(solution)/shard_map/ppermute | solution.py:346
  43.4 1.4 collective-permute-start.8
  44.8 1.9 %collective-permute-start.9 = (bf16[136,1024]{1,0:T(8,128)(2,1)S(1)}, bf16[136,1024]{1,0:T(8,128)(2,1)}, u32[]{:S(2)}, u32[]{:S(2)}) collective-permute-start(bf16[136,1024]{1,0:T(8,128)(2,1)S(1)} %collective-permute-done.6.refs_6_), channel_id=1, source_target_pairs={{1,113},{17,1},{33,17},{49,33},{65,49},{81,65},{97,81},{113,97},{3... | collective-permute-start | bytes 835592 | tf_op jit(solution)/shard_map/ppermute | solution.py:361
  46.7 7.2 %all-to-all-start = ((bf16[16,64,128]{2,1,0:T(8,128)(2,1)}), bf16[16,64,128]{2,1,0:T(8,128)(2,1)S(1)}, u32[]{:S(2)}, u32[]{:S(2)}) async-start(bf16[16,64,128]{2,1,0:T(8,128)(2,1)} %collective-permute-done.19), calls=%async_computation | async-start | bytes 524288 | tf_op jit(solution)/shard_map/all_to_all | solution.py:385
  53.9 0.7 copy-done.1
  54.7 0.7 copy-done.3
  55.9 1.3 collective-permute-start.17
  57.2 4.5 %collective-permute-start.18 = (bf16[136,1024]{1,0:T(8,128)(2,1)}, bf16[136,1024]{1,0:T(8,128)(2,1)}, u32[]{:S(2)}, u32[]{:S(2)}) collective-permute-start(bf16[136,1024]{1,0:T(8,128)(2,1)} %collective-permute-done.9.refs_9_), channel_id=1, source_target_pairs={{1,0},{3,2},{5,4},{7,6},{9,8},{11,10},{13,12},{15,14},{17,16},{19,... | collective-permute-start | bytes 835592 | tf_op jit(solution)/shard_map/ppermute | solution.py:384
  61.7 1.2 constant_dynamic-slice_fusion
  63.0 2.5 %all-to-all-done.refs_19_ = bf16[16,64,128]{2,1,0:T(8,128)(2,1)S(1)} async-done(((bf16[16,64,128]{2,1,0:T(8,128)(2,1)}), bf16[16,64,128]{2,1,0:T(8,128)(2,1)S(1)}, u32[]{:S(2)}, u32[]{:S(2)}) %all-to-all-start) | async-done | bytes 262176 | tf_op jit(solution)/shard_map/all_to_all | solution.py:385
  65.5 0.7 broadcast_in_dim.4.refs_20_.gain
  66.2 1.0 copy-done.2
  67.1 1.0 copy-done.4
  68.1 12.9 %head_pass.1 = (bf16[16,128,1024]{2,1,0:T(8,128)(2,1)S(1)}, bf16[128,1024]{1,0:T(8,128)(2,1)S(1)}, bf16[16,320,128]{2,1,0:T(8,128)(2,1)S(1)}) custom-call(s32[20]{0:T(128)S(1)} %concatenate.6.refs_0_.meta, bf16[136,1024]{1,0:T(8,128)(2,1)S(1)} %collective-permute-done.1.refs_1_, bf16[136,1024]{1,0:T(8,128)(2,1)S(1)} %collective-permute-done.2.refs_2_, ...), custom_call_target="tpu_custom_call" | custom-call | tf_op jit(solution)/shard_map/head_pass/pallas_call | solution.py:175
  81.0 2.7 %collective-permute-start.20 = (bf16[16,320,128]{2,1,0:T(8,128)(2,1)S(1)}, bf16[16,320,128]{2,1,0:T(8,128)(2,1)S(1)}, u32[]{:S(2)}, u32[]{:S(2)}) collective-permute-start(bf16[16,320,128]{2,1,0:T(8,128)(2,1)S(1)} %get-tuple-element.7.part), channel_id=1, source_target_pairs={{0,1},{1,0},{2,3},{3,2},{4,5},{5,4},{6,7},{7,6},{8,9},{9,8},{10,11... | collective-permute-start | bytes 3932168 | tf_op jit(solution)/shard_map/ppermute | solution.py:333
  83.7 2.7 %collective-permute-done.20.came = bf16[16,320,128]{2,1,0:T(8,128)(2,1)S(1)} collective-permute-done((bf16[16,320,128]{2,1,0:T(8,128)(2,1)S(1)}, bf16[16,320,128]{2,1,0:T(8,128)(2,1)S(1)}, u32[]{:S(2)}, u32[]{:S(2)}) %collective-permute-start.20) | collective-permute-done | bytes 1310752 | tf_op jit(solution)/shard_map/ppermute | solution.py:333
  86.4 3.0 %weight_pass.1 = (bf16[8,32,384]{2,1,0:T(8,128)(2,1)S(1)}, bf16[8,32,384]{2,1,0:T(8,128)(2,1)S(1)}) custom-call(s32[20]{0:T(128)S(1)} %concatenate.6.refs_0_.meta, bf16[16,128,1024]{2,1,0:T(8,128)(2,1)S(1)} %get-tuple-element.9.normed, bf16[16,320,128]{2,1,0:T(8,128)(2,1)S(1)} %get-tuple-element.7.part, bf16[16,320,128]{2,1,0:T(8,128)(2,1)S(1)} %collective-permute-done.20.came), custom_call_target="tpu_custom_call" | custom-call | tf_op jit(solution)/shard_map/weight_pass/pallas_call | solution.py:236
  89.4 2.5 %collective-permute-start.22 = (bf16[8,32,384]{2,1,0:T(8,128)(2,1)S(1)}, bf16[8,32,384]{2,1,0:T(8,128)(2,1)S(1)}, u32[]{:S(2)}, u32[]{:S(2)}) collective-permute-start(bf16[8,32,384]{2,1,0:T(8,128)(2,1)S(1)} %get-tuple-element.10), channel_id=1, source_target_pairs={{0,0},{1,128},{16,16},{17,144},{32,32},{33,160},{48,48},{49,176},{... | collective-permute-start | bytes 589832 | tf_op jit(solution)/shard_map/ppermute | solution.py:346
  92.0 1.6 %join_pass.1 = bf16[8,384,128]{2,1,0:T(8,128)(2,1)} custom-call(s32[20]{0:T(128)S(1)} %concatenate.6.refs_0_.meta, bf16[16,320,128]{2,1,0:T(8,128)(2,1)S(1)} %get-tuple-element.7.part, bf16[16,320,128]{2,1,0:T(8,128)(2,1)S(1)} %collective-permute-done.20.came), custom_call_target="tpu_custom_call" | custom-call | tf_op jit(solution)/shard_map/join_pass/pallas_call | solution.py:262
  93.6 4.3 %all-to-all-start.1 = ((bf16[8,384,128]{2,1,0:T(8,128)(2,1)}), bf16[8,384,128]{2,1,0:T(8,128)(2,1)S(1)}, u32[]{:S(2)}, u32[]{:S(2)}) async-start(bf16[8,384,128]{2,1,0:T(8,128)(2,1)} %join_pass.1), calls=%async_computation.1 | async-start | bytes 1572864 | tf_op jit(solution)/shard_map/all_to_all | solution.py:390
  98.0 1.6 %collective-permute-start.24 = (bf16[8,32,384]{2,1,0:T(8,128)(2,1)S(1)}, bf16[8,32,384]{2,1,0:T(8,128)(2,1)S(1)}, u32[]{:S(2)}, u32[]{:S(2)}) collective-permute-start(bf16[8,32,384]{2,1,0:T(8,128)(2,1)S(1)} %add_convert_fusion.3), channel_id=1, source_target_pairs={{0,4},{4,0},{8,12},{12,8},{1,5},{5,1},{9,13},{13,9},{2,6},{6,2},{1... | collective-permute-start | bytes 589832 | tf_op jit(solution)/shard_map/ppermute | solution.py:333
  99.6 3.5 %collective-permute-done.24 = bf16[8,32,384]{2,1,0:T(8,128)(2,1)S(1)} collective-permute-done((bf16[8,32,384]{2,1,0:T(8,128)(2,1)S(1)}, bf16[8,32,384]{2,1,0:T(8,128)(2,1)S(1)}, u32[]{:S(2)}, u32[]{:S(2)}) %collective-permute-start.24) | collective-permute-done | bytes 196640 | tf_op jit(solution)/shard_map/ppermute | solution.py:333
  103.1 3.0 %collective-permute-start.25 = (bf16[8,32,384]{2,1,0:T(8,128)(2,1)S(1)}, bf16[8,32,384]{2,1,0:T(8,128)(2,1)S(1)}, u32[]{:S(2)}, u32[]{:S(2)}) collective-permute-start(bf16[8,32,384]{2,1,0:T(8,128)(2,1)S(1)} %add_convert_fusion.2), channel_id=1, source_target_pairs={{0,8},{4,12},{8,0},{12,4},{1,9},{5,13},{9,1},{13,5},{2,10},{6,14},... | collective-permute-start | bytes 589832 | tf_op jit(solution)/shard_map/ppermute | solution.py:333
  106.1 3.5 %collective-permute-done.25 = bf16[8,32,384]{2,1,0:T(8,128)(2,1)S(1)} collective-permute-done((bf16[8,32,384]{2,1,0:T(8,128)(2,1)S(1)}, bf16[8,32,384]{2,1,0:T(8,128)(2,1)S(1)}, u32[]{:S(2)}, u32[]{:S(2)}) %collective-permute-start.25) | collective-permute-done | bytes 196640 | tf_op jit(solution)/shard_map/ppermute | solution.py:333
  109.7 3.4 %collective-permute-start.26 = (bf16[8,32,384]{2,1,0:T(8,128)(2,1)S(1)}, bf16[8,32,384]{2,1,0:T(8,128)(2,1)S(1)}, u32[]{:S(2)}, u32[]{:S(2)}) collective-permute-start(bf16[8,32,384]{2,1,0:T(8,128)(2,1)S(1)} %add_convert_fusion.1), channel_id=1, source_target_pairs={{0,2},{2,0},{1,3},{3,1},{4,6},{6,4},{5,7},{7,5},{8,10},{10,8},{9,1... | collective-permute-start | bytes 589832 | tf_op jit(solution)/shard_map/ppermute | solution.py:333
  113.1 3.1 %collective-permute-done.26 = bf16[8,32,384]{2,1,0:T(8,128)(2,1)S(1)} collective-permute-done((bf16[8,32,384]{2,1,0:T(8,128)(2,1)S(1)}, bf16[8,32,384]{2,1,0:T(8,128)(2,1)S(1)}, u32[]{:S(2)}, u32[]{:S(2)}) %collective-permute-start.26) | collective-permute-done | bytes 196640 | tf_op jit(solution)/shard_map/ppermute | solution.py:333
  116.1 0.7 add_convert_fusion
  116.8 4.7 %all-to-all-done.1.back = bf16[8,384,128]{2,1,0:T(8,128)(2,1)S(1)} async-done(((bf16[8,384,128]{2,1,0:T(8,128)(2,1)}), bf16[8,384,128]{2,1,0:T(8,128)(2,1)S(1)}, u32[]{:S(2)}, u32[]{:S(2)}) %all-to-all-start.1) | async-done | bytes 786464 | tf_op jit(solution)/shard_map/all_to_all | solution.py:390
  121.5 3.4 %all-to-all-start.2 = ((bf16[8,32,384]{2,1,0:T(8,128)(2,1)}), bf16[8,32,384]{2,1,0:T(8,128)(2,1)S(1)}, u32[]{:S(2)}, u32[]{:S(2)}) async-start(bf16[8,32,384]{2,1,0:T(8,128)(2,1)} %add_convert_fusion), calls=%async_computation.2 | async-start | bytes 393216 | tf_op jit(solution)/shard_map/all_to_all | solution.py:398
  124.9 2.8 %copy-done = bf16[1024,3072]{1,0:T(8,128)(2,1)S(1)} copy-done((bf16[1024,3072]{1,0:T(8,128)(2,1)S(1)}, bf16[1024,3072]{1,0:T(8,128)(2,1)}, u32[]{:S(2)}) %copy-start) | copy-done | bytes 6291480
  127.7 2.9 %rows_pass.1 = bf16[128,1024]{1,0:T(8,128)(2,1)S(1)} custom-call(bf16[8,384,128]{2,1,0:T(8,128)(2,1)S(1)} %all-to-all-done.1.back, bf16[128,1024]{1,0:T(8,128)(2,1)S(1)} %copy-done.6, f32[8,1024]{1,0:T(8,128)S(1)} %broadcast_in_dim.4.refs_20_.gain, bf16[1024,3072]{1,0:T(8,128)(2,1)S(1)} %copy-done), custom_call_target="tpu_custom_call" | custom-call | tf_op jit(solution)/shard_map/rows_pass/pallas_call | solution.py:290
  130.7 6.9 %collective-permute-start.21 = (bf16[128,1024]{1,0:T(8,128)(2,1)S(1)}, bf16[128,1024]{1,0:T(8,128)(2,1)S(1)}, u32[]{:S(2)}, u32[]{:S(2)}) collective-permute-start(bf16[128,1024]{1,0:T(8,128)(2,1)S(1)} %rows_pass.1), channel_id=1, source_target_pairs={{0,0},{1,128},{16,16},{17,144},{32,32},{33,160},{48,48},{49,176},{... | collective-permute-start | bytes 786440 | tf_op jit(solution)/shard_map/ppermute | solution.py:346
  137.7 1.4 %collective-permute-done.27.other = bf16[8,32,384]{2,1,0:T(8,128)(2,1)S(1)} collective-permute-done((bf16[8,32,384]{2,1,0:T(8,128)(2,1)S(1)}, bf16[8,32,384]{2,1,0:T(8,128)(2,1)S(1)}, u32[]{:S(2)}, u32[]{:S(2)}) %collective-permute-start.27) | collective-permute-done | bytes 196640 | tf_op jit(solution)/shard_map/ppermute | solution.py:333
  139.1 1.5 %final_pass.1 = f32[64,3072]{1,0:T(8,128)} custom-call(s32[20]{0:T(128)S(1)} %concatenate.6.refs_0_.meta, bf16[8,32,384]{2,1,0:T(8,128)(2,1)S(1)} %all-to-all-done.2.own, bf16[8,32,384]{2,1,0:T(8,128)(2,1)S(1)} %collective-permute-done.27.other), custom_call_target="tpu_custom_call" | custom-call | tf_op jit(solution)/shard_map/final_pass/pallas_call | solution.py:327
  140.6 1.0 collective-permute-done.21
  141.6 0.7 copy.11
  (52 shorter events, 2.9 us)
Async XLA Ops:
  2.7 14.6 %collective-permute-start.3 = (bf16[136,1024]{1,0:T(8,128)(2,1)S(1)}, bf16[136,1024]{1,0:T(8,128)(2,1)S(1)}, u32[]{:S(2)}, u32[]{:S(2)}) collective-permute-start(bf16[136,1024]{1,0:T(8,128)(2,1)S(1)} %fusion.1), channel_id=1, source_target_pairs={{0,16},{1,144},{16,32},{17,160},{32,48},{33,176},{48,64},{49,192},... | collective-permute-start | bytes 835592 | tf_op jit(solution)/shard_map/ppermute | solution.py:346
  6.8 10.5 %collective-permute-start.2 = (bf16[136,1024]{1,0:T(8,128)(2,1)S(1)}, bf16[136,1024]{1,0:T(8,128)(2,1)S(1)}, u32[]{:S(2)}, u32[]{:S(2)}) collective-permute-start(bf16[136,1024]{1,0:T(8,128)(2,1)S(1)} %fusion.1), channel_id=1, source_target_pairs={{0,112},{1,240},{16,0},{17,128},{32,16},{33,144},{48,32},{49,160},... | collective-permute-start | bytes 835592 | tf_op jit(solution)/shard_map/ppermute | solution.py:346
  17.3 9.7 %collective-permute-start.5 = (bf16[136,1024]{1,0:T(8,128)(2,1)S(1)}, bf16[136,1024]{1,0:T(8,128)(2,1)S(1)}, u32[]{:S(2)}, u32[]{:S(2)}) collective-permute-start(bf16[136,1024]{1,0:T(8,128)(2,1)S(1)} %collective-permute-done.3.refs_3_), channel_id=1, source_target_pairs={{0,16},{16,32},{32,48},{48,64},{64,80},{80,96},{96,112},{112,0},{1... | collective-permute-start | bytes 835592 | tf_op jit(solution)/shard_map/ppermute | solution.py:337
  17.3 9.7 %collective-permute-start.4 = (bf16[136,1024]{1,0:T(8,128)(2,1)S(1)}, bf16[136,1024]{1,0:T(8,128)(2,1)S(1)}, u32[]{:S(2)}, u32[]{:S(2)}) collective-permute-start(bf16[136,1024]{1,0:T(8,128)(2,1)S(1)} %collective-permute-done.2.refs_2_), channel_id=1, source_target_pairs={{0,112},{16,0},{32,16},{48,32},{64,48},{80,64},{96,80},{112,96},{1... | collective-permute-start | bytes 835592 | tf_op jit(solution)/shard_map/ppermute | solution.py:337
  19.9 22.8 %collective-permute-start.1 = (bf16[136,1024]{1,0:T(8,128)(2,1)S(1)}, bf16[136,1024]{1,0:T(8,128)(2,1)S(1)}, u32[]{:S(2)}, u32[]{:S(2)}) collective-permute-start(bf16[136,1024]{1,0:T(8,128)(2,1)S(1)} %fusion.1), channel_id=1, source_target_pairs={{0,0},{1,128},{16,16},{17,144},{32,32},{33,160},{48,48},{49,176},{... | collective-permute-start | bytes 835592 | tf_op jit(solution)/shard_map/ppermute | solution.py:346
  23.9 19.4 %collective-permute-start.12 = (bf16[136,1024]{1,0:T(8,128)(2,1)S(1)}, bf16[136,1024]{1,0:T(8,128)(2,1)S(1)}, u32[]{:S(2)}, u32[]{:S(2)}) collective-permute-start(bf16[136,1024]{1,0:T(8,128)(2,1)S(1)} %collective-permute-done.3.refs_3_), channel_id=1, source_target_pairs={{0,1},{1,0},{2,3},{3,2},{4,5},{5,4},{6,7},{7,6},{8,9},{9,8},{10,11... | collective-permute-start | bytes 835592 | tf_op jit(solution)/shard_map/ppermute | solution.py:333
  27.0 16.4 %collective-permute-start.7 = (bf16[136,1024]{1,0:T(8,128)(2,1)S(1)}, bf16[136,1024]{1,0:T(8,128)(2,1)S(1)}, u32[]{:S(2)}, u32[]{:S(2)}) collective-permute-start(bf16[136,1024]{1,0:T(8,128)(2,1)S(1)} %collective-permute-done.5.refs_5_), channel_id=1, source_target_pairs={{0,16},{16,32},{32,48},{48,64},{64,80},{80,96},{96,112},{112,0},{1... | collective-permute-start | bytes 835592 | tf_op jit(solution)/shard_map/ppermute | solution.py:337
  27.0 17.7 %collective-permute-start.6 = (bf16[136,1024]{1,0:T(8,128)(2,1)S(1)}, bf16[136,1024]{1,0:T(8,128)(2,1)S(1)}, u32[]{:S(2)}, u32[]{:S(2)}) collective-permute-start(bf16[136,1024]{1,0:T(8,128)(2,1)S(1)} %collective-permute-done.4.refs_4_), channel_id=1, source_target_pairs={{0,112},{16,0},{32,16},{48,32},{64,48},{80,64},{96,80},{112,96},{1... | collective-permute-start | bytes 835592 | tf_op jit(solution)/shard_map/ppermute | solution.py:337
  29.7 5.3 %collective-permute-start = (s32[16]{0:T(128)}, s32[16]{0:T(128)S(1)}, u32[]{:S(2)}, u32[]{:S(2)}) collective-permute-start(s32[16]{0:T(128)} %bitcast.19), channel_id=1, source_target_pairs={{0,0},{1,128},{16,16},{17,144},{32,32},{33,160},{48,48},{49,176},{... | collective-permute-start | bytes 200 | tf_op jit(solution)/shard_map/ppermute | solution.py:346
  35.0 7.8 %collective-permute-start.19 = (bf16[16,64,128]{2,1,0:T(8,128)(2,1)S(1)}, bf16[16,64,128]{2,1,0:T(8,128)(2,1)}, u32[]{:S(2)}, u32[]{:S(2)}) collective-permute-start(bf16[16,64,128]{2,1,0:T(8,128)(2,1)S(1)} %bitcast.18), channel_id=1, source_target_pairs={{0,0},{1,128},{16,16},{17,144},{32,32},{33,160},{48,48},{49,176},{... | collective-permute-start | bytes 786440 | tf_op jit(solution)/shard_map/ppermute | solution.py:346
  42.8 11.1 %collective-permute-start.11 = (bf16[136,1024]{1,0:T(8,128)(2,1)S(1)}, bf16[136,1024]{1,0:T(8,128)(2,1)S(1)}, u32[]{:S(2)}, u32[]{:S(2)}) collective-permute-start(bf16[136,1024]{1,0:T(8,128)(2,1)S(1)} %collective-permute-done.2.refs_2_), channel_id=1, source_target_pairs={{0,1},{1,0},{2,3},{3,2},{4,5},{5,4},{6,7},{7,6},{8,9},{9,8},{10,11... | collective-permute-start | bytes 835592 | tf_op jit(solution)/shard_map/ppermute | solution.py:333
  42.8 11.9 %collective-permute-start.10 = (bf16[136,1024]{1,0:T(8,128)(2,1)S(1)}, bf16[136,1024]{1,0:T(8,128)(2,1)S(1)}, u32[]{:S(2)}, u32[]{:S(2)}) collective-permute-start(bf16[136,1024]{1,0:T(8,128)(2,1)S(1)} %collective-permute-done.1.refs_1_), channel_id=1, source_target_pairs={{0,1},{1,0},{2,3},{3,2},{4,5},{5,4},{6,7},{7,6},{8,9},{9,8},{10,11... | collective-permute-start | bytes 835592 | tf_op jit(solution)/shard_map/ppermute | solution.py:333
  43.3 12.5 %collective-permute-start.14 = (bf16[136,1024]{1,0:T(8,128)(2,1)S(1)}, bf16[136,1024]{1,0:T(8,128)(2,1)}, u32[]{:S(2)}, u32[]{:S(2)}) collective-permute-start(bf16[136,1024]{1,0:T(8,128)(2,1)S(1)} %collective-permute-done.5.refs_5_), channel_id=1, source_target_pairs={{0,1},{1,0},{2,3},{3,2},{4,5},{5,4},{6,7},{7,6},{8,9},{9,8},{10,11... | collective-permute-start | bytes 835592 | tf_op jit(solution)/shard_map/ppermute | solution.py:333
  43.4 12.5 %collective-permute-start.8 = (bf16[136,1024]{1,0:T(8,128)(2,1)S(1)}, bf16[136,1024]{1,0:T(8,128)(2,1)}, u32[]{:S(2)}, u32[]{:S(2)}) collective-permute-start(bf16[136,1024]{1,0:T(8,128)(2,1)S(1)} %collective-permute-done.7.refs_7_), channel_id=1, source_target_pairs={{0,16},{16,32},{32,48},{48,64},{64,80},{80,96},{96,112},{112,0},{2... | collective-permute-start | bytes 835592 | tf_op jit(solution)/shard_map/ppermute | solution.py:360
  44.8 12.5 %collective-permute-start.9 = (bf16[136,1024]{1,0:T(8,128)(2,1)S(1)}, bf16[136,1024]{1,0:T(8,128)(2,1)}, u32[]{:S(2)}, u32[]{:S(2)}) collective-permute-start(bf16[136,1024]{1,0:T(8,128)(2,1)S(1)} %collective-permute-done.6.refs_6_), channel_id=1, source_target_pairs={{1,113},{17,1},{33,17},{49,33},{65,49},{81,65},{97,81},{113,97},{3... | collective-permute-start | bytes 835592 | tf_op jit(solution)/shard_map/ppermute | solution.py:361
  46.7 18.8 %all-to-all-start = ((bf16[16,64,128]{2,1,0:T(8,128)(2,1)}), bf16[16,64,128]{2,1,0:T(8,128)(2,1)S(1)}, u32[]{:S(2)}, u32[]{:S(2)}) async-start(bf16[16,64,128]{2,1,0:T(8,128)(2,1)} %collective-permute-done.19), calls=%async_computation | async-start | bytes 524288 | tf_op jit(solution)/shard_map/all_to_all | solution.py:385
  53.9 0.7 copy-start.1
  54.6 10.9 %collective-permute-start.13 = (bf16[136,1024]{1,0:T(8,128)(2,1)S(1)}, bf16[136,1024]{1,0:T(8,128)(2,1)}, u32[]{:S(2)}, u32[]{:S(2)}) collective-permute-start(bf16[136,1024]{1,0:T(8,128)(2,1)S(1)} %collective-permute-done.4.refs_4_), channel_id=1, source_target_pairs={{0,1},{1,0},{2,3},{3,2},{4,5},{5,4},{6,7},{7,6},{8,9},{9,8},{10,11... | collective-permute-start | bytes 835592 | tf_op jit(solution)/shard_map/ppermute | solution.py:333
  54.7 0.7 copy-start.3
  55.4 10.0 %collective-permute-start.16 = (bf16[136,1024]{1,0:T(8,128)(2,1)S(1)}, bf16[136,1024]{1,0:T(8,128)(2,1)}, u32[]{:S(2)}, u32[]{:S(2)}) collective-permute-start(bf16[136,1024]{1,0:T(8,128)(2,1)S(1)} %collective-permute-done.7.refs_7_), channel_id=1, source_target_pairs={{0,1},{1,0},{2,3},{3,2},{4,5},{5,4},{6,7},{7,6},{8,9},{9,8},{10,11... | collective-permute-start | bytes 835592 | tf_op jit(solution)/shard_map/ppermute | solution.py:333
  55.8 9.6 %collective-permute-start.15 = (bf16[136,1024]{1,0:T(8,128)(2,1)S(1)}, bf16[136,1024]{1,0:T(8,128)(2,1)}, u32[]{:S(2)}, u32[]{:S(2)}) collective-permute-start(bf16[136,1024]{1,0:T(8,128)(2,1)S(1)} %collective-permute-done.6.refs_6_), channel_id=1, source_target_pairs={{0,1},{1,0},{2,3},{3,2},{4,5},{5,4},{6,7},{7,6},{8,9},{9,8},{10,11... | collective-permute-start | bytes 835592 | tf_op jit(solution)/shard_map/ppermute | solution.py:333
  55.9 9.5 %collective-permute-start.17 = (bf16[136,1024]{1,0:T(8,128)(2,1)}, bf16[136,1024]{1,0:T(8,128)(2,1)}, u32[]{:S(2)}, u32[]{:S(2)}) collective-permute-start(bf16[136,1024]{1,0:T(8,128)(2,1)} %collective-permute-done.8.refs_8_), channel_id=1, source_target_pairs={{0,1},{2,3},{4,5},{6,7},{8,9},{10,11},{12,13},{14,15},{16,17},{18,... | collective-permute-start | bytes 835592 | tf_op jit(solution)/shard_map/ppermute | solution.py:383
  57.2 8.2 %collective-permute-start.18 = (bf16[136,1024]{1,0:T(8,128)(2,1)}, bf16[136,1024]{1,0:T(8,128)(2,1)}, u32[]{:S(2)}, u32[]{:S(2)}) collective-permute-start(bf16[136,1024]{1,0:T(8,128)(2,1)} %collective-permute-done.9.refs_9_), channel_id=1, source_target_pairs={{1,0},{3,2},{5,4},{7,6},{9,8},{11,10},{13,12},{15,14},{17,16},{19,... | collective-permute-start | bytes 835592 | tf_op jit(solution)/shard_map/ppermute | solution.py:384
  66.2 1.0 copy-start.2
  67.1 1.0 copy-start.4
  81.0 8.4 %copy-start.5 = (bf16[128,1024]{1,0:T(8,128)(2,1)}, bf16[128,1024]{1,0:T(8,128)(2,1)S(1)}, u32[]{:S(2)}) copy-start(bf16[128,1024]{1,0:T(8,128)(2,1)S(1)} %get-tuple-element.8.mine) | copy-start | bytes 786436
  81.0 5.4 %collective-permute-start.20 = (bf16[16,320,128]{2,1,0:T(8,128)(2,1)S(1)}, bf16[16,320,128]{2,1,0:T(8,128)(2,1)S(1)}, u32[]{:S(2)}, u32[]{:S(2)}) collective-permute-start(bf16[16,320,128]{2,1,0:T(8,128)(2,1)S(1)} %get-tuple-element.7.part), channel_id=1, source_target_pairs={{0,1},{1,0},{2,3},{3,2},{4,5},{5,4},{6,7},{7,6},{8,9},{9,8},{10,11... | collective-permute-start | bytes 3932168 | tf_op jit(solution)/shard_map/ppermute | solution.py:333
  89.4 35.5 %copy-start.6 = (bf16[128,1024]{1,0:T(8,128)(2,1)S(1)}, bf16[128,1024]{1,0:T(8,128)(2,1)}, u32[]{:S(2)}) copy-start(bf16[128,1024]{1,0:T(8,128)(2,1)} %copy-done.5) | copy-start | bytes 786436
  89.4 8.5 %collective-permute-start.22 = (bf16[8,32,384]{2,1,0:T(8,128)(2,1)S(1)}, bf16[8,32,384]{2,1,0:T(8,128)(2,1)S(1)}, u32[]{:S(2)}, u32[]{:S(2)}) collective-permute-start(bf16[8,32,384]{2,1,0:T(8,128)(2,1)S(1)} %get-tuple-element.10), channel_id=1, source_target_pairs={{0,0},{1,128},{16,16},{17,144},{32,32},{33,160},{48,48},{49,176},{... | collective-permute-start | bytes 589832 | tf_op jit(solution)/shard_map/ppermute | solution.py:346
  91.9 6.0 %collective-permute-start.23 = (bf16[8,32,384]{2,1,0:T(8,128)(2,1)S(1)}, bf16[8,32,384]{2,1,0:T(8,128)(2,1)S(1)}, u32[]{:S(2)}, u32[]{:S(2)}) collective-permute-start(bf16[8,32,384]{2,1,0:T(8,128)(2,1)S(1)} %get-tuple-element.11), channel_id=1, source_target_pairs={{0,1},{1,129},{16,17},{17,145},{32,33},{33,161},{48,49},{49,177},{... | collective-permute-start | bytes 589832 | tf_op jit(solution)/shard_map/ppermute | solution.py:346
  93.6 27.9 %all-to-all-start.1 = ((bf16[8,384,128]{2,1,0:T(8,128)(2,1)}), bf16[8,384,128]{2,1,0:T(8,128)(2,1)S(1)}, u32[]{:S(2)}, u32[]{:S(2)}) async-start(bf16[8,384,128]{2,1,0:T(8,128)(2,1)} %join_pass.1), calls=%async_computation.1 | async-start | bytes 1572864 | tf_op jit(solution)/shard_map/all_to_all | solution.py:390
  98.0 5.0 %collective-permute-start.24 = (bf16[8,32,384]{2,1,0:T(8,128)(2,1)S(1)}, bf16[8,32,384]{2,1,0:T(8,128)(2,1)S(1)}, u32[]{:S(2)}, u32[]{:S(2)}) collective-permute-start(bf16[8,32,384]{2,1,0:T(8,128)(2,1)S(1)} %add_convert_fusion.3), channel_id=1, source_target_pairs={{0,4},{4,0},{8,12},{12,8},{1,5},{5,1},{9,13},{13,9},{2,6},{6,2},{1... | collective-permute-start | bytes 589832 | tf_op jit(solution)/shard_map/ppermute | solution.py:333
  103.1 6.5 %collective-permute-start.25 = (bf16[8,32,384]{2,1,0:T(8,128)(2,1)S(1)}, bf16[8,32,384]{2,1,0:T(8,128)(2,1)S(1)}, u32[]{:S(2)}, u32[]{:S(2)}) collective-permute-start(bf16[8,32,384]{2,1,0:T(8,128)(2,1)S(1)} %add_convert_fusion.2), channel_id=1, source_target_pairs={{0,8},{4,12},{8,0},{12,4},{1,9},{5,13},{9,1},{13,5},{2,10},{6,14},... | collective-permute-start | bytes 589832 | tf_op jit(solution)/shard_map/ppermute | solution.py:333
  109.7 6.5 %collective-permute-start.26 = (bf16[8,32,384]{2,1,0:T(8,128)(2,1)S(1)}, bf16[8,32,384]{2,1,0:T(8,128)(2,1)S(1)}, u32[]{:S(2)}, u32[]{:S(2)}) collective-permute-start(bf16[8,32,384]{2,1,0:T(8,128)(2,1)S(1)} %add_convert_fusion.1), channel_id=1, source_target_pairs={{0,2},{2,0},{1,3},{3,1},{4,6},{6,4},{5,7},{7,5},{8,10},{10,8},{9,1... | collective-permute-start | bytes 589832 | tf_op jit(solution)/shard_map/ppermute | solution.py:333
  121.5 16.1 %all-to-all-start.2 = ((bf16[8,32,384]{2,1,0:T(8,128)(2,1)}), bf16[8,32,384]{2,1,0:T(8,128)(2,1)S(1)}, u32[]{:S(2)}, u32[]{:S(2)}) async-start(bf16[8,32,384]{2,1,0:T(8,128)(2,1)} %add_convert_fusion), calls=%async_computation.2 | async-start | bytes 393216 | tf_op jit(solution)/shard_map/all_to_all | solution.py:398
  124.9 2.8 %copy-start = (bf16[1024,3072]{1,0:T(8,128)(2,1)S(1)}, bf16[1024,3072]{1,0:T(8,128)(2,1)}, u32[]{:S(2)}) copy-start(bf16[1024,3072]{1,0:T(8,128)(2,1)} %w.1) | copy-start | bytes 18874372
  130.7 11.0 %collective-permute-start.21 = (bf16[128,1024]{1,0:T(8,128)(2,1)S(1)}, bf16[128,1024]{1,0:T(8,128)(2,1)S(1)}, u32[]{:S(2)}, u32[]{:S(2)}) collective-permute-start(bf16[128,1024]{1,0:T(8,128)(2,1)S(1)} %rows_pass.1), channel_id=1, source_target_pairs={{0,0},{1,128},{16,16},{17,144},{32,32},{33,160},{48,48},{49,176},{... | collective-permute-start | bytes 786440 | tf_op jit(solution)/shard_map/ppermute | solution.py:346
  137.6 1.5 %collective-permute-start.27 = (bf16[8,32,384]{2,1,0:T(8,128)(2,1)S(1)}, bf16[8,32,384]{2,1,0:T(8,128)(2,1)S(1)}, u32[]{:S(2)}, u32[]{:S(2)}) collective-permute-start(bf16[8,32,384]{2,1,0:T(8,128)(2,1)S(1)} %all-to-all-done.2.own), channel_id=1, source_target_pairs={{0,1},{1,0},{2,3},{3,2},{4,5},{5,4},{6,7},{7,6},{8,9},{9,8},{10,11... | collective-permute-start | bytes 589832 | tf_op jit(solution)/shard_map/ppermute | solution.py:333

commit v6 on v2

--- a/solution.py
+++ b/solution.py
@@ -187,51 +187,41 @@
     return first, second, both.astype(BF16)
 
 
-def weight_kernel(meta, normed, part, came, here, there, dw_s):
-    step = pl.program_id(0)
+def weight_kernel(meta, normed, part, came, here, there, grads):
     half = meta[NBLK + 1]
     y = meta[NBLK + 2]
-    first, second, both = total_of(part, came, half, slice(None))
-    dq = jnp.concatenate([first, second], axis=1).reshape(KROWS, HEAD)
-    dk = both[:, 0:BLOCK, :].reshape(KROWS, HEAD)
-    dv = both[:, BLOCK:, :].reshape(KROWS, HEAD)
-    grads = jnp.concatenate([dq, dk, dv], axis=1)
-    made = dot(normed[...].reshape(KROWS, D // 2), grads, 0, 0)
-
-    @pl.when(step == 0)
-    def _():
-        dw_s[...] = made
-
-    @pl.when(step > 0)
-    def _():
-        dw_s[...] += made
-
-    @pl.when(step == STEPS - 1)
-    def _():
-        every = dw_s[...].reshape(8, 2, 32, 3 * HEAD)
-        here[...] = jnp.where(y == 0, every[:, 0], every[:, 1]).astype(BF16)
-        there[...] = jnp.where(y == 0, every[:, 1], every[:, 0]).astype(BF16)
+    for b in range(NBLK):
+        first, second, both = total_of(part, came, half, b)
+        grads[b, 0:HALF, 0:HEAD] = first
+        grads[b, HALF:BLOCK, 0:HEAD] = second
+        grads[b, :, HEAD : 2 * HEAD] = both[0:BLOCK]
+        grads[b, :, 2 * HEAD :] = both[BLOCK:]
+    made = dot(normed[...].reshape(NBLK * BLOCK, D // 2), grads[...].reshape(NBLK * BLOCK, 3 * HEAD), 0, 0)
+    every = made.reshape(8, 2, 32, 3 * HEAD)
+    here[...] = jnp.where(y == 0, every[:, 0], every[:, 1]).astype(BF16)
+    there[...] = jnp.where(y == 0, every[:, 1], every[:, 0]).astype(BF16)
 
 
 def weight_pass(meta, normed, part, came):
-    pack = (4, HALF + 2 * BLOCK, HEAD)
+    pack = (NBLK, HALF + 2 * BLOCK, HEAD)
     shape = (8, 32, 3 * HEAD)
     grid_spec = pltpu.PrefetchScalarGridSpec(
         num_scalar_prefetch=1,
-        grid=(STEPS,),
+        grid=(1,),
         in_specs=[
-            pl.BlockSpec((4, BLOCK, D // 2), lambda i, m: (i, 0, m[NBLK + 1])),
-            pl.BlockSpec(pack, lambda i, m: (i, 0, 0)),
-            pl.BlockSpec(pack, lambda i, m: (i, 0, 0)),
+            pl.BlockSpec((NBLK, BLOCK, D // 2), lambda i, m: (0, 0, m[NBLK + 1])),
+            pl.BlockSpec(pack, lambda i, m: (0, 0, 0)),
+            pl.BlockSpec(pack, lambda i, m: (0, 0, 0)),
         ],
         out_specs=[pl.BlockSpec(shape, lambda i, m: (0, 0, 0))] * 2,
-        scratch_shapes=[pltpu.VMEM((D // 2, 3 * HEAD), F32)],
+        scratch_shapes=[pltpu.VMEM((NBLK, BLOCK, 3 * HEAD), BF16)],
     )
     return pl.pallas_call(
         weight_kernel,
         grid_spec=grid_spec,
         out_shape=[jax.ShapeDtypeStruct(shape, BF16)] * 2,
-        name="weight_pass", compiler_params=pltpu.CompilerParams(vmem_limit_bytes=10 * 1024 * 1024),
+        name="weight_pass",
+        compiler_params=pltpu.CompilerParams(vmem_limit_bytes=18 * 1024 * 1024),
     )(meta, normed, part, came)
 
 
@@ -353,7 +343,8 @@
         made += [down, up]
     far = ring(up[:HALF], "z", 1, 8)
     made.append(far)
-    made.append(ring(down[HALF:], "z", -1, 8))
+    far = ring(down[HALF:], "z", -1, 8)
+    made.append(far)
     return made
 
 

time: 136 us -> 135 us (level)
  no operation moved by 1% of the time
where the time goes in v6:
time: 135 us
  starting transfers between devices  64.5 us (48%)
  waiting for transfers between devices  37.8 us (28%)
  Pallas kernels  20 us (15%)
  local copies, waits for them, and re-layouts  8.77 us (6%)
  other arithmetic  2.55 us (2%)
    ppermute x8, starting transfers between devices, turn(): return lax.ppermute(x, ('y_lo', 'z', 'core'), pairs)  25.2 us
    ppermute x14, starting transfers between devices, flip(): return lax.ppermute(x, axis, [(i, i ^ bit) for i in range(size)])  17.4 us
    ppermute x14, waiting for transfers between devices, flip(): return lax.ppermute(x, axis, [(i, i ^ bit) for i in range(size)])  14.9 us
    pallas_call x1, Pallas kernels, head_pass(): pl.pallas_call(head_kernel, grid_spec=grid_spec, out_shape=[jax.ShapeDtyp...  12 us
    ppermute x6, starting transfers between devices, ring(): return lax.ppermute(x, axis, [(i, (i + by) % size) for i in range(size)])  9.93 us
    ppermute x8, waiting for transfers between devices, turn(): return lax.ppermute(x, ('y_lo', 'z', 'core'), pairs)  9.26 us
    ppermute x6, waiting for transfers between devices, ring(): return lax.ppermute(x, axis, [(i, (i + by) % size) for i in range(size)])  9.19 us
    unnamed x18, local copies, waits for them, and re-layouts  7.11 us
  transfers between devices with their start and end apart: 31, of which 14 were waited for; matrix products, arithmetic and copies ran while one was open for 2% of the time, Pallas kernels for 4%

profile of v6, /device:TPU:1, one launch (start us, length us, event | category | flops | bytes accessed | tf_op | source)
XLA Modules:
  0.0 134.5 jit_solution(7488205793442316025)
XLA Ops:
  0.7 0.7 convert_reduce_fusion
  1.7 1.0 fusion.1
  2.7 8.0 %collective-permute-start.2 = (bf16[136,1024]{1,0:T(8,128)(2,1)S(1)}, bf16[136,1024]{1,0:T(8,128)(2,1)S(1)}, u32[]{:S(2)}, u32[]{:S(2)}) collective-permute-start(bf16[136,1024]{1,0:T(8,128)(2,1)S(1)} %fusion.1), channel_id=1, source_target_pairs={{0,112},{1,240},{16,0},{17,128},{32,16},{33,144},{48,32},{49,160},... | collective-permute-start | bytes 835592 | tf_op jit(solution)/shard_map/ppermute | solution.py:330
  10.7 6.0 %collective-permute-done.2.refs_2_ = bf16[136,1024]{1,0:T(8,128)(2,1)S(1)} collective-permute-done((bf16[136,1024]{1,0:T(8,128)(2,1)S(1)}, bf16[136,1024]{1,0:T(8,128)(2,1)S(1)}, u32[]{:S(2)}, u32[]{:S(2)}) %collective-permute-start.2) | collective-permute-done | bytes 278560 | tf_op jit(solution)/shard_map/ppermute | solution.py:330
  16.7 4.0 %collective-permute-start.4 = (bf16[136,1024]{1,0:T(8,128)(2,1)S(1)}, bf16[136,1024]{1,0:T(8,128)(2,1)S(1)}, u32[]{:S(2)}, u32[]{:S(2)}) collective-permute-start(bf16[136,1024]{1,0:T(8,128)(2,1)S(1)} %collective-permute-done.2.refs_2_), channel_id=1, source_target_pairs={{0,112},{16,0},{32,16},{48,32},{64,48},{80,64},{96,80},{112,96},{1... | collective-permute-start | bytes 835592 | tf_op jit(solution)/shard_map/ppermute | solution.py:321
  20.8 3.1 %collective-permute-start.1 = (bf16[136,1024]{1,0:T(8,128)(2,1)S(1)}, bf16[136,1024]{1,0:T(8,128)(2,1)S(1)}, u32[]{:S(2)}, u32[]{:S(2)}) collective-permute-start(bf16[136,1024]{1,0:T(8,128)(2,1)S(1)} %fusion.1), channel_id=1, source_target_pairs={{0,0},{1,128},{16,16},{17,144},{32,32},{33,160},{48,48},{49,176},{... | collective-permute-start | bytes 835592 | tf_op jit(solution)/shard_map/ppermute | solution.py:330
  23.8 3.3 %collective-permute-done.4.refs_4_ = bf16[136,1024]{1,0:T(8,128)(2,1)S(1)} collective-permute-done((bf16[136,1024]{1,0:T(8,128)(2,1)S(1)}, bf16[136,1024]{1,0:T(8,128)(2,1)S(1)}, u32[]{:S(2)}, u32[]{:S(2)}) %collective-permute-start.4) | collective-permute-done | bytes 278560 | tf_op jit(solution)/shard_map/ppermute | solution.py:321
  27.1 3.2 %collective-permute-start.6 = (bf16[136,1024]{1,0:T(8,128)(2,1)S(1)}, bf16[136,1024]{1,0:T(8,128)(2,1)S(1)}, u32[]{:S(2)}, u32[]{:S(2)}) collective-permute-start(bf16[136,1024]{1,0:T(8,128)(2,1)S(1)} %collective-permute-done.4.refs_4_), channel_id=1, source_target_pairs={{0,112},{16,0},{32,16},{48,32},{64,48},{80,64},{96,80},{112,96},{1... | collective-permute-start | bytes 835592 | tf_op jit(solution)/shard_map/ppermute | solution.py:321
  30.3 1.0 copy.9
  31.3 1.9 %collective-permute-start.19 = (bf16[16,64,128]{2,1,0:T(8,128)(2,1)S(1)}, bf16[16,64,128]{2,1,0:T(8,128)(2,1)}, u32[]{:S(2)}, u32[]{:S(2)}) collective-permute-start(bf16[16,64,128]{2,1,0:T(8,128)(2,1)S(1)} %bitcast.18), channel_id=1, source_target_pairs={{0,0},{1,128},{16,16},{17,144},{32,32},{33,160},{48,48},{49,176},{... | collective-permute-start | bytes 786440 | tf_op jit(solution)/shard_map/ppermute | solution.py:330
  33.3 3.6 %collective-permute-start = (s32[16]{0:T(128)}, s32[16]{0:T(128)S(1)}, u32[]{:S(2)}, u32[]{:S(2)}) collective-permute-start(s32[16]{0:T(128)} %bitcast.19), channel_id=1, source_target_pairs={{0,0},{1,128},{16,16},{17,144},{32,32},{33,160},{48,48},{49,176},{... | collective-permute-start | bytes 200 | tf_op jit(solution)/shard_map/ppermute | solution.py:330
  36.9 2.2 %collective-permute-done = s32[16]{0:T(128)S(1)} collective-permute-done((s32[16]{0:T(128)}, s32[16]{0:T(128)S(1)}, u32[]{:S(2)}, u32[]{:S(2)}) %collective-permute-start) | collective-permute-done | bytes 96 | tf_op jit(solution)/shard_map/ppermute | solution.py:330
  40.3 4.5 %all-to-all-start = ((bf16[16,64,128]{2,1,0:T(8,128)(2,1)}), bf16[16,64,128]{2,1,0:T(8,128)(2,1)S(1)}, u32[]{:S(2)}, u32[]{:S(2)}) async-start(bf16[16,64,128]{2,1,0:T(8,128)(2,1)} %collective-permute-done.19), calls=%async_computation | async-start | bytes 524288 | tf_op jit(solution)/shard_map/all_to_all | solution.py:369
  44.8 2.6 %collective-permute-start.9 = (bf16[72,1024]{1,0:T(8,128)(2,1)S(1)}, bf16[72,1024]{1,0:T(8,128)(2,1)S(1)}, u32[]{:S(2)}, u32[]{:S(2)}) collective-permute-start(bf16[72,1024]{1,0:T(8,128)(2,1)S(1)} %slice.9), channel_id=1, source_target_pairs={{0,112},{16,0},{32,16},{48,32},{64,48},{80,64},{96,80},{112,96},{1... | collective-permute-start | bytes 442376 | tf_op jit(solution)/shard_map/ppermute | solution.py:321
  47.5 0.7 collective-permute-start.13
  48.1 0.9 collective-permute-done.7.refs_7_
  49.0 2.6 %collective-permute-start.16 = (bf16[136,1024]{1,0:T(8,128)(2,1)S(1)}, bf16[136,1024]{1,0:T(8,128)(2,1)}, u32[]{:S(2)}, u32[]{:S(2)}) collective-permute-start(bf16[136,1024]{1,0:T(8,128)(2,1)S(1)} %collective-permute-done.7.refs_7_), channel_id=1, source_target_pairs={{0,1},{1,0},{2,3},{3,2},{4,5},{5,4},{6,7},{7,6},{8,9},{9,8},{10,11... | collective-permute-start | bytes 835592 | tf_op jit(solution)/shard_map/ppermute | solution.py:317
  51.6 0.7 copy-done.3
  52.4 3.4 %collective-permute-done.9.refs_9_ = bf16[72,1024]{1,0:T(8,128)(2,1)S(1)} collective-permute-done((bf16[72,1024]{1,0:T(8,128)(2,1)S(1)}, bf16[72,1024]{1,0:T(8,128)(2,1)S(1)}, u32[]{:S(2)}, u32[]{:S(2)}) %collective-permute-start.9) | collective-permute-done | bytes 147488 | tf_op jit(solution)/shard_map/ppermute | solution.py:321
  55.8 1.0 collective-permute-start.18
  56.8 1.6 %collective-permute-done.8.refs_8_ = bf16[64,1024]{1,0:T(8,128)(2,1)} collective-permute-done((bf16[64,1024]{1,0:T(8,128)(2,1)S(1)}, bf16[64,1024]{1,0:T(8,128)(2,1)}, u32[]{:S(2)}, u32[]{:S(2)}) %collective-permute-start.8) | collective-permute-done | bytes 131104 | tf_op jit(solution)/shard_map/ppermute | solution.py:321
  58.4 1.3 collective-permute-start.17
  59.7 1.2 constant_dynamic-slice_fusion
  61.1 0.9 copy-done.2
  62.0 1.0 copy-done.4
  63.0 12.0 %head_pass.1 = (bf16[16,128,1024]{2,1,0:T(8,128)(2,1)S(1)}, bf16[128,1024]{1,0:T(8,128)(2,1)S(1)}, bf16[16,320,128]{2,1,0:T(8,128)(2,1)S(1)}) custom-call(s32[20]{0:T(128)S(1)} %concatenate.6.refs_0_.meta, bf16[136,1024]{1,0:T(8,128)(2,1)S(1)} %collective-permute-done.1.refs_1_, bf16[136,1024]{1,0:T(8,128)(2,1)S(1)} %collective-permute-done.2.refs_2_, ...), custom_call_target="tpu_custom_call" | custom-call | tf_op jit(solution)/shard_map/head_pass/pallas_call | solution.py:169
  75.0 3.3 %collective-permute-start.20 = (bf16[16,320,128]{2,1,0:T(8,128)(2,1)S(1)}, bf16[16,320,128]{2,1,0:T(8,128)(2,1)S(1)}, u32[]{:S(2)}, u32[]{:S(2)}) collective-permute-start(bf16[16,320,128]{2,1,0:T(8,128)(2,1)S(1)} %get-tuple-element.7.part), channel_id=1, source_target_pairs={{0,1},{1,0},{2,3},{3,2},{4,5},{5,4},{6,7},{7,6},{8,9},{9,8},{10,11... | collective-permute-start | bytes 3932168 | tf_op jit(solution)/shard_map/ppermute | solution.py:317
  78.2 2.7 %collective-permute-done.20.came = bf16[16,320,128]{2,1,0:T(8,128)(2,1)S(1)} collective-permute-done((bf16[16,320,128]{2,1,0:T(8,128)(2,1)S(1)}, bf16[16,320,128]{2,1,0:T(8,128)(2,1)S(1)}, u32[]{:S(2)}, u32[]{:S(2)}) %collective-permute-start.20) | collective-permute-done | bytes 1310752 | tf_op jit(solution)/shard_map/ppermute | solution.py:317
  80.9 2.0 %weight_pass.1 = (bf16[8,32,384]{2,1,0:T(8,128)(2,1)S(1)}, bf16[8,32,384]{2,1,0:T(8,128)(2,1)S(1)}) custom-call(s32[20]{0:T(128)S(1)} %concatenate.6.refs_0_.meta, bf16[16,128,1024]{2,1,0:T(8,128)(2,1)S(1)} %get-tuple-element.9.normed, bf16[16,320,128]{2,1,0:T(8,128)(2,1)S(1)} %get-tuple-element.7.part, bf16[16,320,128]{2,1,0:T(8,128)(2,1)S(1)} %collective-permute-done.20.came), custom_call_target="tpu_custom_call" | custom-call | tf_op jit(solution)/shard_map/weight_pass/pallas_call | solution.py:219
  82.9 2.1 %collective-permute-start.22 = (bf16[8,32,384]{2,1,0:T(8,128)(2,1)S(1)}, bf16[8,32,384]{2,1,0:T(8,128)(2,1)S(1)}, u32[]{:S(2)}, u32[]{:S(2)}) collective-permute-start(bf16[8,32,384]{2,1,0:T(8,128)(2,1)S(1)} %get-tuple-element.10), channel_id=1, source_target_pairs={{0,0},{1,128},{16,16},{17,144},{32,32},{33,160},{48,48},{49,176},{... | collective-permute-start | bytes 589832 | tf_op jit(solution)/shard_map/ppermute | solution.py:330
  85.1 1.6 %join_pass.1 = bf16[8,384,128]{2,1,0:T(8,128)(2,1)} custom-call(s32[20]{0:T(128)S(1)} %concatenate.6.refs_0_.meta, bf16[16,320,128]{2,1,0:T(8,128)(2,1)S(1)} %get-tuple-element.7.part, bf16[16,320,128]{2,1,0:T(8,128)(2,1)S(1)} %collective-permute-done.20.came), custom_call_target="tpu_custom_call" | custom-call | tf_op jit(solution)/shard_map/join_pass/pallas_call | solution.py:246
  86.6 4.0 %all-to-all-start.1 = ((bf16[8,384,128]{2,1,0:T(8,128)(2,1)}), bf16[8,384,128]{2,1,0:T(8,128)(2,1)S(1)}, u32[]{:S(2)}, u32[]{:S(2)}) async-start(bf16[8,384,128]{2,1,0:T(8,128)(2,1)} %join_pass.1), calls=%async_computation.1 | async-start | bytes 1572864 | tf_op jit(solution)/shard_map/all_to_all | solution.py:374
  90.7 1.3 collective-permute-start.24
  92.0 3.6 %collective-permute-done.24 = bf16[8,32,384]{2,1,0:T(8,128)(2,1)S(1)} collective-permute-done((bf16[8,32,384]{2,1,0:T(8,128)(2,1)S(1)}, bf16[8,32,384]{2,1,0:T(8,128)(2,1)S(1)}, u32[]{:S(2)}, u32[]{:S(2)}) %collective-permute-start.24) | collective-permute-done | bytes 196640 | tf_op jit(solution)/shard_map/ppermute | solution.py:317
  95.6 2.4 %collective-permute-start.25 = (bf16[8,32,384]{2,1,0:T(8,128)(2,1)S(1)}, bf16[8,32,384]{2,1,0:T(8,128)(2,1)S(1)}, u32[]{:S(2)}, u32[]{:S(2)}) collective-permute-start(bf16[8,32,384]{2,1,0:T(8,128)(2,1)S(1)} %add_convert_fusion.2), channel_id=1, source_target_pairs={{0,8},{4,12},{8,0},{12,4},{1,9},{5,13},{9,1},{13,5},{2,10},{6,14},... | collective-permute-start | bytes 589832 | tf_op jit(solution)/shard_map/ppermute | solution.py:317
  98.1 4.3 %collective-permute-done.25 = bf16[8,32,384]{2,1,0:T(8,128)(2,1)S(1)} collective-permute-done((bf16[8,32,384]{2,1,0:T(8,128)(2,1)S(1)}, bf16[8,32,384]{2,1,0:T(8,128)(2,1)S(1)}, u32[]{:S(2)}, u32[]{:S(2)}) %collective-permute-start.25) | collective-permute-done | bytes 196640 | tf_op jit(solution)/shard_map/ppermute | solution.py:317
  102.5 3.5 %collective-permute-start.26 = (bf16[8,32,384]{2,1,0:T(8,128)(2,1)S(1)}, bf16[8,32,384]{2,1,0:T(8,128)(2,1)S(1)}, u32[]{:S(2)}, u32[]{:S(2)}) collective-permute-start(bf16[8,32,384]{2,1,0:T(8,128)(2,1)S(1)} %add_convert_fusion.1), channel_id=1, source_target_pairs={{0,2},{2,0},{1,3},{3,1},{4,6},{6,4},{5,7},{7,5},{8,10},{10,8},{9,1... | collective-permute-start | bytes 589832 | tf_op jit(solution)/shard_map/ppermute | solution.py:317
  105.9 3.1 %collective-permute-done.26 = bf16[8,32,384]{2,1,0:T(8,128)(2,1)S(1)} collective-permute-done((bf16[8,32,384]{2,1,0:T(8,128)(2,1)S(1)}, bf16[8,32,384]{2,1,0:T(8,128)(2,1)S(1)}, u32[]{:S(2)}, u32[]{:S(2)}) %collective-permute-start.26) | collective-permute-done | bytes 196640 | tf_op jit(solution)/shard_map/ppermute | solution.py:317
  109.0 0.7 add_convert_fusion
  109.7 4.5 %all-to-all-done.1.back = bf16[8,384,128]{2,1,0:T(8,128)(2,1)S(1)} async-done(((bf16[8,384,128]{2,1,0:T(8,128)(2,1)}), bf16[8,384,128]{2,1,0:T(8,128)(2,1)S(1)}, u32[]{:S(2)}, u32[]{:S(2)}) %all-to-all-start.1) | async-done | bytes 786464 | tf_op jit(solution)/shard_map/all_to_all | solution.py:374
  114.2 3.4 %all-to-all-start.2 = ((bf16[8,32,384]{2,1,0:T(8,128)(2,1)}), bf16[8,32,384]{2,1,0:T(8,128)(2,1)S(1)}, u32[]{:S(2)}, u32[]{:S(2)}) async-start(bf16[8,32,384]{2,1,0:T(8,128)(2,1)} %add_convert_fusion), calls=%async_computation.2 | async-start | bytes 393216 | tf_op jit(solution)/shard_map/all_to_all | solution.py:382
  117.6 2.8 %copy-done = bf16[1024,3072]{1,0:T(8,128)(2,1)S(1)} copy-done((bf16[1024,3072]{1,0:T(8,128)(2,1)S(1)}, bf16[1024,3072]{1,0:T(8,128)(2,1)}, u32[]{:S(2)}) %copy-start) | copy-done | bytes 6291480
  120.4 2.9 %rows_pass.1 = bf16[128,1024]{1,0:T(8,128)(2,1)S(1)} custom-call(bf16[8,384,128]{2,1,0:T(8,128)(2,1)S(1)} %all-to-all-done.1.back, bf16[128,1024]{1,0:T(8,128)(2,1)S(1)} %copy-done.6, f32[8,1024]{1,0:T(8,128)S(1)} %broadcast_in_dim.4.refs_20_.gain, bf16[1024,3072]{1,0:T(8,128)(2,1)S(1)} %copy-done), custom_call_target="tpu_custom_call" | custom-call | tf_op jit(solution)/shard_map/rows_pass/pallas_call | solution.py:274
  123.3 6.4 %collective-permute-start.21 = (bf16[128,1024]{1,0:T(8,128)(2,1)S(1)}, bf16[128,1024]{1,0:T(8,128)(2,1)S(1)}, u32[]{:S(2)}, u32[]{:S(2)}) collective-permute-start(bf16[128,1024]{1,0:T(8,128)(2,1)S(1)} %rows_pass.1), channel_id=1, source_target_pairs={{0,0},{1,128},{16,16},{17,144},{32,32},{33,160},{48,48},{49,176},{... | collective-permute-start | bytes 786440 | tf_op jit(solution)/shard_map/ppermute | solution.py:330
  130.2 1.1 collective-permute-done.27.other
  131.3 1.5 %final_pass.1 = f32[64,3072]{1,0:T(8,128)} custom-call(s32[20]{0:T(128)S(1)} %concatenate.6.refs_0_.meta, bf16[8,32,384]{2,1,0:T(8,128)(2,1)S(1)} %all-to-all-done.2.own, bf16[8,32,384]{2,1,0:T(8,128)(2,1)S(1)} %collective-permute-done.27.other), custom_call_target="tpu_custom_call" | custom-call | tf_op jit(solution)/shard_map/final_pass/pallas_call | solution.py:311
  132.8 1.0 collective-permute-done.21
  133.8 0.7 copy.11
  (56 shorter events, 2.5 us)
Async XLA Ops:
  0.6 60.4 %copy-start.7 = (f32[1024]{0:T(1024)S(1)}, f32[1024]{0:T(1024)}, u32[]{:S(2)}) copy-start(f32[1024]{0:T(1024)} %param.9) | copy-start | bytes 12292
  2.7 14.1 %collective-permute-start.2 = (bf16[136,1024]{1,0:T(8,128)(2,1)S(1)}, bf16[136,1024]{1,0:T(8,128)(2,1)S(1)}, u32[]{:S(2)}, u32[]{:S(2)}) collective-permute-start(bf16[136,1024]{1,0:T(8,128)(2,1)S(1)} %fusion.1), channel_id=1, source_target_pairs={{0,112},{1,240},{16,0},{17,128},{32,16},{33,144},{48,32},{49,160},... | collective-permute-start | bytes 835592 | tf_op jit(solution)/shard_map/ppermute | solution.py:330
  10.7 10.0 %collective-permute-start.3 = (bf16[136,1024]{1,0:T(8,128)(2,1)S(1)}, bf16[136,1024]{1,0:T(8,128)(2,1)S(1)}, u32[]{:S(2)}, u32[]{:S(2)}) collective-permute-start(bf16[136,1024]{1,0:T(8,128)(2,1)S(1)} %fusion.1), channel_id=1, source_target_pairs={{0,16},{1,144},{16,32},{17,160},{32,48},{33,176},{48,64},{49,192},... | collective-permute-start | bytes 835592 | tf_op jit(solution)/shard_map/ppermute | solution.py:330
  16.7 10.3 %collective-permute-start.4 = (bf16[136,1024]{1,0:T(8,128)(2,1)S(1)}, bf16[136,1024]{1,0:T(8,128)(2,1)S(1)}, u32[]{:S(2)}, u32[]{:S(2)}) collective-permute-start(bf16[136,1024]{1,0:T(8,128)(2,1)S(1)} %collective-permute-done.2.refs_2_), channel_id=1, source_target_pairs={{0,112},{16,0},{32,16},{48,32},{64,48},{80,64},{96,80},{112,96},{1... | collective-permute-start | bytes 835592 | tf_op jit(solution)/shard_map/ppermute | solution.py:321
  20.7 18.9 %collective-permute-start.5 = (bf16[136,1024]{1,0:T(8,128)(2,1)S(1)}, bf16[136,1024]{1,0:T(8,128)(2,1)S(1)}, u32[]{:S(2)}, u32[]{:S(2)}) collective-permute-start(bf16[136,1024]{1,0:T(8,128)(2,1)S(1)} %collective-permute-done.3.refs_3_), channel_id=1, source_target_pairs={{0,16},{16,32},{32,48},{48,64},{64,80},{80,96},{96,112},{112,0},{1... | collective-permute-start | bytes 835592 | tf_op jit(solution)/shard_map/ppermute | solution.py:321
  20.8 18.9 %collective-permute-start.1 = (bf16[136,1024]{1,0:T(8,128)(2,1)S(1)}, bf16[136,1024]{1,0:T(8,128)(2,1)S(1)}, u32[]{:S(2)}, u32[]{:S(2)}) collective-permute-start(bf16[136,1024]{1,0:T(8,128)(2,1)S(1)} %fusion.1), channel_id=1, source_target_pairs={{0,0},{1,128},{16,16},{17,144},{32,32},{33,160},{48,48},{49,176},{... | collective-permute-start | bytes 835592 | tf_op jit(solution)/shard_map/ppermute | solution.py:330
  27.1 12.8 %collective-permute-start.6 = (bf16[136,1024]{1,0:T(8,128)(2,1)S(1)}, bf16[136,1024]{1,0:T(8,128)(2,1)S(1)}, u32[]{:S(2)}, u32[]{:S(2)}) collective-permute-start(bf16[136,1024]{1,0:T(8,128)(2,1)S(1)} %collective-permute-done.4.refs_4_), channel_id=1, source_target_pairs={{0,112},{16,0},{32,16},{48,32},{64,48},{80,64},{96,80},{112,96},{1... | collective-permute-start | bytes 835592 | tf_op jit(solution)/shard_map/ppermute | solution.py:321
  31.3 7.8 %collective-permute-start.19 = (bf16[16,64,128]{2,1,0:T(8,128)(2,1)S(1)}, bf16[16,64,128]{2,1,0:T(8,128)(2,1)}, u32[]{:S(2)}, u32[]{:S(2)}) collective-permute-start(bf16[16,64,128]{2,1,0:T(8,128)(2,1)S(1)} %bitcast.18), channel_id=1, source_target_pairs={{0,0},{1,128},{16,16},{17,144},{32,32},{33,160},{48,48},{49,176},{... | collective-permute-start | bytes 786440 | tf_op jit(solution)/shard_map/ppermute | solution.py:330
  33.3 5.9 %collective-permute-start = (s32[16]{0:T(128)}, s32[16]{0:T(128)S(1)}, u32[]{:S(2)}, u32[]{:S(2)}) collective-permute-start(s32[16]{0:T(128)} %bitcast.19), channel_id=1, source_target_pairs={{0,0},{1,128},{16,16},{17,144},{32,32},{33,160},{48,48},{49,176},{... | collective-permute-start | bytes 200 | tf_op jit(solution)/shard_map/ppermute | solution.py:330
  39.1 5.7 %collective-permute-start.12 = (bf16[136,1024]{1,0:T(8,128)(2,1)S(1)}, bf16[136,1024]{1,0:T(8,128)(2,1)S(1)}, u32[]{:S(2)}, u32[]{:S(2)}) collective-permute-start(bf16[136,1024]{1,0:T(8,128)(2,1)S(1)} %collective-permute-done.3.refs_3_), channel_id=1, source_target_pairs={{0,1},{1,0},{2,3},{3,2},{4,5},{5,4},{6,7},{7,6},{8,9},{9,8},{10,11... | collective-permute-start | bytes 835592 | tf_op jit(solution)/shard_map/ppermute | solution.py:317
  39.1 8.3 %collective-permute-start.11 = (bf16[136,1024]{1,0:T(8,128)(2,1)S(1)}, bf16[136,1024]{1,0:T(8,128)(2,1)S(1)}, u32[]{:S(2)}, u32[]{:S(2)}) collective-permute-start(bf16[136,1024]{1,0:T(8,128)(2,1)S(1)} %collective-permute-done.2.refs_2_), channel_id=1, source_target_pairs={{0,1},{1,0},{2,3},{3,2},{4,5},{5,4},{6,7},{7,6},{8,9},{9,8},{10,11... | collective-permute-start | bytes 835592 | tf_op jit(solution)/shard_map/ppermute | solution.py:317
  39.7 9.3 %collective-permute-start.7 = (bf16[136,1024]{1,0:T(8,128)(2,1)S(1)}, bf16[136,1024]{1,0:T(8,128)(2,1)S(1)}, u32[]{:S(2)}, u32[]{:S(2)}) collective-permute-start(bf16[136,1024]{1,0:T(8,128)(2,1)S(1)} %collective-permute-done.5.refs_5_), channel_id=1, source_target_pairs={{0,16},{16,32},{32,48},{48,64},{64,80},{80,96},{96,112},{112,0},{1... | collective-permute-start | bytes 835592 | tf_op jit(solution)/shard_map/ppermute | solution.py:321
  39.7 11.9 %collective-permute-start.10 = (bf16[136,1024]{1,0:T(8,128)(2,1)S(1)}, bf16[136,1024]{1,0:T(8,128)(2,1)S(1)}, u32[]{:S(2)}, u32[]{:S(2)}) collective-permute-start(bf16[136,1024]{1,0:T(8,128)(2,1)S(1)} %collective-permute-done.1.refs_1_), channel_id=1, source_target_pairs={{0,1},{1,0},{2,3},{3,2},{4,5},{5,4},{6,7},{7,6},{8,9},{9,8},{10,11... | collective-permute-start | bytes 835592 | tf_op jit(solution)/shard_map/ppermute | solution.py:317
  39.9 12.4 %collective-permute-start.14 = (bf16[136,1024]{1,0:T(8,128)(2,1)S(1)}, bf16[136,1024]{1,0:T(8,128)(2,1)}, u32[]{:S(2)}, u32[]{:S(2)}) collective-permute-start(bf16[136,1024]{1,0:T(8,128)(2,1)S(1)} %collective-permute-done.5.refs_5_), channel_id=1, source_target_pairs={{0,1},{1,0},{2,3},{3,2},{4,5},{5,4},{6,7},{7,6},{8,9},{9,8},{10,11... | collective-permute-start | bytes 835592 | tf_op jit(solution)/shard_map/ppermute | solution.py:317
  40.3 20.7 %all-to-all-start = ((bf16[16,64,128]{2,1,0:T(8,128)(2,1)}), bf16[16,64,128]{2,1,0:T(8,128)(2,1)S(1)}, u32[]{:S(2)}, u32[]{:S(2)}) async-start(bf16[16,64,128]{2,1,0:T(8,128)(2,1)} %collective-permute-done.19), calls=%async_computation | async-start | bytes 524288 | tf_op jit(solution)/shard_map/all_to_all | solution.py:369
  44.8 11.0 %collective-permute-start.9 = (bf16[72,1024]{1,0:T(8,128)(2,1)S(1)}, bf16[72,1024]{1,0:T(8,128)(2,1)S(1)}, u32[]{:S(2)}, u32[]{:S(2)}) collective-permute-start(bf16[72,1024]{1,0:T(8,128)(2,1)S(1)} %slice.9), channel_id=1, source_target_pairs={{0,112},{16,0},{32,16},{48,32},{64,48},{80,64},{96,80},{112,96},{1... | collective-permute-start | bytes 442376 | tf_op jit(solution)/shard_map/ppermute | solution.py:321
  47.5 10.9 %copy-start.1 = (bf16[136,1024]{1,0:T(8,128)(2,1)}, bf16[136,1024]{1,0:T(8,128)(2,1)S(1)}, u32[]{:S(2)}) copy-start(bf16[136,1024]{1,0:T(8,128)(2,1)S(1)} %collective-permute-done.11.refs_11_) | copy-start | bytes 835588
  47.5 13.5 %collective-permute-start.13 = (bf16[136,1024]{1,0:T(8,128)(2,1)S(1)}, bf16[136,1024]{1,0:T(8,128)(2,1)}, u32[]{:S(2)}, u32[]{:S(2)}) collective-permute-start(bf16[136,1024]{1,0:T(8,128)(2,1)S(1)} %collective-permute-done.4.refs_4_), channel_id=1, source_target_pairs={{0,1},{1,0},{2,3},{3,2},{4,5},{5,4},{6,7},{7,6},{8,9},{9,8},{10,11... | collective-permute-start | bytes 835592 | tf_op jit(solution)/shard_map/ppermute | solution.py:317
  49.0 12.0 %collective-permute-start.16 = (bf16[136,1024]{1,0:T(8,128)(2,1)S(1)}, bf16[136,1024]{1,0:T(8,128)(2,1)}, u32[]{:S(2)}, u32[]{:S(2)}) collective-permute-start(bf16[136,1024]{1,0:T(8,128)(2,1)S(1)} %collective-permute-done.7.refs_7_), channel_id=1, source_target_pairs={{0,1},{1,0},{2,3},{3,2},{4,5},{5,4},{6,7},{7,6},{8,9},{9,8},{10,11... | collective-permute-start | bytes 835592 | tf_op jit(solution)/shard_map/ppermute | solution.py:317
  51.6 0.7 copy-start.3
  52.3 8.8 %collective-permute-start.15 = (bf16[136,1024]{1,0:T(8,128)(2,1)S(1)}, bf16[136,1024]{1,0:T(8,128)(2,1)}, u32[]{:S(2)}, u32[]{:S(2)}) collective-permute-start(bf16[136,1024]{1,0:T(8,128)(2,1)S(1)} %collective-permute-done.6.refs_6_), channel_id=1, source_target_pairs={{0,1},{1,0},{2,3},{3,2},{4,5},{5,4},{6,7},{7,6},{8,9},{9,8},{10,11... | collective-permute-start | bytes 835592 | tf_op jit(solution)/shard_map/ppermute | solution.py:317
  52.3 6.1 %collective-permute-start.8 = (bf16[64,1024]{1,0:T(8,128)(2,1)S(1)}, bf16[64,1024]{1,0:T(8,128)(2,1)}, u32[]{:S(2)}, u32[]{:S(2)}) collective-permute-start(bf16[64,1024]{1,0:T(8,128)(2,1)S(1)} %slice.8), channel_id=1, source_target_pairs={{0,16},{16,32},{32,48},{48,64},{64,80},{80,96},{96,112},{112,0},{1... | collective-permute-start | bytes 393224 | tf_op jit(solution)/shard_map/ppermute | solution.py:321
  55.8 5.2 %collective-permute-start.18 = (bf16[72,1024]{1,0:T(8,128)(2,1)S(1)}, bf16[72,1024]{1,0:T(8,128)(2,1)}, u32[]{:S(2)}, u32[]{:S(2)}) collective-permute-start(bf16[72,1024]{1,0:T(8,128)(2,1)S(1)} %collective-permute-done.9.refs_9_), channel_id=1, source_target_pairs={{0,1},{1,0},{2,3},{3,2},{4,5},{5,4},{6,7},{7,6},{8,9},{9,8},{10,11... | collective-permute-start | bytes 442376 | tf_op jit(solution)/shard_map/ppermute | solution.py:317
  58.4 2.6 %collective-permute-start.17 = (bf16[64,1024]{1,0:T(8,128)(2,1)}, bf16[64,1024]{1,0:T(8,128)(2,1)}, u32[]{:S(2)}, u32[]{:S(2)}) collective-permute-start(bf16[64,1024]{1,0:T(8,128)(2,1)} %collective-permute-done.8.refs_8_), channel_id=1, source_target_pairs={{0,1},{1,0},{2,3},{3,2},{4,5},{5,4},{6,7},{7,6},{8,9},{9,8},{10,11... | collective-permute-start | bytes 393224 | tf_op jit(solution)/shard_map/ppermute | solution.py:317
  61.0 1.0 copy-start.2
  62.0 1.0 copy-start.4
  75.0 7.9 %copy-start.5 = (bf16[128,1024]{1,0:T(8,128)(2,1)}, bf16[128,1024]{1,0:T(8,128)(2,1)S(1)}, u32[]{:S(2)}) copy-start(bf16[128,1024]{1,0:T(8,128)(2,1)S(1)} %get-tuple-element.8.mine) | copy-start | bytes 786436
  75.0 5.9 %collective-permute-start.20 = (bf16[16,320,128]{2,1,0:T(8,128)(2,1)S(1)}, bf16[16,320,128]{2,1,0:T(8,128)(2,1)S(1)}, u32[]{:S(2)}, u32[]{:S(2)}) collective-permute-start(bf16[16,320,128]{2,1,0:T(8,128)(2,1)S(1)} %get-tuple-element.7.part), channel_id=1, source_target_pairs={{0,1},{1,0},{2,3},{3,2},{4,5},{5,4},{6,7},{7,6},{8,9},{9,8},{10,11... | collective-permute-start | bytes 3932168 | tf_op jit(solution)/shard_map/ppermute | solution.py:317
  82.9 34.7 %copy-start.6 = (bf16[128,1024]{1,0:T(8,128)(2,1)S(1)}, bf16[128,1024]{1,0:T(8,128)(2,1)}, u32[]{:S(2)}) copy-start(bf16[128,1024]{1,0:T(8,128)(2,1)} %copy-done.5) | copy-start | bytes 786436
  82.9 7.7 %collective-permute-start.22 = (bf16[8,32,384]{2,1,0:T(8,128)(2,1)S(1)}, bf16[8,32,384]{2,1,0:T(8,128)(2,1)S(1)}, u32[]{:S(2)}, u32[]{:S(2)}) collective-permute-start(bf16[8,32,384]{2,1,0:T(8,128)(2,1)S(1)} %get-tuple-element.10), channel_id=1, source_target_pairs={{0,0},{1,128},{16,16},{17,144},{32,32},{33,160},{48,48},{49,176},{... | collective-permute-start | bytes 589832 | tf_op jit(solution)/shard_map/ppermute | solution.py:330
  85.0 5.6 %collective-permute-start.23 = (bf16[8,32,384]{2,1,0:T(8,128)(2,1)S(1)}, bf16[8,32,384]{2,1,0:T(8,128)(2,1)S(1)}, u32[]{:S(2)}, u32[]{:S(2)}) collective-permute-start(bf16[8,32,384]{2,1,0:T(8,128)(2,1)S(1)} %get-tuple-element.11), channel_id=1, source_target_pairs={{0,1},{1,129},{16,17},{17,145},{32,33},{33,161},{48,49},{49,177},{... | collective-permute-start | bytes 589832 | tf_op jit(solution)/shard_map/ppermute | solution.py:330
  86.6 27.5 %all-to-all-start.1 = ((bf16[8,384,128]{2,1,0:T(8,128)(2,1)}), bf16[8,384,128]{2,1,0:T(8,128)(2,1)S(1)}, u32[]{:S(2)}, u32[]{:S(2)}) async-start(bf16[8,384,128]{2,1,0:T(8,128)(2,1)} %join_pass.1), calls=%async_computation.1 | async-start | bytes 1572864 | tf_op jit(solution)/shard_map/all_to_all | solution.py:374
  90.7 4.9 %collective-permute-start.24 = (bf16[8,32,384]{2,1,0:T(8,128)(2,1)S(1)}, bf16[8,32,384]{2,1,0:T(8,128)(2,1)S(1)}, u32[]{:S(2)}, u32[]{:S(2)}) collective-permute-start(bf16[8,32,384]{2,1,0:T(8,128)(2,1)S(1)} %add_convert_fusion.3), channel_id=1, source_target_pairs={{0,4},{4,0},{8,12},{12,8},{1,5},{5,1},{9,13},{13,9},{2,6},{6,2},{1... | collective-permute-start | bytes 589832 | tf_op jit(solution)/shard_map/ppermute | solution.py:317
  95.6 6.8 %collective-permute-start.25 = (bf16[8,32,384]{2,1,0:T(8,128)(2,1)S(1)}, bf16[8,32,384]{2,1,0:T(8,128)(2,1)S(1)}, u32[]{:S(2)}, u32[]{:S(2)}) collective-permute-start(bf16[8,32,384]{2,1,0:T(8,128)(2,1)S(1)} %add_convert_fusion.2), channel_id=1, source_target_pairs={{0,8},{4,12},{8,0},{12,4},{1,9},{5,13},{9,1},{13,5},{2,10},{6,14},... | collective-permute-start | bytes 589832 | tf_op jit(solution)/shard_map/ppermute | solution.py:317
  102.5 6.5 %collective-permute-start.26 = (bf16[8,32,384]{2,1,0:T(8,128)(2,1)S(1)}, bf16[8,32,384]{2,1,0:T(8,128)(2,1)S(1)}, u32[]{:S(2)}, u32[]{:S(2)}) collective-permute-start(bf16[8,32,384]{2,1,0:T(8,128)(2,1)S(1)} %add_convert_fusion.1), channel_id=1, source_target_pairs={{0,2},{2,0},{1,3},{3,1},{4,6},{6,4},{5,7},{7,5},{8,10},{10,8},{9,1... | collective-permute-start | bytes 589832 | tf_op jit(solution)/shard_map/ppermute | solution.py:317
  114.2 15.6 %all-to-all-start.2 = ((bf16[8,32,384]{2,1,0:T(8,128)(2,1)}), bf16[8,32,384]{2,1,0:T(8,128)(2,1)S(1)}, u32[]{:S(2)}, u32[]{:S(2)}) async-start(bf16[8,32,384]{2,1,0:T(8,128)(2,1)} %add_convert_fusion), calls=%async_computation.2 | async-start | bytes 393216 | tf_op jit(solution)/shard_map/all_to_all | solution.py:382
  117.6 2.8 %copy-start = (bf16[1024,3072]{1,0:T(8,128)(2,1)S(1)}, bf16[1024,3072]{1,0:T(8,128)(2,1)}, u32[]{:S(2)}) copy-start(bf16[1024,3072]{1,0:T(8,128)(2,1)} %w.1) | copy-start | bytes 18874372
  123.3 10.5 %collective-permute-start.21 = (bf16[128,1024]{1,0:T(8,128)(2,1)S(1)}, bf16[128,1024]{1,0:T(8,128)(2,1)S(1)}, u32[]{:S(2)}, u32[]{:S(2)}) collective-permute-start(bf16[128,1024]{1,0:T(8,128)(2,1)S(1)} %rows_pass.1), channel_id=1, source_target_pairs={{0,0},{1,128},{16,16},{17,144},{32,32},{33,160},{48,48},{49,176},{... | collective-permute-start | bytes 786440 | tf_op jit(solution)/shard_map/ppermute | solution.py:330
  129.8 1.5 %collective-permute-start.27 = (bf16[8,32,384]{2,1,0:T(8,128)(2,1)S(1)}, bf16[8,32,384]{2,1,0:T(8,128)(2,1)S(1)}, u32[]{:S(2)}, u32[]{:S(2)}) collective-permute-start(bf16[8,32,384]{2,1,0:T(8,128)(2,1)S(1)} %all-to-all-done.2.own), channel_id=1, source_target_pairs={{0,1},{1,0},{2,3},{3,2},{4,5},{5,4},{6,7},{7,6},{8,9},{9,8},{10,11... | collective-permute-start | bytes 589832 | tf_op jit(solution)/shard_map/ppermute | solution.py:317
